TPU v7x, 32 devices: a whole 2x2x4 slice. The times are simulated.
32 devices in a mesh: dp: 16 (over z, x, core), tensor: 2 (over y).
Axes of the slice: x: 2, y: 2, z: 4, core: 2. Of those that a mesh axis runs over, the one named last changes fastest.
Arguments:
- inputs: bfloat16 [16384, 1536], P(('dp', 'tensor')), may hold values from -6 to 6
- text_states: bfloat16 [16, 64, 1536], P('dp'), may hold values from -6 to 6
- self_query: bfloat16 [1536, 1536], P('dp', 'tensor'), may hold values from -0.15625 to 0.15625
- self_key: bfloat16 [1536, 1536], P('dp', 'tensor'), may hold values from -0.15625 to 0.15625
- self_value: bfloat16 [1536, 1536], P('dp', 'tensor'), may hold values from -0.15625 to 0.15625
- self_output: bfloat16 [1536, 1536], P('tensor', 'dp'), may hold values from -1.25 to 1.25
- cross_query: bfloat16 [1536, 1536], P('dp', 'tensor'), may hold values from -0.15625 to 0.15625
- cross_key: bfloat16 [1536, 1536], P('dp', 'tensor'), may hold values from -0.15625 to 0.15625
- cross_value: bfloat16 [1536, 1536], P('dp', 'tensor'), may hold values from -0.15625 to 0.15625
- cross_output: bfloat16 [1536, 1536], P('tensor', 'dp'), may hold values from -0.625 to 0.625
- inner_weight: bfloat16 [1536, 6144], P('dp', 'tensor'), may hold values from -0.15625 to 0.15625
- outer_weight: bfloat16 [6144, 1536], P('tensor', 'dp'), may hold values from -0.078125 to 0.078125
- norm_gains: float32 [3, 1536], replicated, may hold values from 0.25 to 1.75
- norm_shifts: float32 [3, 1536], replicated, may hold values from -2 to 2
- cotangent: bfloat16 [16384, 1536], P(('dp', 'tensor')), may hold values from -6 to 6
Outputs:
- output: bfloat16 [16384, 1536], P(('dp', 'tensor'))
- input_grad: float32 [16384, 1536], P(('dp', 'tensor'))
- text_grad: float32 [16, 64, 1536], P('dp', None, 'tensor')
- self_query_grad: float32 [1536, 1536], P('dp', 'tensor')
- self_key_grad: float32 [1536, 1536], P('dp', 'tensor')
- self_value_grad: float32 [1536, 1536], P('dp', 'tensor')
- self_output_grad: float32 [1536, 1536], P('tensor', 'dp')
- cross_query_grad: float32 [1536, 1536], P('dp', 'tensor')
- cross_key_grad: float32 [1536, 1536], P('dp', 'tensor')
- cross_value_grad: float32 [1536, 1536], P('dp', 'tensor')
- cross_output_grad: float32 [1536, 1536], P('tensor', 'dp')
- inner_weight_grad: float32 [1536, 6144], P('dp', 'tensor')
- outer_weight_grad: float32 [6144, 1536], P('tensor', 'dp')
- gains_grad: float32 [3, 1536], replicated
- shifts_grad: float32 [3, 1536], replicated
All inputs are finite; a program needn't handle non-finite values.
Results may differ from a plain program's by a relative error of at most 0.02.
Values may be sent and summed in bfloat16 or wider, within the bound.
No kernel may reach another device: no remote copies, remote signals or barrier semaphores. Data moves between devices by JAX's collectives and lax.ppermute only.
A program may use at most 320 MiB of HBM per device.

v0:
```python
from functools import partial
import math

import jax
import jax.numpy as jnp
from jax import lax
from jax.sharding import PartitionSpec as P

HD = 64
TEXT = 64
LEN = 1024


EPS = 1e-05
MASKED = -1e30


def norm_rows(value, gain, shift):
    mean = jnp.mean(value, axis=-1, keepdims=True)
    centred = value - mean
    spread = jnp.mean(centred * centred, axis=-1, keepdims=True)
    return centred * lax.rsqrt(spread + EPS) * gain + shift


def norm_back(value, gain, shift, incoming):
    ignored, pullback = jax.vjp(norm_rows, value, gain, shift)
    return pullback(incoming)


def gelu_exact(value):
    return jax.nn.gelu(value, approximate=False)


def transposed_times(left, right):
    return lax.dot_general(
        left, right, (((0,), (0,)), ((), ())), preferred_element_type=jnp.float32
    )


def times_t(left, right):
    return lax.dot_general(
        left, right, (((1,), (1,)), ((), ())), preferred_element_type=jnp.float32
    )


def apply_projection(left, right):
    return jnp.dot(left, right, preferred_element_type=jnp.float32).astype(jnp.bfloat16)


def scores_of(query, key, masked):
    scale = 1.0 / math.sqrt(HD)
    scores = jnp.einsum("qhd,khd->hqk", query, key, preferred_element_type=jnp.float32) * scale
    if masked:
        places = jnp.arange(query.shape[0])
        allowed = places[:, None] >= places[None, :]
        scores = jnp.where(allowed[None], scores, MASKED)
    return scores


def attend(block, masked):
    query, key, value = block
    scores = scores_of(query, key, masked)
    highest = jnp.max(scores, axis=-1, keepdims=True)
    total = jnp.sum(jnp.exp(scores - highest), axis=-1, keepdims=True)
    log_total = highest + jnp.log(total)
    weights = jnp.exp(scores - log_total).astype(jnp.bfloat16)
    mixed = jnp.einsum("hqk,khd->qhd", weights, value, preferred_element_type=jnp.float32)
    return (mixed.astype(jnp.bfloat16), log_total)


def attend_back(block, masked):
    query, key, value, log_total, grad_mixed = block
    scale = 1.0 / math.sqrt(HD)
    weights = jnp.exp(scores_of(query, key, masked) - log_total)
    rounded = weights.astype(jnp.bfloat16)
    d_value = jnp.einsum("hqk,qhd->khd", rounded, grad_mixed, preferred_element_type=jnp.float32)
    d_weights = jnp.einsum("qhd,khd->hqk", grad_mixed, value, preferred_element_type=jnp.float32)
    centred = d_weights - jnp.sum(weights * d_weights, axis=-1, keepdims=True)
    d_scores = (weights * centred).astype(jnp.bfloat16)
    d_query = jnp.einsum("hqk,khd->qhd", d_scores, key, preferred_element_type=jnp.float32) * scale
    d_key = jnp.einsum("hqk,qhd->khd", d_scores, query, preferred_element_type=jnp.float32) * scale
    return (d_query.astype(jnp.bfloat16), d_key.astype(jnp.bfloat16), d_value.astype(jnp.bfloat16))


def spread_rows(normed):
    return lax.all_gather(normed, "tensor", axis=0, tiled=True)


def spread_grads(grad):
    return lax.all_gather(grad.astype(jnp.bfloat16), "tensor", axis=0, tiled=True)


def branch_total(mixed, weight):
    return lax.psum_scatter(
        jnp.dot(mixed, weight, preferred_element_type=jnp.float32),
        "tensor",
        scatter_dimension=0,
        tiled=True,
    )


def normalized_total(pairs):
    total = None
    for grad, weight in pairs:
        added = times_t(grad, weight)
        total = added if total is None else total + added
    return lax.psum_scatter(total, "tensor", scatter_dimension=0, tiled=True)


def on_device(
    inputs,
    text_states,
    self_query,
    self_key,
    self_value,
    self_output,
    cross_query,
    cross_key,
    cross_value,
    cross_output,
    inner_weight,
    outer_weight,
    norm_gains,
    norm_shifts,
    cotangent,
):
    (
        gathered_self_query,
        gathered_self_key,
        gathered_self_value,
        full_soutput,
        full_cquery,
        full_ckey,
        full_cvalue,
        full_coutput,
        full_inner,
        full_outer,
    ) = (
        lax.all_gather(self_query, "dp", axis=0, tiled=True),
        lax.all_gather(self_key, "dp", axis=0, tiled=True),
        lax.all_gather(self_value, "dp", axis=0, tiled=True),
        lax.all_gather(self_output, "dp", axis=1, tiled=True),
        lax.all_gather(cross_query, "dp", axis=0, tiled=True),
        lax.all_gather(cross_key, "dp", axis=0, tiled=True),
        lax.all_gather(cross_value, "dp", axis=0, tiled=True),
        lax.all_gather(cross_output, "dp", axis=1, tiled=True),
        lax.all_gather(inner_weight, "dp", axis=0, tiled=True),
        lax.all_gather(outer_weight, "dp", axis=1, tiled=True),
    )
    width = inputs.shape[1]
    clips = text_states.shape[0]
    local_heads = gathered_self_query.shape[1] // HD

    def heads(value, length):
        return value.reshape(clips, length, local_heads, HD)

    def flatten(value):
        return value.reshape(-1, local_heads * HD)

    start = inputs.astype(jnp.float32)
    first_rows = spread_rows(norm_rows(start, norm_gains[0], norm_shifts[0]).astype(jnp.bfloat16))
    query1 = apply_projection(first_rows, gathered_self_query)
    first_key = apply_projection(first_rows, gathered_self_key)
    value1 = apply_projection(first_rows, gathered_self_value)
    mixed1, lse1 = lax.map(
        partial(attend, masked=True),
        (heads(query1, LEN), heads(first_key, LEN), heads(value1, LEN)),
    )
    mixed1 = flatten(mixed1)
    state1 = start + branch_total(mixed1, full_soutput)
    rows2 = spread_rows(norm_rows(state1, norm_gains[1], norm_shifts[1]).astype(jnp.bfloat16))
    query2 = apply_projection(rows2, full_cquery)
    text_flat = text_states.reshape(-1, width)
    key2 = apply_projection(text_flat, full_ckey)
    value2 = apply_projection(text_flat, full_cvalue)
    mixed2, lse2 = lax.map(
        partial(attend, masked=False), (heads(query2, LEN), heads(key2, TEXT), heads(value2, TEXT))
    )
    mixed2 = flatten(mixed2)
    state2 = state1 + branch_total(mixed2, full_coutput)
    rows3 = spread_rows(norm_rows(state2, norm_gains[2], norm_shifts[2]).astype(jnp.bfloat16))
    inner = jnp.dot(rows3, full_inner, preferred_element_type=jnp.float32)
    active_float, gelu_pull = jax.vjp(gelu_exact, inner)
    active = active_float.astype(jnp.bfloat16)
    result = state2 + branch_total(active, full_outer)
    output = result.astype(jnp.bfloat16)
    grad3 = cotangent.astype(jnp.float32)
    grads_outer = spread_grads(grad3)
    d_outer = transposed_times(active, grads_outer)
    d_inner = gelu_pull(times_t(grads_outer, full_outer))[0].astype(jnp.bfloat16)
    d_innerw = transposed_times(rows3, d_inner)
    back3 = normalized_total(((d_inner, full_inner),))
    d_state2, gain_three, shift_three = norm_back(state2, norm_gains[2], norm_shifts[2], back3)
    grad2 = grad3 + d_state2
    grads_cross = spread_grads(grad2)
    d_coutput = transposed_times(mixed2, grads_cross)
    d_mixed2 = times_t(grads_cross, full_coutput).astype(jnp.bfloat16)
    d_query2, d_key2, d_value2 = lax.map(
        partial(attend_back, masked=False),
        (heads(query2, LEN), heads(key2, TEXT), heads(value2, TEXT), lse2, heads(d_mixed2, LEN)),
    )
    d_query2 = flatten(d_query2)
    d_key2 = flatten(d_key2)
    d_value2 = flatten(d_value2)
    d_cquery = transposed_times(rows2, d_query2)
    d_ckey = transposed_times(text_flat, d_key2)
    d_cvalue = transposed_times(text_flat, d_value2)
    text_terms = (times_t(d_key2, full_ckey) + times_t(d_value2, full_cvalue)).reshape(
        clips, TEXT, width
    )
    text_grad = lax.psum_scatter(
        text_terms.astype(jnp.bfloat16), "tensor", scatter_dimension=2, tiled=True
    ).astype(jnp.float32)
    back2 = normalized_total(((d_query2, full_cquery),))
    d_state1, gain_two, shift_two = norm_back(state1, norm_gains[1], norm_shifts[1], back2)
    grad1 = grad2 + d_state1
    grads_self = spread_grads(grad1)
    d_soutput = transposed_times(mixed1, grads_self)
    d_mixed1 = times_t(grads_self, full_soutput).astype(jnp.bfloat16)
    first_query_grad, first_key_grad, first_value_grad = lax.map(
        partial(attend_back, masked=True),
        (heads(query1, LEN), heads(first_key, LEN), heads(value1, LEN), lse1, heads(d_mixed1, LEN)),
    )
    first_query_grad = flatten(first_query_grad)
    first_key_grad = flatten(first_key_grad)
    first_value_grad = flatten(first_value_grad)
    d_squery = transposed_times(first_rows, first_query_grad)
    self_key_partial = transposed_times(first_rows, first_key_grad)
    d_svalue = transposed_times(first_rows, first_value_grad)
    first_backward = normalized_total(
        (
            (first_query_grad, gathered_self_query),
            (first_key_grad, gathered_self_key),
            (first_value_grad, gathered_self_value),
        )
    )
    d_start, gain_one, shift_one = norm_back(start, norm_gains[0], norm_shifts[0], first_backward)
    input_grad = grad1 + d_start
    gains_grad, shifts_grad = lax.psum(
        (
            jnp.stack([gain_one, gain_two, gain_three]),
            jnp.stack([shift_one, shift_two, shift_three]),
        ),
        ("dp", "tensor"),
    )
    summed = (
        lax.psum_scatter(
            d_squery.astype(jnp.bfloat16), "dp", scatter_dimension=0, tiled=True
        ).astype(jnp.float32),
        lax.psum_scatter(
            self_key_partial.astype(jnp.bfloat16), "dp", scatter_dimension=0, tiled=True
        ).astype(jnp.float32),
        lax.psum_scatter(
            d_svalue.astype(jnp.bfloat16), "dp", scatter_dimension=0, tiled=True
        ).astype(jnp.float32),
        lax.psum_scatter(
            d_soutput.astype(jnp.bfloat16), "dp", scatter_dimension=1, tiled=True
        ).astype(jnp.float32),
        lax.psum_scatter(
            d_cquery.astype(jnp.bfloat16), "dp", scatter_dimension=0, tiled=True
        ).astype(jnp.float32),
        lax.psum_scatter(d_ckey.astype(jnp.bfloat16), "dp", scatter_dimension=0, tiled=True).astype(
            jnp.float32
        ),
        lax.psum_scatter(
            d_cvalue.astype(jnp.bfloat16), "dp", scatter_dimension=0, tiled=True
        ).astype(jnp.float32),
        lax.psum_scatter(
            d_coutput.astype(jnp.bfloat16), "dp", scatter_dimension=1, tiled=True
        ).astype(jnp.float32),
        lax.psum_scatter(
            d_innerw.astype(jnp.bfloat16), "dp", scatter_dimension=0, tiled=True
        ).astype(jnp.float32),
        lax.psum_scatter(
            d_outer.astype(jnp.bfloat16), "dp", scatter_dimension=1, tiled=True
        ).astype(jnp.float32),
    )
    return (
        output,
        input_grad,
        text_grad,
        summed[0],
        summed[1],
        summed[2],
        summed[3],
        summed[4],
        summed[5],
        summed[6],
        summed[7],
        summed[8],
        summed[9],
        gains_grad,
        shifts_grad,
    )


def solution(mesh):
    in_specs = (
        P(("dp", "tensor"), None),
        P("dp", None, None),
        P("dp", "tensor"),
        P("dp", "tensor"),
        P("dp", "tensor"),
        P("tensor", "dp"),
        P("dp", "tensor"),
        P("dp", "tensor"),
        P("dp", "tensor"),
        P("tensor", "dp"),
        P("dp", "tensor"),
        P("tensor", "dp"),
        P(),
        P(),
        P(("dp", "tensor"), None),
    )
    out_specs = (
        P(("dp", "tensor"), None),
        P(("dp", "tensor"), None),
        P("dp", None, "tensor"),
        P("dp", "tensor"),
        P("dp", "tensor"),
        P("dp", "tensor"),
        P("tensor", "dp"),
        P("dp", "tensor"),
        P("dp", "tensor"),
        P("dp", "tensor"),
        P("tensor", "dp"),
        P("dp", "tensor"),
        P("tensor", "dp"),
        P(),
        P(),
    )
    return jax.shard_map(
        on_device, mesh=mesh, in_specs=in_specs, out_specs=out_specs, check_vma=False
    )
```

profile of v0, /device:TPU:0, one launch (start us, length us, event | category | flops | bytes accessed | tf_op | source)
XLA Modules:
  0.0 2202.1 jit_solution(16883860188223177039)
XLA Ops:
  16.6 44.7 %all-gather.17.cloned.1.call-done = bf16[1024,1536]{1,0:T(8,128)(2,1)} async-done(((bf16[512,1536]{1,0:T(8,128)(2,1)}), bf16[1024,1536]{1,0:T(8,128)(2,1)}) %all-gather.17.cloned.1.call-update) | async-done | bytes 3145744 | tf_op jit(solution)/shard_map/all_gather | solution.py:86
  61.4 44.6 %all-gather.23.cloned.1.call-done = bf16[1536,768]{1,0:T(8,128)(2,1)} async-done(((bf16[96,768]{1,0:T(8,128)(2,1)}), bf16[1536,768]{1,0:T(8,128)(2,1)}) %all-gather.23.cloned.1.call-update) | async-done | bytes 2359312 | tf_op jit(solution)/shard_map/all_gather | solution.py:140
  112.4 36.9 %all-gather.21.cloned.1.call-done = bf16[1536,768]{1,0:T(8,128)(2,1)} async-done(((bf16[96,768]{1,0:T(8,128)(2,1)}), bf16[1536,768]{1,0:T(8,128)(2,1)}) %all-gather.21.cloned.1.call-update) | async-done | bytes 2359312 | tf_op jit(solution)/shard_map/all_gather | solution.py:139
  244.2 73.7 %reduce-scatter.22.cloned.1.call-done = f32[512,1536]{1,0:T(8,128)} async-done(((f32[1024,1536]{1,0:T(8,128)}), f32[512,1536]{1,0:T(8,128)}) %reduce-scatter.22.cloned.1.call-update) | async-done | bytes 3145744 | tf_op jit(solution)/shard_map/reduce_scatter | solution.py:94
  323.8 38.8 %all-gather.33.cloned.1.call-done = bf16[1536,768]{1,0:T(8,128)(2,1)} async-done(((bf16[96,768]{1,0:T(8,128)(2,1)}), bf16[1536,768]{1,0:T(8,128)(2,1)}) %all-gather.33.cloned.1.call-update) | async-done | bytes 2359312 | tf_op jit(solution)/shard_map/all_gather | solution.py:144
  366.5 39.4 %all-gather.27.cloned.1.call-done = bf16[1536,768]{1,0:T(8,128)(2,1)} async-done(((bf16[96,768]{1,0:T(8,128)(2,1)}), bf16[1536,768]{1,0:T(8,128)(2,1)}) %all-gather.27.cloned.1.call-update) | async-done | bytes 2359312 | tf_op jit(solution)/shard_map/all_gather | solution.py:145
  410.6 38.7 %all-gather.31.cloned.1.call-done = bf16[1536,768]{1,0:T(8,128)(2,1)} async-done(((bf16[96,768]{1,0:T(8,128)(2,1)}), bf16[1536,768]{1,0:T(8,128)(2,1)}) %all-gather.31.cloned.1.call-update) | async-done | bytes 2359312 | tf_op jit(solution)/shard_map/all_gather | solution.py:143
  449.3 45.6 %all-gather.29.cloned.1.call-done = bf16[1024,1536]{1,0:T(8,128)(2,1)} async-done(((bf16[512,1536]{1,0:T(8,128)(2,1)}), bf16[1024,1536]{1,0:T(8,128)(2,1)}) %all-gather.29.cloned.1.call-update) | async-done | bytes 3145744 | tf_op jit(solution)/shard_map/all_gather | solution.py:86
  505.0 34.6 %all-gather.35.cloned.1.call-done = bf16[768,1536]{0,1:T(8,128)(2,1)} async-done(((bf16[768,96]{0,1:T(8,128)(2,1)}), bf16[768,1536]{0,1:T(8,128)(2,1)}) %all-gather.35.cloned.1.call-update) | async-done | bytes 2359312 | tf_op jit(solution)/shard_map/all_gather | solution.py:146
  547.8 75.2 %reduce-scatter.24.cloned.1.call-done = f32[512,1536]{1,0:T(8,128)} async-done(((f32[1024,1536]{1,0:T(8,128)}), f32[512,1536]{1,0:T(8,128)}) %reduce-scatter.24.cloned.1.call-update) | async-done | bytes 3145744 | tf_op jit(solution)/shard_map/reduce_scatter | solution.py:94
  630.4 75.8 %all-gather.39.cloned.1.call-done = bf16[1536,3072]{1,0:T(8,128)(2,1)} async-done(((bf16[96,3072]{1,0:T(8,128)(2,1)}), bf16[1536,3072]{1,0:T(8,128)(2,1)}) %all-gather.39.cloned.1.call-update) | async-done | bytes 9437200 | tf_op jit(solution)/shard_map/all_gather | solution.py:147
  706.2 45.3 %all-gather.37.cloned.1.call-done = bf16[1024,1536]{1,0:T(8,128)(2,1)} async-done(((bf16[512,1536]{1,0:T(8,128)(2,1)}), bf16[1024,1536]{1,0:T(8,128)(2,1)}) %all-gather.37.cloned.1.call-update) | async-done | bytes 3145744 | tf_op jit(solution)/shard_map/all_gather | solution.py:86
  767.6 30.3 %all-gather.43.cloned.1.call-done = bf16[1024,1536]{1,0:T(8,128)(2,1)} async-done(((bf16[512,1536]{1,0:T(8,128)(2,1)}), bf16[1024,1536]{1,0:T(8,128)(2,1)}) %all-gather.43.cloned.1.call-update) | async-done | bytes 3145744 | tf_op jit(solution)/shard_map/all_gather | solution.py:90
  797.9 83.1 %all-gather.41.cloned.1.call-done = bf16[3072,1536]{0,1:T(8,128)(2,1)} async-done(((bf16[3072,96]{0,1:T(8,128)(2,1)}), bf16[3072,1536]{0,1:T(8,128)(2,1)}) %all-gather.41.cloned.1.call-update) | async-done | bytes 9437200 | tf_op jit(solution)/shard_map/all_gather | solution.py:148
  880.9 42.1 %add_convert_fusion = (bf16[1024,3072]{1,0:T(8,128)(2,1)S(1)}, f32[1024,3072]{1,0:T(8,128)}) fusion(f32[1024,3072]{1,0:T(8,128)} %fusion.56, bf16[1024,1536]{1,0:T(8,128)(2,1)} %all-gather.43.cloned.1.call-done, bf16[3072,1536]{0,1:T(8,128)(2,1)} %all-gather.41.cloned.1.call-done), kind=kOutput, calls=%fused_computation.9 | convolution fusion | flops 9890168832 | bytes 44040192 | tf_op jit(solution)/shard_map/dot_general | solution.py:41
  965.3 49.8 %reduce-scatter.28.cloned.1.call-done = f32[512,1536]{1,0:T(8,128)} async-done(((f32[1024,1536]{1,0:T(8,128)}), f32[512,1536]{1,0:T(8,128)}) %reduce-scatter.28.cloned.1.call-update) | async-done | bytes 3145744 | tf_op jit(solution)/shard_map/reduce_scatter | solution.py:107
  1018.6 75.8 %reduce-scatter.26.cloned.1.call-done = f32[512,1536]{1,0:T(8,128)} async-done(((f32[1024,1536]{1,0:T(8,128)}), f32[512,1536]{1,0:T(8,128)}) %reduce-scatter.26.cloned.1.call-update) | async-done | bytes 3145744 | tf_op jit(solution)/shard_map/reduce_scatter | solution.py:94
  1102.3 44.8 %all-gather.45.cloned.1.call-done = bf16[1024,1536]{1,0:T(8,128)(2,1)} async-done(((bf16[512,1536]{1,0:T(8,128)(2,1)}), bf16[1024,1536]{1,0:T(8,128)(2,1)}) %all-gather.45.cloned.1.call-update) | async-done | bytes 3145744 | tf_op jit(solution)/shard_map/all_gather | solution.py:90
  1162.5 77.2 %reduce-scatter.30.cloned.1.call-done = f32[512,1536]{1,0:T(8,128)} async-done(((f32[1024,1536]{1,0:T(8,128)}), f32[512,1536]{1,0:T(8,128)}) %reduce-scatter.30.cloned.1.call-update) | async-done | bytes 3145744 | tf_op jit(solution)/shard_map/reduce_scatter | solution.py:107
  1348.2 34.7 %multiply_reduce_fusion = (f32[12,1024]{1,0:T(8,128)S(1)}, f32[12,1024,1024]{1,2,0:T(8,128)}) fusion(f32[12,1024,1024]{1,2,0:T(8,128)} %get-tuple-element.180, f32[12,1024]{1,0:T(8,128)S(1)} %copy-done.46, pred[1024,1024]{0,1:T(8,128)(4,1)S(1)} %copy-done.11, bf16[1024,12,64]{0,2,1:T(8,128)(2,1)} %bitcast.149, bf16[1024,12,64]{0,2,1:T(8,128)(2,1)} %bitcast.147), kind=kOutput, calls=%fused_computation.1 | convolution fusion | flops 1673515008 | bytes 104955904 | tf_op jit(solution)/shard_map/while/body/eval_jaxpr/qhd,khd->hqk/dot_general | solution.py:77
  1383.2 42.7 %multiply_convert_fusion = bf16[12,1024,1024]{1,2,0:T(8,128)(2,1)} fusion(f32[12,1024,1024]{1,2,0:T(8,128)} %get-tuple-element.186, f32[12,1024,1024]{1,2,0:T(8,128)} %get-tuple-element.180, f32[12,1024]{1,0:T(8,128)S(1)} %get-tuple-element.185, f32[12,1024]{1,0:T(8,128)S(1)} %copy-done.46, pred[1024,1024]{0,1:T(8,128)(4,1)S(1)} %copy-done.11), kind=kLoop, calls=%fused_computation | loop fusion | flops 75497472 | bytes 126976000 | tf_op jit(solution)/shard_map/while/body/eval_jaxpr/convert_element_type | solution.py:79
  1481.9 42.1 %reduce-scatter.48.cloned.1.call-done = bf16[96,3072]{1,0:T(8,128)(2,1)} async-done(((bf16[1536,3072]{1,0:T(8,128)(2,1)}), bf16[96,3072]{1,0:T(8,128)(2,1)}) %reduce-scatter.48.cloned.1.call-update) | async-done | bytes 589840 | tf_op jit(solution)/shard_map/reduce_scatter | solution.py:271
  1538.9 65.4 %reduce-scatter.54.cloned.1.call-done = bf16[96,768]{1,0:T(8,128)(2,1)} async-done(((bf16[1536,768]{1,0:T(8,128)(2,1)}), bf16[96,768]{1,0:T(8,128)(2,1)}) %reduce-scatter.54.cloned.1.call-update) | async-done | bytes 147472
  1606.3 63.9 %reduce-scatter.52.cloned.1.call-done = bf16[96,768]{1,0:T(8,128)(2,1)} async-done(((bf16[1536,768]{1,0:T(8,128)(2,1)}), bf16[96,768]{1,0:T(8,128)(2,1)}) %reduce-scatter.52.cloned.1.call-update) | async-done | bytes 147472
  1672.1 63.9 %reduce-scatter.46.cloned.1.call-done = bf16[768,96]{0,1:T(8,128)(2,1)} async-done(((bf16[768,1536]{0,1:T(8,128)(2,1)}), bf16[768,96]{0,1:T(8,128)(2,1)}) %reduce-scatter.46.cloned.1.call-update) | async-done | bytes 147472 | tf_op jit(solution)/shard_map/reduce_scatter | solution.py:268
  1737.7 64.4 %reduce-scatter.44.cloned.1.call-done = bf16[96,768]{1,0:T(8,128)(2,1)} async-done(((bf16[1536,768]{1,0:T(8,128)(2,1)}), bf16[96,768]{1,0:T(8,128)(2,1)}) %reduce-scatter.44.cloned.1.call-update) | async-done | bytes 147472 | tf_op jit(solution)/shard_map/reduce_scatter | solution.py:259
  1803.7 64.3 %reduce-scatter.42.cloned.1.call-done = bf16[768,96]{0,1:T(8,128)(2,1)} async-done(((bf16[768,1536]{0,1:T(8,128)(2,1)}), bf16[768,96]{0,1:T(8,128)(2,1)}) %reduce-scatter.42.cloned.1.call-update) | async-done | bytes 147472 | tf_op jit(solution)/shard_map/reduce_scatter | solution.py:256
  1869.7 64.2 %reduce-scatter.40.cloned.1.call-done = bf16[96,768]{1,0:T(8,128)(2,1)} async-done(((bf16[1536,768]{1,0:T(8,128)(2,1)}), bf16[96,768]{1,0:T(8,128)(2,1)}) %reduce-scatter.40.cloned.1.call-update) | async-done | bytes 147472 | tf_op jit(solution)/shard_map/reduce_scatter | solution.py:253
  1935.6 64.4 %reduce-scatter.38.cloned.1.call-done = bf16[96,768]{1,0:T(8,128)(2,1)} async-done(((bf16[1536,768]{1,0:T(8,128)(2,1)}), bf16[96,768]{1,0:T(8,128)(2,1)}) %reduce-scatter.38.cloned.1.call-update) | async-done | bytes 147472 | tf_op jit(solution)/shard_map/reduce_scatter | solution.py:250
  2001.6 64.4 %reduce-scatter.36.cloned.1.call-done = bf16[96,768]{1,0:T(8,128)(2,1)} async-done(((bf16[1536,768]{1,0:T(8,128)(2,1)}), bf16[96,768]{1,0:T(8,128)(2,1)}) %reduce-scatter.36.cloned.1.call-update) | async-done | bytes 147472 | tf_op jit(solution)/shard_map/reduce_scatter | solution.py:247
  2067.7 76.7 %reduce-scatter.32.cloned.1.call-done = f32[512,1536]{1,0:T(8,128)} async-done(((f32[1024,1536]{1,0:T(8,128)}), f32[512,1536]{1,0:T(8,128)}) %reduce-scatter.32.cloned.1.call-update) | async-done | bytes 3145744 | tf_op jit(solution)/shard_map/reduce_scatter | solution.py:107
  2148.6 40.4 %all-reduce = (f32[3,1536]{1,0:T(4,128)}, f32[3,1536]{1,0:T(4,128)}) all-reduce(f32[3,1536]{1,0:T(4,128)S(1)} %get-tuple-element.187, f32[3,1536]{1,0:T(4,128)S(1)} %get-tuple-element.188), channel_id=1, replica_groups=mesh['dp'=16,'tensor'=2] {'dp','tensor'}, use_global_device_ids=true, to_apply=%region_38.39 | all-reduce | flops 9216 | bytes 73728 | tf_op jit(solution)/shard_map/psum | solution.py:239
  (361 shorter events, 437.9 us)
Async XLA Ops:
  13.6 92.4 %all-gather.23.cloned.1.call-start = ((), (), s32[]{:S(2)}) async-start(), calls=%async_computation.20 | async-start | bytes 2506752 | tf_op jit(solution)/shard_map/all_gather | solution.py:140
  14.3 135.0 %all-gather.21.cloned.1.call-start = ((), (), s32[]{:S(2)}) async-start(), calls=%async_computation.19 | async-start | bytes 2506752 | tf_op jit(solution)/shard_map/all_gather | solution.py:139
  15.1 180.9 %all-gather.19.cloned.1.call-start = ((), (), s32[]{:S(2)}) async-start(), calls=%async_computation.18 | async-start | bytes 2506752 | tf_op jit(solution)/shard_map/all_gather | solution.py:141
  15.6 220.1 %all-gather.25.cloned.1.call-start = ((), (), s32[]{:S(2)}) async-start(), calls=%async_computation.21 | async-start | bytes 2506752 | tf_op jit(solution)/shard_map/all_gather | solution.py:142
  16.2 301.7 %reduce-scatter.22.cloned.1.call-start = ((), (), s32[]{:S(2)}) async-start(), calls=%async_computation.22 | async-start | bytes 9437184 | tf_op jit(solution)/shard_map/reduce_scatter | solution.py:94
  242.0 120.6 %all-gather.33.cloned.1.call-start = ((), (), s32[]{:S(2)}) async-start(), calls=%async_computation.26 | async-start | bytes 2506752 | tf_op jit(solution)/shard_map/all_gather | solution.py:144
  242.7 163.2 %all-gather.27.cloned.1.call-start = ((), (), s32[]{:S(2)}) async-start(), calls=%async_computation.23 | async-start | bytes 2506752 | tf_op jit(solution)/shard_map/all_gather | solution.py:145
  243.5 205.8 %all-gather.31.cloned.1.call-start = ((), (), s32[]{:S(2)}) async-start(), calls=%async_computation.25 | async-start | bytes 2506752 | tf_op jit(solution)/shard_map/all_gather | solution.py:143
  244.2 250.7 %all-gather.29.cloned.1.call-start = ((), (), s32[]{:S(2)}) async-start(), calls=%async_computation.24 | async-start | bytes 4718592 | tf_op jit(solution)/shard_map/all_gather | solution.py:86
  323.0 216.6 %all-gather.35.cloned.1.call-start = ((), (), s32[]{:S(2)}) async-start(), calls=%async_computation.27 | async-start | bytes 2506752 | tf_op jit(solution)/shard_map/all_gather | solution.py:146
  323.7 299.3 %reduce-scatter.24.cloned.1.call-start = ((), (), s32[]{:S(2)}) async-start(), calls=%async_computation.28 | async-start | bytes 9437184 | tf_op jit(solution)/shard_map/reduce_scatter | solution.py:94
  547.0 159.2 %all-gather.39.cloned.1.call-start = ((), (), s32[]{:S(2)}) async-start(), calls=%async_computation.30 | async-start | bytes 10027008 | tf_op jit(solution)/shard_map/all_gather | solution.py:147
  547.7 203.8 %all-gather.37.cloned.1.call-start = ((), (), s32[]{:S(2)}) async-start(), calls=%async_computation.29 | async-start | bytes 4718592 | tf_op jit(solution)/shard_map/all_gather | solution.py:86
  629.0 168.9 %all-gather.43.cloned.1.call-start = ((), (), s32[]{:S(2)}) async-start(), calls=%async_computation.33 | async-start | bytes 4718592 | tf_op jit(solution)/shard_map/all_gather | solution.py:90
  629.6 251.3 %all-gather.41.cloned.1.call-start = ((), (), s32[]{:S(2)}) async-start(), calls=%async_computation.31 | async-start | bytes 10027008 | tf_op jit(solution)/shard_map/all_gather | solution.py:148
  630.2 384.9 %reduce-scatter.28.cloned.1.call-start = ((), (), s32[]{:S(2)}) async-start(), calls=%async_computation.34 | async-start | bytes 9437184 | tf_op jit(solution)/shard_map/reduce_scatter | solution.py:107
  939.4 155.1 %reduce-scatter.26.cloned.1.call-start = ((), (), s32[]{:S(2)}) async-start(), calls=%async_computation.32 | async-start | bytes 9437184 | tf_op jit(solution)/shard_map/reduce_scatter | solution.py:94
  965.3 181.8 %all-gather.45.cloned.1.call-start = ((), (), s32[]{:S(2)}) async-start(), calls=%async_computation.35 | async-start | bytes 4718592 | tf_op jit(solution)/shard_map/all_gather | solution.py:90
  1102.1 137.6 %reduce-scatter.30.cloned.1.call-start = ((), (), s32[]{:S(2)}) async-start(), calls=%async_computation.36 | async-start | bytes 9437184 | tf_op jit(solution)/shard_map/reduce_scatter | solution.py:107
  1162.4 148.1 %all-gather.47.cloned.1.call-start = ((), (), s32[]{:S(2)}) async-start(), calls=%async_computation.37 | async-start | bytes 4718592 | tf_op jit(solution)/shard_map/all_gather | solution.py:90
  1248.6 231.1 %reduce-scatter.50.cloned.1.call-start = ((), (), s32[]{:S(2)}) async-start(), calls=%async_computation.47 | async-start | bytes 10027008 | tf_op jit(solution)/shard_map/reduce_scatter | solution.py:274
  1264.1 259.8 %reduce-scatter.48.cloned.1.call-start = ((), (), s32[]{:S(2)}) async-start(), calls=%async_computation.46 | async-start | bytes 10027008 | tf_op jit(solution)/shard_map/reduce_scatter | solution.py:271
  1281.0 256.3 %reduce-scatter.34.cloned.1.call-start = ((), (), s32[]{:S(2)}) async-start(), calls=%async_computation.39 | async-start | bytes 294912 | tf_op jit(solution)/shard_map/reduce_scatter | solution.py:211
  1290.1 314.3 %reduce-scatter.54.cloned.1.call-start = ((), (), s32[]{:S(2)}) async-start(), calls=%async_computation.49 | async-start | bytes 2506752
  1293.5 376.7 %reduce-scatter.52.cloned.1.call-start = ((), (), s32[]{:S(2)}) async-start(), calls=%async_computation.48 | async-start | bytes 2506752
  1296.8 439.3 %reduce-scatter.46.cloned.1.call-start = ((), (), s32[]{:S(2)}) async-start(), calls=%async_computation.45 | async-start | bytes 2506752 | tf_op jit(solution)/shard_map/reduce_scatter | solution.py:268
  1303.7 498.4 %reduce-scatter.44.cloned.1.call-start = ((), (), s32[]{:S(2)}) async-start(), calls=%async_computation.44 | async-start | bytes 2506752 | tf_op jit(solution)/shard_map/reduce_scatter | solution.py:259
  1310.1 558.0 %reduce-scatter.42.cloned.1.call-start = ((), (), s32[]{:S(2)}) async-start(), calls=%async_computation.43 | async-start | bytes 2506752 | tf_op jit(solution)/shard_map/reduce_scatter | solution.py:256
  1341.6 592.3 %reduce-scatter.40.cloned.1.call-start = ((), (), s32[]{:S(2)}) async-start(), calls=%async_computation.42 | async-start | bytes 2506752 | tf_op jit(solution)/shard_map/reduce_scatter | solution.py:253
  1382.9 617.0 %reduce-scatter.38.cloned.1.call-start = ((), (), s32[]{:S(2)}) async-start(), calls=%async_computation.41 | async-start | bytes 2506752 | tf_op jit(solution)/shard_map/reduce_scatter | solution.py:250
  1448.3 617.7 %reduce-scatter.36.cloned.1.call-start = ((), (), s32[]{:S(2)}) async-start(), calls=%async_computation.40 | async-start | bytes 2506752 | tf_op jit(solution)/shard_map/reduce_scatter | solution.py:247
  1466.6 677.7 %reduce-scatter.32.cloned.1.call-start = ((), (), s32[]{:S(2)}) async-start(), calls=%async_computation.38 | async-start | bytes 9437184 | tf_op jit(solution)/shard_map/reduce_scatter | solution.py:107
  (94 other events, 6472.3 us)
Sparse Core Ops, SparseCore 0:
  13.7 47.6 all-gather.16
  63.6 42.2 all-gather.22
  108.3 41.0 all-gather.20
  151.5 41.0 all-gather.18
  194.7 41.0 all-gather.24
  242.1 75.8 reduce-scatter.21
  320.2 42.3 all-gather.32
  364.9 41.0 all-gather.26
  408.2 41.0 all-gather.30
  451.3 43.6 all-gather.28
  497.2 42.2 all-gather.34
  547.1 75.8 reduce-scatter.23
  625.3 80.8 all-gather.38
  708.2 43.3 all-gather.36
  752.9 44.8 all-gather.42
  800.0 80.8 all-gather.40
  939.5 75.5 reduce-scatter.27
  1017.3 77.1 reduce-scatter.25
  1102.2 44.8 all-gather.44
  1162.5 77.1 reduce-scatter.29
  1248.7 44.9 all-gather.46
  1297.7 111.2 reduce-scatter.49
  1413.1 110.8 reduce-scatter.47
  1541.1 63.2 reduce-scatter.53
  1608.0 62.1 reduce-scatter.51
  1673.8 62.1 reduce-scatter.45
  1739.8 62.2 reduce-scatter.43
  1805.8 62.2 reduce-scatter.41
  1871.7 62.1 reduce-scatter.39
  1937.7 62.2 reduce-scatter.37
  2003.7 62.2 reduce-scatter.35
  2068.2 76.1 reduce-scatter.31
  (1 shorter events, 10.6 us)
where the time goes:
time: 2210 us; the launch traced here: 2200 us
  waiting for transfers between devices  1620 us (73%)
  matrix products  354 us (16%)
  other arithmetic  133 us (6%)
  blocking collectives  40.4 us (2%)
  local copies, waits for them, and re-layouts  34.5 us (2%)
    reduce_scatter x3, waiting for transfers between devices, branch_total(): lax.psum_scatter(jnp.dot(mixed, weight, preferred_element_type=jnp.float3...  225 us
    reduce_scatter x3, waiting for transfers between devices, normalized_total(): return lax.psum_scatter(total, 'tensor', scatter_dimension=0, tiled=True)  204 us
    unnamed x35, waiting for transfers between devices  136 us
    all_gather x3, waiting for transfers between devices, spread_rows(): return lax.all_gather(normed, 'tensor', axis=0, tiled=True)  136 us
    dot_general x10, matrix products, times_t(): lax.dot_general(left, right, (((1,), (1,)), ((), ())), preferred_element_...  88.9 us
    all_gather x1, waiting for transfers between devices, on_device(): lax.all_gather(outer_weight, 'dp', axis=1, tiled=True)  83.1 us
    all_gather x1, waiting for transfers between devices, on_device(): lax.all_gather(inner_weight, 'dp', axis=0, tiled=True)  75.8 us
    all_gather x3, waiting for transfers between devices, spread_grads(): lax.all_gather(grad.astype(jnp.bfloat16), 'tensor', axis=0, tiled=True)  75.1 us
  transfers between devices with their start and end apart: 33, of which 30 were waited for; matrix products, arithmetic and copies ran while one was open for 18% of the time, Pallas kernels for 0%

commit v1 on v0

--- a/solution.py
+++ b/solution.py
@@ -4,6 +4,8 @@
 import jax
 import jax.numpy as jnp
 from jax import lax
+from jax.experimental import pallas as pl
+from jax.experimental.pallas import tpu as pltpu
 from jax.sharding import PartitionSpec as P
 
 HD = 64
@@ -294,6 +296,574 @@
     )
 
 
+BF = jnp.bfloat16
+F32 = jnp.float32
+NN = (((1,), (0,)), ((), ()))
+NT = (((1,), (1,)), ((), ()))
+TN = (((0,), (0,)), ((), ()))
+QB = 256
+PAIR = 128
+QUAD = 256
+
+
+def mm(left, right, dims):
+    return lax.dot_general(left, right, dims, preferred_element_type=F32)
+
+
+def lanes_of(width, head):
+    lane = lax.broadcasted_iota(jnp.int32, (1, width), 1)
+    return (lane >= head * HD) & (lane < (head + 1) * HD)
+
+
+def only(value, mask):
+    return jnp.where(mask, value, jnp.zeros_like(value))
+
+
+def pieces_of(block):
+    start = block * QB
+    found = [(0, start, False)] if block else []
+    return found + [(start, start + QB, True)]
+
+
+def causal():
+    key = lax.broadcasted_iota(jnp.int32, (QB, QB), 0)
+    place = lax.broadcasted_iota(jnp.int32, (QB, QB), 1)
+    return key <= place
+
+
+def to_places(t, ref, held, half):
+    low = pl.multiple_of(t * half, half)
+    high = pl.multiple_of((1 - t) * half, half)
+    held[0:half, :] = ref[pl.ds(low, half), :]
+    held[half : 2 * half, :] = ref[pl.ds(high, half), :]
+
+
+def row_of(t, start, half):
+    side = start // half
+    base = (1 - t) * half if side else t * half
+    return pl.multiple_of(base + start % half, QB)
+
+
+def self_kernel(t_ref, q_ref, k_ref, v_ref, o_ref, lse_ref, qs, ks, vs):
+    t = t_ref[0]
+    length = q_ref.shape[0]
+    half = length // 2
+    for ref, held in ((q_ref, qs), (k_ref, ks), (v_ref, vs)):
+        to_places(t, ref, held, half)
+    allowed = causal()
+    for block in range(length // QB):
+        rows = slice(block * QB, (block + 1) * QB)
+        query = qs[rows, :] * BF(0.125)
+        mixed = []
+        for head in range(2):
+            mine = only(query, lanes_of(PAIR, head))
+            parts = []
+            for a, b, edge in pieces_of(block):
+                score = mm(ks[a:b, :], mine, NT)
+                parts.append(jnp.where(allowed, score, MASKED) if edge else score)
+            top = jnp.max(parts[0], axis=0, keepdims=True)
+            for part in parts[1:]:
+                top = jnp.maximum(top, jnp.max(part, axis=0, keepdims=True))
+            total, out = None, None
+            for part, (a, b, edge) in zip(parts, pieces_of(block)):
+                power = jnp.exp(part - top)
+                added = jnp.sum(power, axis=0, keepdims=True)
+                term = mm(vs[a:b, :], power.astype(BF), TN)
+                total = added if total is None else total + added
+                out = term if out is None else out + term
+            lse_ref[0, head : head + 1, rows] = top + jnp.log(total)
+            mixed.append(out[head * HD : (head + 1) * HD, :] / total)
+        both = jnp.concatenate(mixed, axis=0)
+        o_ref[pl.ds(row_of(t, block * QB, half), QB), :] = both.T.astype(BF)
+
+
+def self_forward(t, qkv):
+    length, width = qkv.shape
+    pairs = width // (3 * PAIR)
+    spec = lambda part: pl.BlockSpec((length, PAIR), lambda j, s: (0, part * pairs + j))
+    return pl.pallas_call(
+        self_kernel,
+        out_shape=(
+            jax.ShapeDtypeStruct((length, pairs * PAIR), BF),
+            jax.ShapeDtypeStruct((pairs, 8, length), F32),
+        ),
+        grid_spec=pltpu.PrefetchScalarGridSpec(
+            num_scalar_prefetch=1,
+            grid=(pairs,),
+            in_specs=[spec(0), spec(1), spec(2)],
+            out_specs=[
+                pl.BlockSpec((length, PAIR), lambda j, s: (0, j)),
+                pl.BlockSpec((1, 8, length), lambda j, s: (j, 0, 0)),
+            ],
+            scratch_shapes=[pltpu.VMEM((length, PAIR), BF)] * 3,
+        ),
+        name="self_attend",
+        cost_estimate=pl.CostEstimate(
+            flops=16 * length * length * PAIR * pairs // 3,
+            transcendentals=length * length * pairs,
+            bytes_accessed=8 * length * PAIR * pairs,
+        ),
+    )(t, qkv, qkv, qkv)
+
+
+def self_back_kernel(
+    t_ref, q_ref, k_ref, v_ref, o_ref, do_ref, lse_ref, out_ref, qs, ks, vs, os, dos, dk, dv, dkb, dvb
+):
+    t = t_ref[0]
+    length = q_ref.shape[0]
+    half = length // 2
+    step = pl.program_id(1)
+
+    @pl.when(step == 0)
+    def _():
+        for ref, held in ((q_ref, qs), (k_ref, ks), (v_ref, vs), (o_ref, os), (do_ref, dos)):
+            to_places(t, ref, held, half)
+        allowed = causal()
+        blocks = length // QB
+        for block in reversed(range(blocks)):
+            rows = slice(block * QB, (block + 1) * QB)
+            query = qs[rows, :] * BF(0.125)
+            grad = dos[rows, :]
+            product = (grad.astype(F32) * os[rows, :].astype(F32)).T
+            mine = [only(query, lanes_of(PAIR, head)) for head in range(2)]
+            mine_grad = [only(grad, lanes_of(PAIR, head)) for head in range(2)]
+            both_query = jnp.concatenate(mine, axis=0)
+            both_grad = jnp.concatenate(mine_grad, axis=0)
+            d_query = [None, None]
+            for a, b, edge in pieces_of(block):
+                weights, d_scores = [], []
+                for head in range(2):
+                    drop = jnp.sum(product[head * HD : (head + 1) * HD, :], axis=0, keepdims=True)
+                    score = mm(ks[a:b, :], mine[head], NT)
+                    power = jnp.exp(score - lse_ref[0, head : head + 1, rows])
+                    if edge:
+                        power = jnp.where(allowed, power, 0.0)
+                    d_power = mm(vs[a:b, :], mine_grad[head], NT)
+                    d_score = (power * (d_power - drop)).astype(BF)
+                    weights.append(power.astype(BF))
+                    d_scores.append(d_score)
+                    term = mm(ks[a:b, :], d_score, TN)
+                    d_query[head] = term if d_query[head] is None else d_query[head] + term
+                add_v = mm(jnp.concatenate(weights, axis=1), both_grad, NN)
+                add_k = mm(jnp.concatenate(d_scores, axis=1), both_query, NN)
+                if block == blocks - 1:
+                    dv[a:b, :] = add_v
+                    dk[a:b, :] = add_k
+                else:
+                    dv[a:b, :] += add_v
+                    dk[a:b, :] += add_k
+            both = jnp.concatenate([d_query[0][:HD, :], d_query[1][HD:, :]], axis=0) * 0.125
+            out_ref[pl.ds(row_of(t, block * QB, half), QB), :] = both.T.astype(BF)
+        for block in range(blocks):
+            rows = slice(block * QB, (block + 1) * QB)
+            place = row_of(t, block * QB, half)
+            dkb[pl.ds(place, QB), :] = dk[rows, :].astype(BF)
+            dvb[pl.ds(place, QB), :] = dv[rows, :].astype(BF)
+
+    @pl.when(step == 1)
+    def _():
+        out_ref[...] = dkb[...]
+
+    @pl.when(step == 2)
+    def _():
+        out_ref[...] = dvb[...]
+
+
+def self_backward(t, qkv, mixed, d_mixed, lse):
+    length, width = qkv.shape
+    pairs = width // (3 * PAIR)
+    spec = lambda part: pl.BlockSpec((length, PAIR), lambda j, s, r: (0, part * pairs + j))
+    return pl.pallas_call(
+        self_back_kernel,
+        out_shape=jax.ShapeDtypeStruct((length, width), BF),
+        grid_spec=pltpu.PrefetchScalarGridSpec(
+            num_scalar_prefetch=1,
+            grid=(pairs, 3),
+            in_specs=[
+                spec(0),
+                spec(1),
+                spec(2),
+                pl.BlockSpec((length, PAIR), lambda j, s, r: (0, j)),
+                pl.BlockSpec((length, PAIR), lambda j, s, r: (0, j)),
+                pl.BlockSpec((1, 8, length), lambda j, s, r: (j, 0, 0)),
+            ],
+            out_specs=pl.BlockSpec((length, PAIR), lambda j, s, r: (0, s * pairs + j)),
+            scratch_shapes=[pltpu.VMEM((length, PAIR), BF)] * 5
+            + [pltpu.VMEM((length, PAIR), F32)] * 2
+            + [pltpu.VMEM((length, PAIR), BF)] * 2,
+        ),
+        name="self_attend_back",
+        cost_estimate=pl.CostEstimate(
+            flops=40 * length * length * PAIR * pairs // 3,
+            transcendentals=length * length * pairs,
+            bytes_accessed=16 * length * PAIR * pairs,
+        ),
+    )(t, qkv, qkv, qkv, mixed, d_mixed, lse)
+
+
+def spread_heads(value):
+    count = QUAD // HD
+    return jnp.concatenate([only(value, lanes_of(QUAD, head)) for head in range(count)], axis=0)
+
+
+def cross_kernel(q_ref, k_ref, v_ref, o_ref, lse_ref):
+    keys = k_ref.shape[0]
+    scores = mm(spread_heads(k_ref[...] * BF(0.125)), q_ref[...], NT)
+    powers, totals = [], []
+    for head in range(QUAD // HD):
+        score = scores[head * keys : (head + 1) * keys, :]
+        top = jnp.max(score, axis=0, keepdims=True)
+        power = jnp.exp(score - top)
+        total = jnp.sum(power, axis=0, keepdims=True)
+        lse_ref[0, head : head + 1, :] = top + jnp.log(total)
+        powers.append(power.astype(BF))
+        totals.append(total)
+    mixed = mm(spread_heads(v_ref[...]), jnp.concatenate(powers, axis=0), TN)
+    scaled = [
+        mixed[head * HD : (head + 1) * HD, :] / totals[head] for head in range(QUAD // HD)
+    ]
+    o_ref[...] = jnp.concatenate(scaled, axis=0).T.astype(BF)
+
+
+def cross_specs(rows, keys, quads):
+    return [
+        pl.BlockSpec((rows, QUAD), lambda j: (0, j)),
+        pl.BlockSpec((keys, QUAD), lambda j: (0, j)),
+        pl.BlockSpec((keys, QUAD), lambda j: (0, j)),
+    ]
+
+
+def cross_forward(query, key, value):
+    rows, width = query.shape
+    keys = key.shape[0]
+    quads = width // QUAD
+    return pl.pallas_call(
+        cross_kernel,
+        grid=(quads,),
+        out_shape=(
+            jax.ShapeDtypeStruct((rows, width), BF),
+            jax.ShapeDtypeStruct((quads, 8, rows), F32),
+        ),
+        in_specs=cross_specs(rows, keys, quads),
+        out_specs=[
+            pl.BlockSpec((rows, QUAD), lambda j: (0, j)),
+            pl.BlockSpec((1, 8, rows), lambda j: (j, 0, 0)),
+        ],
+        name="cross_attend",
+        cost_estimate=pl.CostEstimate(
+            flops=4 * rows * QUAD * width, transcendentals=rows * width, bytes_accessed=4 * rows * width
+        ),
+    )(query, key, value)
+
+
+def cross_back_kernel(q_ref, k_ref, v_ref, o_ref, do_ref, lse_ref, dq_ref, dk_ref, dv_ref):
+    keys = k_ref.shape[0]
+    count = QUAD // HD
+    query, grad = q_ref[...], do_ref[...]
+    key = spread_heads(k_ref[...] * BF(0.125))
+    scores = mm(key, query, NT)
+    d_powers = mm(spread_heads(v_ref[...]), grad, NT)
+    product = (grad.astype(F32) * o_ref[...].astype(F32)).T
+    weights, d_scores = [], []
+    for head in range(count):
+        group = slice(head * keys, (head + 1) * keys)
+        drop = jnp.sum(product[head * HD : (head + 1) * HD, :], axis=0, keepdims=True)
+        power = jnp.exp(scores[group, :] - lse_ref[0, head : head + 1, :])
+        weights.append(power.astype(BF))
+        d_scores.append((power * (d_powers[group, :] - drop)).astype(BF))
+    weights = jnp.concatenate(weights, axis=0)
+    d_scores = jnp.concatenate(d_scores, axis=0)
+    dq_ref[...] = mm(key, d_scores, TN).T.astype(BF)
+    d_key = mm(d_scores, query, NN)
+    d_value = mm(weights, grad, NN)
+    for ref, found, scale in ((dk_ref, d_key, 0.125), (dv_ref, d_value, 1.0)):
+        total = None
+        for head in range(count):
+            term = only(found[head * keys : (head + 1) * keys, :], lanes_of(QUAD, head))
+            total = term if total is None else total + term
+        ref[...] = total * scale
+
+
+def cross_backward(query, key, value, mixed, d_mixed, lse):
+    rows, width = query.shape
+    keys = key.shape[0]
+    quads = width // QUAD
+    wide = pl.BlockSpec((rows, QUAD), lambda j: (0, j))
+    return pl.pallas_call(
+        cross_back_kernel,
+        grid=(quads,),
+        out_shape=(
+            jax.ShapeDtypeStruct((rows, width), BF),
+            jax.ShapeDtypeStruct((keys, width), F32),
+            jax.ShapeDtypeStruct((keys, width), F32),
+        ),
+        in_specs=cross_specs(rows, keys, quads)
+        + [wide, wide, pl.BlockSpec((1, 8, rows), lambda j: (j, 0, 0))],
+        out_specs=[
+            wide,
+            pl.BlockSpec((keys, QUAD), lambda j: (0, j)),
+            pl.BlockSpec((keys, QUAD), lambda j: (0, j)),
+        ],
+        name="cross_attend_back",
+        cost_estimate=pl.CostEstimate(
+            flops=10 * rows * QUAD * width, transcendentals=rows * width, bytes_accessed=8 * rows * width
+        ),
+    )(query, key, value, mixed, d_mixed, lse)
+
+
+FF_STEP = 1024
+FF_PART = 256
+
+
+def ffn_kernel(n_ref, g_ref, wi_ref, wo_ref, *refs):
+    act_ref, din_ref = refs[-2:]
+    for part in range(wi_ref.shape[1] // FF_PART):
+        cols = slice(part * FF_PART, (part + 1) * FF_PART)
+        inner = mm(n_ref[...], wi_ref[:, cols], NN)
+        d_act = mm(g_ref[...], wo_ref[:, cols], NN)
+        phi = 0.5 + 0.5 * lax.erf(inner * (1.0 / math.sqrt(2.0)))
+        bell = jnp.exp(inner * inner * -0.5) * (1.0 / math.sqrt(2.0 * math.pi))
+        act_ref[:, cols] = (inner * phi).astype(BF)
+        din_ref[:, cols] = (d_act * (phi + inner * bell)).astype(BF)
+
+
+def ffn_middle(normed, grads, weights, block, blocks, kept=()):
+    rows, width = normed.shape
+    hidden = weights.shape[1] // 2
+    steps = hidden // FF_STEP
+    out_shape = jax.ShapeDtypeStruct((rows * blocks, hidden), BF)
+    whole = pl.BlockSpec((rows, width), lambda j: (0, 0))
+    out_spec = pl.BlockSpec((rows, FF_STEP), lambda j: (block, j))
+    return pl.pallas_call(
+        ffn_kernel,
+        grid=(steps,),
+        out_shape=(out_shape, out_shape),
+        in_specs=[
+            whole,
+            whole,
+            pl.BlockSpec((width, FF_STEP), lambda j: (0, j)),
+            pl.BlockSpec((width, FF_STEP), lambda j: (0, steps + j)),
+        ]
+        + [pl.BlockSpec(memory_space=pl.ANY)] * len(kept),
+        out_specs=[out_spec, out_spec],
+        input_output_aliases={4 + i: i for i in range(len(kept))},
+        name="ffn_middle",
+        cost_estimate=pl.CostEstimate(
+            flops=4 * rows * width * hidden,
+            transcendentals=2 * rows * hidden,
+            bytes_accessed=4 * width * hidden + 4 * rows * hidden,
+        ),
+    )(normed, grads, weights, weights, *kept)
+
+
+def stats_of(value):
+    mean = jnp.mean(value, axis=-1, keepdims=True)
+    centred = value - mean
+    spread = jnp.mean(centred * centred, axis=-1, keepdims=True)
+    return centred, lax.rsqrt(spread + EPS)
+
+
+def norm_grad(value, gain, incoming):
+    centred, scale = stats_of(value)
+    hat = centred * scale
+    scaled = incoming * gain
+    mean = jnp.mean(scaled, axis=-1, keepdims=True)
+    along = jnp.mean(scaled * hat, axis=-1, keepdims=True)
+    return (
+        scale * (scaled - mean - hat * along),
+        jnp.sum(incoming * hat, axis=0),
+        jnp.sum(incoming, axis=0),
+    )
+
+
+def on_pair(
+    inputs,
+    text_states,
+    self_query,
+    self_key,
+    self_value,
+    self_output,
+    cross_query,
+    cross_key,
+    cross_value,
+    cross_output,
+    inner_weight,
+    outer_weight,
+    norm_gains,
+    norm_shifts,
+    cotangent,
+    *,
+    groups,
+):
+    rows, width = inputs.shape
+    half = width // 2
+    hidden = inner_weight.shape[1]
+    shard = self_query.shape[0]
+    tensor = lax.axis_index("tensor")
+    place = lax.axis_index("dp")
+    core, column = place % 2, (place // 2) % 2
+    core_swap = [(i, i ^ 1) for i in range(groups)]
+    column_swap = [(i, i ^ 2) for i in range(groups)]
+    lines = [[i + 4 * j for j in range(groups // 4)] for i in range(4)]
+    t_ref = tensor.astype(jnp.int32).reshape(1)
+
+    def peer(value):
+        return lax.ppermute(value, "tensor", [(0, 1), (1, 0)])
+
+    def gather(parts):
+        return lax.all_gather(jnp.concatenate(parts, axis=1), "dp", axis=0, tiled=True)
+
+    def halved(value, bit, swap):
+        send = lax.dynamic_index_in_dim(value, 1 - bit, 1, False)
+        keep = lax.dynamic_index_in_dim(value, bit, 1, False)
+        got = lax.ppermute(send, "dp", swap)
+        return (keep.astype(F32) + got.astype(F32)).astype(BF)
+
+    def core_sum(grad):
+        cut = grad.reshape(groups // 2, 2, shard, grad.shape[1])
+        return halved(cut, core, core_swap)
+
+    def column_sum(grad):
+        cut = grad.reshape(groups // 4, 2, shard, grad.shape[-1])
+        return halved(cut, column, column_swap)
+
+    def line_sum(parts):
+        whole = jnp.concatenate(parts, axis=-1) if len(parts) > 1 else parts[0]
+        whole = whole.reshape(-1, whole.shape[-1])
+        return lax.psum_scatter(
+            whole, "dp", scatter_dimension=0, tiled=True, axis_index_groups=lines
+        ).astype(F32)
+
+    def pair_sum(grad):
+        got = peer(grad[..., half:])
+        return (grad[..., :half].astype(F32) + got.astype(F32)).astype(BF)
+
+    inputs_peer = peer(inputs)
+    cross_two = jnp.concatenate([cross_query, cross_output.T], axis=1)
+    cross_peer = peer(cross_two)
+    grads_peer = peer(cotangent)
+
+    first = gather([self_query, self_key, self_value, self_output.T, cross_key, cross_value])
+    second = gather(
+        [cross_query, cross_peer[:, :half], cross_two[:, half:], cross_peer[:, half:]]
+    )
+    third = gather([inner_weight, outer_weight.T])
+    w_qkv = first[:, : 3 * half]
+    w_self_out = first[:, 3 * half : 4 * half]
+    w_text = first[:, 4 * half :]
+    w_cross_query = second[:, :width]
+    w_cross_out = second[:, width:]
+    w_inner = third[:, :hidden]
+    w_outer = third[:, hidden:]
+
+    start = jnp.concatenate([inputs, inputs_peer], axis=0).astype(F32)
+    normed1 = norm_rows(start, norm_gains[0], norm_shifts[0]).astype(BF)
+    qkv = mm(normed1, w_qkv, NN).astype(BF)
+    text = text_states.reshape(-1, width)
+    text_own = mm(text, w_text, NN).astype(BF)
+    text_peer = peer(text_own)
+    key2 = jnp.concatenate([text_own[:, :half], text_peer[:, :half]], axis=1)
+    value2 = jnp.concatenate([text_own[:, half:], text_peer[:, half:]], axis=1)
+    mixed1, lse1 = self_forward(t_ref, qkv)
+    away = peer(mm(mixed1[rows:], w_self_out, NT).astype(BF))
+    home = mm(mixed1[:rows], w_self_out, NT)
+    state1 = inputs.astype(F32) + home + away.astype(F32)
+
+    normed2 = norm_rows(state1, norm_gains[1], norm_shifts[1]).astype(BF)
+    query2 = mm(normed2, w_cross_query, NN).astype(BF)
+    mixed2, lse2 = cross_forward(query2, key2, value2)
+    state2 = state1 + mm(mixed2, w_cross_out, NT)
+
+    normed3 = norm_rows(state2, norm_gains[2], norm_shifts[2]).astype(BF)
+    normed3_peer = peer(normed3)
+    active, d_inner = ffn_middle(normed3, cotangent, third, 0, 2)
+    active, d_inner = ffn_middle(normed3_peer, grads_peer, third, 1, 2, (active, d_inner))
+    back3_away = peer(mm(d_inner[rows:], w_inner, NT).astype(BF))
+    grads3 = jnp.concatenate([cotangent, grads_peer], axis=0)
+    d_outer = column_sum(core_sum(mm(grads3, active, TN).astype(BF)))
+    outer_sum = line_sum([d_outer])
+    rows3 = jnp.concatenate([normed3, normed3_peer], axis=0)
+    d_innerw = column_sum(core_sum(mm(rows3, d_inner, TN).astype(BF)))
+    inner_sum = line_sum([d_innerw])
+    out_away = peer(mm(active[rows:], w_outer, NT).astype(BF))
+    output = (state2 + mm(active[:rows], w_outer, NT) + out_away.astype(F32)).astype(BF)
+
+    back3 = mm(d_inner[:rows], w_inner, NT) + back3_away.astype(F32)
+    d_state2, gain3, shift3 = norm_grad(state2, norm_gains[2], back3)
+    grad2 = cotangent.astype(F32) + d_state2
+    g2 = grad2.astype(BF)
+    d_mixed2 = mm(g2, w_cross_out, NN).astype(BF)
+    d_query2, d_key2, d_value2 = cross_backward(query2, key2, value2, mixed2, d_mixed2, lse2)
+    back2 = mm(d_query2, w_cross_query, NT)
+    d_state1, gain2, shift2 = norm_grad(state1, norm_gains[1], back2)
+    grad1 = grad2 + d_state1
+    g1 = grad1.astype(BF)
+    g1_peer = peer(g1)
+
+    d_text_send = jnp.concatenate([d_key2[:, half:], d_value2[:, half:]], axis=1)
+    d_text_keep = jnp.concatenate([d_key2[:, :half], d_value2[:, :half]], axis=1)
+    d_text = (d_text_keep + peer(d_text_send.astype(BF)).astype(F32)).astype(BF)
+    d_coutput = pair_sum(core_sum(mm(g2, mixed2, TN).astype(BF)))
+    d_cquery = pair_sum(core_sum(mm(normed2, d_query2, TN).astype(BF)))
+    d_ckv = core_sum(mm(text, d_text, TN).astype(BF))
+    cross_sum = line_sum([column_sum(v) for v in (d_coutput, d_cquery, d_ckv)])
+    text_terms = mm(d_text, w_text, NT).astype(BF)
+    text_keep = lax.dynamic_slice_in_dim(text_terms, tensor * half, half, 1)
+    text_send = lax.dynamic_slice_in_dim(text_terms, (1 - tensor) * half, half, 1)
+    text_grad = (text_keep.astype(F32) + peer(text_send).astype(F32)).reshape(1, -1, half)
+
+    grads1 = jnp.concatenate([g1, g1_peer], axis=0)
+    d_mixed1 = mm(grads1, w_self_out, NN).astype(BF)
+    d_soutput = column_sum(core_sum(mm(grads1, mixed1, TN).astype(BF)))
+    so_sum = line_sum([d_soutput])
+    d_qkv = self_backward(t_ref, qkv, mixed1, d_mixed1, lse1)
+    qkv_sum = line_sum([column_sum(core_sum(mm(normed1, d_qkv, TN).astype(BF)))])
+    back1_away = peer(mm(d_qkv[rows:], w_qkv, NT).astype(BF))
+    back1 = mm(d_qkv[:rows], w_qkv, NT) + back1_away.astype(F32)
+    d_start, gain1, shift1 = norm_grad(inputs.astype(F32), norm_gains[0], back1)
+    input_grad = grad1 + d_start
+
+    small = jnp.stack([gain1, gain2, gain3, shift1, shift2, shift3])
+    small = small + peer(small)
+    bit = 1
+    while bit < groups:
+        small = small + lax.ppermute(small, "dp", [(i, i ^ bit) for i in range(groups)])
+        bit *= 2
+    return (
+        output,
+        input_grad,
+        text_grad,
+        qkv_sum[:, :half],
+        qkv_sum[:, half : 2 * half],
+        qkv_sum[:, 2 * half :],
+        so_sum.T,
+        cross_sum[:, half : 2 * half],
+        cross_sum[:, 2 * half : 3 * half],
+        cross_sum[:, 3 * half :],
+        cross_sum[:, :half].T,
+        inner_sum,
+        outer_sum.T,
+        small[:3],
+        small[3:],
+    )
+
+
+def pairs_up(mesh, inputs, text_states, inner_weight):
+    groups, sides = mesh.shape["dp"], mesh.shape["tensor"]
+    width = inputs.shape[1]
+    return (
+        sides == 2
+        and groups >= 4
+        and groups & (groups - 1) == 0
+        and text_states.shape[0] == groups
+        and text_states.shape[1] == TEXT
+        and inputs.shape[0] == groups * LEN
+        and width % (2 * QUAD) == 0
+        and width % (32 * groups) in (0, 16 * groups)
+        and inner_weight.shape[1] % (2 * FF_STEP) == 0
+    )
+
+
 def solution(mesh):
     in_specs = (
         P(("dp", "tensor"), None),
@@ -329,6 +899,13 @@
         P(),
         P(),
     )
-    return jax.shard_map(
-        on_device, mesh=mesh, in_specs=in_specs, out_specs=out_specs, check_vma=False
-    )
+
+    def layer(*args):
+        body = on_device
+        if pairs_up(mesh, args[0], args[1], args[10]):
+            body = partial(on_pair, groups=mesh.shape["dp"])
+        return jax.shard_map(
+            body, mesh=mesh, in_specs=in_specs, out_specs=out_specs, check_vma=False
+        )(*args)
+
+    return layer

time: 2210 us -> 819 us (0.37)
  waiting for transfers between devices: 1620 us -> 362 us
  matrix products: 354 us -> 172 us
  Pallas kernels: 0 us -> 109 us
  other arithmetic: 133 us -> 70.3 us
  blocking collectives: 40.4 us -> 0 us
  starting transfers between devices: 3.86 us -> 33.7 us
    reduce_scatter x15 -> x5, waiting for transfers between devices: 867 us -> 0.01 us  [line_sum(): lax.psum_scatter(whole, 'dp', scatter_dimension=0, tiled=True, axis_index...]
    all_gather x16 -> x3, waiting for transfers between devices: 617 us -> 97.9 us  [gather(): lax.all_gather(jnp.concatenate(parts, axis=1), 'dp', axis=0, tiled=True)]
    ppermute x0 -> x33, waiting for transfers between devices: none -> 264 us  [the longest x15 178 us: peer(): return lax.ppermute(value, 'tensor', [(0, 1), (1, 0)])]
    dot_general x42 -> x23, matrix products: 354 us -> 172 us  [mm(): return lax.dot_general(left, right, dims, preferred_element_type=F32)]
    unnamed x35 -> x8, waiting for transfers between devices: 136 us -> 0.13 us
    pallas_call x0 -> x6, Pallas kernels: none -> 109 us  [the longest x1 39.7 us: self_backward(): pl.pallas_call(self_back_kernel, out_shape=jax.ShapeDtypeStruct((length,...]
    psum x1 -> x0, blocking collectives: 40.4 us -> none  [on_device(): lax.psum((jnp.stack([gain_one, gain_two, gain_three]), jnp.stack([shift_o...]
    reduce_sum x8 -> x2, other arithmetic: 38.6 us -> 0.83 us  [the longest x1 0.55 us: stats_of(): spread = jnp.mean(centred * centred, axis=-1, keepdims=True)]
  transfers between devices with their start and end apart: 33 -> 41, of which waited for: 30 -> 18; matrix products, arithmetic and copies ran while one was open for 18% -> 32% of each run, Pallas kernels for 0% -> 11%
where the time goes in v1:
time: 819 us; the launch traced here: 811 us
  waiting for transfers between devices  362 us (44%)
  matrix products  172 us (21%)
  Pallas kernels  109 us (13%)
  other arithmetic  70.3 us (9%)
  local copies, waits for them, and re-layouts  47.2 us (6%)
  starting transfers between devices  33.7 us (4%)
  between operations  15.7 us (2%)
    ppermute x15, waiting for transfers between devices, peer(): return lax.ppermute(value, 'tensor', [(0, 1), (1, 0)])  178 us
    dot_general x23, matrix products, mm(): return lax.dot_general(left, right, dims, preferred_element_type=F32)  172 us
    all_gather x3, waiting for transfers between devices, gather(): lax.all_gather(jnp.concatenate(parts, axis=1), 'dp', axis=0, tiled=True)  97.9 us
    ppermute x14, waiting for transfers between devices, halved(): got = lax.ppermute(send, 'dp', swap)  74 us
    pallas_call x1, Pallas kernels, self_backward(): pl.pallas_call(self_back_kernel, out_shape=jax.ShapeDtypeStruct((length,...  39.7 us
    convert_element_type x14, other arithmetic, halved(): return (keep.astype(F32) + got.astype(F32)).astype(BF)  37 us
    pallas_call x2, Pallas kernels, ffn_middle(): pl.pallas_call(ffn_kernel, grid=(steps,), out_shape=(out_shape, out_shape...  34 us
    pallas_call x1, Pallas kernels, self_forward(): pl.pallas_call(self_kernel, out_shape=(jax.ShapeDtypeStruct((length, pair...  21.3 us
  transfers between devices with their start and end apart: 41, of which 18 were waited for; matrix products, arithmetic and copies ran while one was open for 32% of the time, Pallas kernels for 11%

profile of v1, /device:TPU:0, one launch (start us, length us, event | category | flops | bytes accessed | tf_op | source)
XLA Modules:
  0.0 810.7 jit_solution(9686534458815770767)
XLA Ops:
  18.2 7.0 collective-permute-done.2
  29.3 33.7 %collective-permute-done = bf16[512,1536]{1,0:T(8,128)(2,1)S(1)} collective-permute-done((bf16[512,1536]{1,0:T(8,128)(2,1)S(1)}, bf16[512,1536]{1,0:T(8,128)(2,1)S(1)}, u32[]{:S(2)}, u32[]{:S(2)}) %collective-permute-start) | collective-permute-done | bytes 1572896 | tf_op jit(solution)/shard_map/ppermute | solution.py:711
  65.8 61.2 %all-gather.4.cloned.1.call-done = bf16[1536,4608]{1,0:T(8,128)(2,1)} async-done(((bf16[96,4608]{1,0:T(8,128)(2,1)}), bf16[1536,4608]{1,0:T(8,128)(2,1)}) %all-gather.4.cloned.1.call-update) | async-done | bytes 14155792 | tf_op jit(solution)/shard_map/all_gather | solution.py:714
  126.9 14.0 %convolution_convert_fusion.6.q_ref.k_ref.v_ref = bf16[1024,2304]{1,0:T(8,128)(2,1)} fusion(bf16[1536,4608]{1,0:T(8,128)(2,1)} %all-gather.4.cloned.1.call-done, f32[1536]{0:T(1024)S(1)} %get-tuple-element.53, f32[1536]{0:T(1024)S(1)} %get-tuple-element.50, f32[1024]{0:T(1024)S(1)} %add_rsqrt_fusion, f32[1024]{0:T(1024)S(1)} %broadcast_multiply_fusion, ...), kind=kOutput, calls=%fused_computation.28 | convolution fusion | flops 7264272384 | bytes 14962688 | tf_op jit(solution)/shard_map/dot_general | solution.py:310
  140.9 21.3 %self_attend.1 = (bf16[1024,768]{1,0:T(8,128)(2,1)}, f32[6,8,1024]{2,1,0:T(8,128)}) custom-call(s32[1]{0:T(128)} %bitcast.t_ref, bf16[1024,2304]{1,0:T(8,128)(2,1)} %convolution_convert_fusion.6.q_ref.k_ref.v_ref, bf16[1024,2304]{1,0:T(8,128)(2,1)} %convolution_convert_fusion.6.q_ref.k_ref.v_ref, bf16[1024,2304]{1,0:T(8,128)(2,1)} %convolution_convert_fusion.6.q_ref.k_ref.v_ref), custom_call_target="tpu_custom_call" | custom-call | flops 4294967296 | bytes 6291456 | tf_op jit(solution)/shard_map/self_attend/pallas_call | solution.py:384
  173.0 67.9 %collective-permute-done.3 = bf16[64,1536]{1,0:T(8,128)(2,1)S(1)} collective-permute-done((bf16[64,1536]{1,0:T(8,128)(2,1)S(1)}, bf16[64,1536]{1,0:T(8,128)(2,1)S(1)}, u32[]{:S(2)}, u32[]{:S(2)}) %collective-permute-start.3) | collective-permute-done | bytes 196640 | tf_op jit(solution)/shard_map/ppermute | solution.py:711
  247.2 7.1 fusion.78.q_ref
  254.4 6.4 cross_attend.1
  260.8 6.7 fusion.149
  271.1 36.8 %all-gather.8.cloned.1.call-done.wi_ref.wo_ref = bf16[1536,6144]{1,0:T(8,128)(2,1)} async-done(((bf16[96,6144]{1,0:T(8,128)(2,1)}), bf16[1536,6144]{1,0:T(8,128)(2,1)}) %all-gather.8.cloned.1.call-update) | async-done | bytes 18874384 | tf_op jit(solution)/shard_map/all_gather | solution.py:714
  307.8 16.9 %ffn_middle.2 = (bf16[1024,3072]{1,0:T(8,128)(2,1)}, bf16[1024,3072]{1,0:T(8,128)(2,1)}) custom-call(bf16[512,1536]{1,0:T(8,128)(2,1)} %add_convert_fusion.n_ref, bf16[512,1536]{1,0:T(8,128)(2,1)} %g_ref.1, bf16[1536,6144]{1,0:T(8,128)(2,1)} %all-gather.8.cloned.1.call-done.wi_ref.wo_ref, bf16[1536,6144]{1,0:T(8,128)(2,1)} %all-gather.8.cloned.1.call-done.wi_ref.wo_ref), custom_call_target="tpu_custom_call" | custom-call | flops 9663676416 | bytes 25165824 | tf_op jit(solution)/shard_map/ffn_middle/pallas_call | solution.py:637
  324.7 17.1 %ffn_middle.3 = (bf16[1024,3072]{1,0:T(8,128)(2,1)}, bf16[1024,3072]{1,0:T(8,128)(2,1)}) custom-call(bf16[512,1536]{1,0:T(8,128)(2,1)} %collective-permute-done.4.n_ref, bf16[512,1536]{1,0:T(8,128)(2,1)} %collective-permute-done.5.g_ref, bf16[1536,6144]{1,0:T(8,128)(2,1)} %all-gather.8.cloned.1.call-done.wi_ref.wo_ref, ...), custom_call_target="tpu_custom_call", output_to_operand_aliasing={{0}: (4, {}), {1}: (5, {})} | custom-call | flops 9663676416 | bytes 25165824 | tf_op jit(solution)/shard_map/ffn_middle/pallas_call | solution.py:637
  341.8 9.6 %fusion.92 = bf16[512,1536]{1,0:T(8,128)(2,1)S(1)} fusion(bf16[1536,6144]{1,0:T(8,128)(2,1)} %all-gather.8.cloned.1.call-done.wi_ref.wo_ref, bf16[1024,3072]{1,0:T(8,128)(2,1)} %get-tuple-element.31), kind=kOutput, calls=%fused_computation.110 | convolution fusion | flops 4832624640 | bytes 14155776 | tf_op jit(solution)/shard_map/dot_general | solution.py:310
  353.0 13.1 %convolution_convert_fusion.1 = bf16[1536,3072]{1,0:T(8,128)(2,1)S(1)} fusion(bf16[1024,3072]{1,0:T(8,128)(2,1)} %get-tuple-element.31, bf16[512,1536]{1,0:T(8,128)(2,1)} %collective-permute-done.4.n_ref, bf16[512,1536]{1,0:T(8,128)(2,1)} %add_convert_fusion.n_ref), kind=kOutput, calls=%fused_computation.1 | convolution fusion | flops 9674686464 | bytes 18874368 | tf_op jit(solution)/shard_map/dot_general | solution.py:310
  371.2 14.5 %convolution_convert_fusion = bf16[1536,3072]{1,0:T(8,128)(2,1)} fusion(bf16[1024,3072]{1,0:T(8,128)(2,1)S(1)} %bitcast.158, bf16[512,1536]{1,0:T(8,128)(2,1)} %collective-permute-done.5.g_ref, bf16[512,1536]{1,0:T(8,128)(2,1)} %g_ref.1), kind=kOutput, calls=%fused_computation | convolution fusion | flops 9674686464 | bytes 18874368 | tf_op jit(solution)/shard_map/dot_general | solution.py:310
  388.1 10.2 %multiply_reduce_fusion = (f32[1536]{0:T(1024)}, f32[512]{0:T(512)S(1)}, f32[512]{0:T(512)S(1)}, f32[1536]{0:T(1024)}, f32[512,1536]{1,0:T(8,128)S(1)}) fusion(f32[512,1536]{1,0:T(8,128)S(1)} %get-tuple-element.74, f32[512]{0:T(512)S(1)} %add_rsqrt_fusion.2, f32[512]{0:T(512)S(1)} %broadcast_multiply_fusion.8, f32[1536]{0:T(1024)S(1)} %get-tuple-element.49, ...), kind=kOutput, calls=%fused_computation.88 | convolution fusion | flops 4840484864 | bytes 20473856 | tf_op jit(solution)/shard_map/dot_general | solution.py:310
  400.8 7.2 fusion.81.do_ref
  408.0 7.4 cross_attend_back.1
  438.6 36.2 %collective-permute-done.10 = bf16[64,1536]{1,0:T(8,128)(2,1)S(1)} collective-permute-done((bf16[64,1536]{1,0:T(8,128)(2,1)S(1)}, bf16[64,1536]{1,0:T(8,128)(2,1)S(1)}, u32[]{:S(2)}, u32[]{:S(2)}) %collective-permute-start.10) | collective-permute-done | bytes 196640 | tf_op jit(solution)/shard_map/ppermute | solution.py:711
  499.2 6.3 fusion.120.do_ref
  505.5 6.8 collective-permute-done.15
  519.8 21.4 %collective-permute-done.17 = bf16[8,96,768]{2,1,0:T(8,128)(2,1)} collective-permute-done((bf16[8,96,768]{2,1,0:T(8,128)(2,1)}, bf16[8,96,768]{2,1,0:T(8,128)(2,1)}, u32[]{:S(2)}, u32[]{:S(2)}) %collective-permute-start.17) | collective-permute-done | bytes 1179680 | tf_op jit(solution)/shard_map/ppermute | solution.py:711
  550.3 11.0 %collective-permute-done.18 = bf16[4,96,768]{2,1,0:T(8,128)(2,1)S(1)} collective-permute-done((bf16[4,96,768]{2,1,0:T(8,128)(2,1)S(1)}, bf16[4,96,768]{2,1,0:T(8,128)(2,1)S(1)}, u32[]{:S(2)}, u32[]{:S(2)}) %collective-permute-start.18) | collective-permute-done | bytes 589856 | tf_op jit(solution)/shard_map/ppermute | solution.py:719
  572.1 39.7 %self_attend_back.1 = bf16[1024,2304]{1,0:T(8,128)(2,1)} custom-call(s32[1]{0:T(128)} %bitcast.t_ref, bf16[1024,2304]{1,0:T(8,128)(2,1)} %convolution_convert_fusion.6.q_ref.k_ref.v_ref, bf16[1024,2304]{1,0:T(8,128)(2,1)} %convolution_convert_fusion.6.q_ref.k_ref.v_ref, bf16[1024,2304]{1,0:T(8,128)(2,1)} %convolution_convert_fusion.6.q_ref.k_ref.v_ref, ...), custom_call_target="tpu_custom_call" | custom-call | flops 10737418240 | bytes 12582912 | tf_op jit(solution)/shard_map/self_attend_back/pallas_call | solution.py:476
  611.9 12.4 %convolution_convert_fusion.2 = bf16[1536,2304]{1,0:T(8,128)(2,1)} fusion(bf16[1024,2304]{1,0:T(8,128)(2,1)} %self_attend_back.1, f32[1536]{0:T(1024)S(1)} %copy-done.54, f32[1536]{0:T(1024)S(1)} %copy-done.38, f32[1024]{0:T(1024)S(1)} %copy-done.58, f32[1024]{0:T(1024)S(1)} %copy-done.46, bf16[512,1536]{1,0:T(8,128)(2,1)S(1)} %copy-done.20, ...), kind=kOutput, calls=%fused_computation.2 | convolution fusion | flops 7265452032 | bytes 14962688 | tf_op jit(solution)/shard_map/dot_general | solution.py:310
  645.1 8.9 %fusion.84 = bf16[512,1536]{1,0:T(8,128)(2,1)} fusion(bf16[1536,4608]{1,0:T(8,128)(2,1)} %all-gather.4.cloned.1.call-done, bf16[1024,2304]{1,0:T(8,128)(2,1)} %self_attend_back.1), kind=kOutput, calls=%fused_computation.107 | convolution fusion | flops 3624665088 | bytes 11010048 | tf_op jit(solution)/shard_map/dot_general | solution.py:310
  655.5 41.0 %collective-permute-done.27 = bf16[4,96,3072]{2,1,0:T(8,128)(2,1)} collective-permute-done((bf16[4,96,3072]{2,1,0:T(8,128)(2,1)}, bf16[4,96,3072]{2,1,0:T(8,128)(2,1)}, u32[]{:S(2)}, u32[]{:S(2)}) %collective-permute-start.27) | collective-permute-done | bytes 2359328 | tf_op jit(solution)/shard_map/ppermute | solution.py:719
  708.9 11.3 %fusion.87 = bf16[512,1536]{1,0:T(8,128)(2,1)} fusion(bf16[1536,6144]{1,0:T(8,128)(2,1)} %all-gather.8.cloned.1.call-done.wi_ref.wo_ref, bf16[1024,3072]{1,0:T(8,128)(2,1)} %get-tuple-element.30), kind=kOutput, calls=%fused_computation.109 | convolution fusion | flops 4832624640 | bytes 14155776 | tf_op jit(solution)/shard_map/dot_general | solution.py:310
  726.4 8.8 %fusion.61 = (f32[1536]{0:T(1024)S(1)}, f32[512]{0:T(512)}, f32[512]{0:T(512)}, f32[1536]{0:T(1024)S(1)}, f32[512,1536]{1,0:T(8,128)}) fusion(bf16[512,1536]{1,0:T(8,128)(2,1)S(1)} %copy-done.3, f32[512]{0:T(512)S(1)} %copy-done.55, f32[512]{0:T(512)S(1)} %copy-done.43, f32[1536]{0:T(1024)S(1)} %copy-done.38, bf16[512,1536]{1,0:T(8,128)(2,1)} %collective-permute-done.9, ...), kind=kOutput, calls=%fused_computation.78 | convolution fusion | flops 3633311744 | bytes 15757312 | tf_op jit(solution)/shard_map/dot_general | solution.py:310
  737.3 10.8 %collective-permute-done.13 = bf16[4,96,2304]{2,1,0:T(8,128)(2,1)S(1)} collective-permute-done((bf16[4,96,2304]{2,1,0:T(8,128)(2,1)}, bf16[4,96,2304]{2,1,0:T(8,128)(2,1)S(1)}, u32[]{:S(2)}, u32[]{:S(2)}) %collective-permute-start.13) | collective-permute-done | bytes 1769504 | tf_op jit(solution)/shard_map/ppermute | solution.py:719
  751.3 6.4 collective-permute-done.6
  757.8 11.9 %fusion.73 = bf16[512,1536]{1,0:T(8,128)(2,1)} fusion(bf16[512,1536]{1,0:T(8,128)(2,1)} %collective-permute-done.6, f32[512,1536]{1,0:T(8,128)} %copy-done.4, bf16[1536,6144]{1,0:T(8,128)(2,1)} %all-gather.8.cloned.1.call-done.wi_ref.wo_ref, bf16[1024,3072]{1,0:T(8,128)(2,1)} %get-tuple-element.30), kind=kOutput, calls=%fused_computation.104 | convolution fusion | flops 4834983936 | bytes 18874368 | tf_op jit(solution)/shard_map/dot_general | solution.py:310
  (346 shorter events, 204.1 us)
Async XLA Ops:
  7.2 119.7 %all-gather.4.cloned.1.call-start = ((), (), s32[]{:S(2)}) async-start(), calls=%async_computation.5 | async-start | bytes 15040512 | tf_op jit(solution)/shard_map/all_gather | solution.py:714
  13.9 233.3 %all-gather.6.cloned.1.call-start = ((), (), s32[]{:S(2)}) async-start(), calls=%async_computation.6 | async-start | bytes 10027008 | tf_op jit(solution)/shard_map/all_gather | solution.py:714
  26.1 281.7 %all-gather.8.cloned.1.call-start = ((), (), s32[]{:S(2)}) async-start(), calls=%async_computation.7 | async-start | bytes 20054016 | tf_op jit(solution)/shard_map/all_gather | solution.py:714
  27.3 764.3 %reduce-scatter.8.cloned.1.call-start = ((), (), s32[]{:S(2)}) async-start(), calls=%async_computation.9 | async-start | bytes 737280 | tf_op jit(solution)/shard_map/reduce_scatter | solution.py:733
  27.3 35.6 %collective-permute-start = (bf16[512,1536]{1,0:T(8,128)(2,1)S(1)}, bf16[512,1536]{1,0:T(8,128)(2,1)S(1)}, u32[]{:S(2)}, u32[]{:S(2)}) collective-permute-start(bf16[512,1536]{1,0:T(8,128)(2,1)S(1)} %copy-done.2), channel_id=1, source_target_pairs={{0,1},{1,0},{2,3},{3,2},{4,5},{5,4},{6,7},{7,6},{8,9},{9,8},{10,11... | collective-permute-start | bytes 4718600 | tf_op jit(solution)/shard_map/ppermute | solution.py:711
  166.4 75.2 %collective-permute-start.1 = (bf16[512,1536]{1,0:T(8,128)(2,1)S(1)}, bf16[512,1536]{1,0:T(8,128)(2,1)S(1)}, u32[]{:S(2)}, u32[]{:S(2)}) collective-permute-start(bf16[512,1536]{1,0:T(8,128)(2,1)S(1)} %convolution_convert_fusion.8), channel_id=1, source_target_pairs={{0,1},{1,0},{2,3},{3,2},{4,5},{5,4},{6,7},{7,6},{8,9},{9,8},{10,11... | collective-permute-start | bytes 4718600 | tf_op jit(solution)/shard_map/ppermute | solution.py:711
  167.6 157.1 %collective-permute-start.5 = (bf16[512,1536]{1,0:T(8,128)(2,1)}, bf16[512,1536]{1,0:T(8,128)(2,1)}, u32[]{:S(2)}, u32[]{:S(2)}) collective-permute-start(bf16[512,1536]{1,0:T(8,128)(2,1)} %g_ref.1), channel_id=1, source_target_pairs={{0,1},{1,0},{2,3},{3,2},{4,5},{5,4},{6,7},{7,6},{8,9},{9,8},{10,11... | collective-permute-start | bytes 4718600 | tf_op jit(solution)/shard_map/ppermute | solution.py:711
  171.9 69.0 %collective-permute-start.3 = (bf16[64,1536]{1,0:T(8,128)(2,1)S(1)}, bf16[64,1536]{1,0:T(8,128)(2,1)S(1)}, u32[]{:S(2)}, u32[]{:S(2)}) collective-permute-start(bf16[64,1536]{1,0:T(8,128)(2,1)S(1)} %fusion.111), channel_id=1, source_target_pairs={{0,1},{1,0},{2,3},{3,2},{4,5},{5,4},{6,7},{7,6},{8,9},{9,8},{10,11... | collective-permute-start | bytes 589832 | tf_op jit(solution)/shard_map/ppermute | solution.py:711
  269.8 55.0 %collective-permute-start.4 = (bf16[512,1536]{1,0:T(8,128)(2,1)}, bf16[512,1536]{1,0:T(8,128)(2,1)}, u32[]{:S(2)}, u32[]{:S(2)}) collective-permute-start(bf16[512,1536]{1,0:T(8,128)(2,1)} %add_convert_fusion.n_ref), channel_id=1, source_target_pairs={{0,1},{1,0},{2,3},{3,2},{4,5},{5,4},{6,7},{7,6},{8,9},{9,8},{10,11... | collective-permute-start | bytes 4718600 | tf_op jit(solution)/shard_map/ppermute | solution.py:711
  351.5 36.6 %collective-permute-start.7 = (bf16[512,1536]{1,0:T(8,128)(2,1)S(1)}, bf16[512,1536]{1,0:T(8,128)(2,1)S(1)}, u32[]{:S(2)}, u32[]{:S(2)}) collective-permute-start(bf16[512,1536]{1,0:T(8,128)(2,1)S(1)} %fusion.92), channel_id=1, source_target_pairs={{0,1},{1,0},{2,3},{3,2},{4,5},{5,4},{6,7},{7,6},{8,9},{9,8},{10,11... | collective-permute-start | bytes 4718600 | tf_op jit(solution)/shard_map/ppermute | solution.py:711
  371.1 192.1 %collective-permute-start.24 = (bf16[8,96,3072]{2,1,0:T(8,128)(2,1)}, bf16[8,96,3072]{2,1,0:T(8,128)(2,1)}, u32[]{:S(2)}, u32[]{:S(2)}) collective-permute-start(bf16[8,96,3072]{2,1,0:T(8,128)(2,1)} %dynamic-slice_bitcast_fusion.1), channel_id=1, source_target_pairs={{0,2},{2,0},{4,6},{6,4},{8,10},{10,8},{12,14},{14,12},{16,18},{18,... | collective-permute-start | bytes 14155784 | tf_op jit(solution)/shard_map/ppermute | solution.py:719
  427.8 56.4 %collective-permute-start.19 = (bf16[8,96,1536]{2,1,0:T(8,128)(2,1)}, bf16[8,96,1536]{2,1,0:T(8,128)(2,1)}, u32[]{:S(2)}, u32[]{:S(2)}) collective-permute-start(bf16[8,96,1536]{2,1,0:T(8,128)(2,1)} %dynamic-slice_bitcast_fusion.6), channel_id=1, source_target_pairs={{0,2},{2,0},{4,6},{6,4},{8,10},{10,8},{12,14},{14,12},{16,18},{18,... | collective-permute-start | bytes 7077896 | tf_op jit(solution)/shard_map/ppermute | solution.py:719
  434.9 45.8 %collective-permute-start.8 = (bf16[512,1536]{1,0:T(8,128)(2,1)S(1)}, bf16[512,1536]{1,0:T(8,128)(2,1)S(1)}, u32[]{:S(2)}, u32[]{:S(2)}) collective-permute-start(bf16[512,1536]{1,0:T(8,128)(2,1)S(1)} %get-tuple-element.55), channel_id=1, source_target_pairs={{0,1},{1,0},{2,3},{3,2},{4,5},{5,4},{6,7},{7,6},{8,9},{9,8},{10,11... | collective-permute-start | bytes 4718600 | tf_op jit(solution)/shard_map/ppermute | solution.py:711
  436.4 38.4 %collective-permute-start.10 = (bf16[64,1536]{1,0:T(8,128)(2,1)S(1)}, bf16[64,1536]{1,0:T(8,128)(2,1)S(1)}, u32[]{:S(2)}, u32[]{:S(2)}) collective-permute-start(bf16[64,1536]{1,0:T(8,128)(2,1)S(1)} %pad_maximum_fusion.12), channel_id=1, source_target_pairs={{0,1},{1,0},{2,3},{3,2},{4,5},{5,4},{6,7},{7,6},{8,9},{9,8},{10,11... | collective-permute-start | bytes 589832 | tf_op jit(solution)/shard_map/ppermute | solution.py:711
  438.6 50.6 %collective-permute-start.16 = (bf16[8,96,1536]{2,1,0:T(8,128)(2,1)}, bf16[8,96,1536]{2,1,0:T(8,128)(2,1)}, u32[]{:S(2)}, u32[]{:S(2)}) collective-permute-start(bf16[8,96,1536]{2,1,0:T(8,128)(2,1)} %dynamic-slice_bitcast_fusion.7), channel_id=1, source_target_pairs={{0,2},{2,0},{4,6},{6,4},{8,10},{10,8},{12,14},{14,12},{16,18},{18,... | collective-permute-start | bytes 7077896 | tf_op jit(solution)/shard_map/ppermute | solution.py:719
  487.7 29.2 %collective-permute-start.20 = (bf16[8,96,768]{2,1,0:T(8,128)(2,1)}, bf16[8,96,768]{2,1,0:T(8,128)(2,1)}, u32[]{:S(2)}, u32[]{:S(2)}) collective-permute-start(bf16[8,96,768]{2,1,0:T(8,128)(2,1)} %slice.204), channel_id=1, source_target_pairs={{0,1},{1,0},{2,3},{3,2},{4,5},{5,4},{6,7},{7,6},{8,9},{9,8},{10,11... | collective-permute-start | bytes 3538952 | tf_op jit(solution)/shard_map/ppermute | solution.py:711
  492.7 48.5 %collective-permute-start.17 = (bf16[8,96,768]{2,1,0:T(8,128)(2,1)}, bf16[8,96,768]{2,1,0:T(8,128)(2,1)}, u32[]{:S(2)}, u32[]{:S(2)}) collective-permute-start(bf16[8,96,768]{2,1,0:T(8,128)(2,1)} %slice.202), channel_id=1, source_target_pairs={{0,1},{1,0},{2,3},{3,2},{4,5},{5,4},{6,7},{7,6},{8,9},{9,8},{10,11... | collective-permute-start | bytes 3538952 | tf_op jit(solution)/shard_map/ppermute | solution.py:711
  498.4 45.8 %collective-permute-start.23 = (bf16[4,96,1536]{2,1,0:T(8,128)(2,1)}, bf16[4,96,1536]{2,1,0:T(8,128)(2,1)}, u32[]{:S(2)}, u32[]{:S(2)}) collective-permute-start(bf16[4,96,1536]{2,1,0:T(8,128)(2,1)} %dynamic-slice_bitcast_fusion.9), channel_id=1, source_target_pairs={{0,4},{2,6},{4,0},{6,2},{8,12},{10,14},{12,8},{14,10},{16,20},{18,... | collective-permute-start | bytes 3538952 | tf_op jit(solution)/shard_map/ppermute | solution.py:719
  512.2 120.4 %collective-permute-start.26 = (bf16[8,96,3072]{2,1,0:T(8,128)(2,1)}, bf16[8,96,3072]{2,1,0:T(8,128)(2,1)}, u32[]{:S(2)}, u32[]{:S(2)}) collective-permute-start(bf16[8,96,3072]{2,1,0:T(8,128)(2,1)} %dynamic-slice_bitcast_fusion), channel_id=1, source_target_pairs={{0,2},{2,0},{4,6},{6,4},{8,10},{10,8},{12,14},{14,12},{16,18},{18,... | collective-permute-start | bytes 14155784 | tf_op jit(solution)/shard_map/ppermute | solution.py:719
  513.2 280.0 %reduce-scatter.10.cloned.1.call-start = ((), (), s32[]{:S(2)}) async-start(), calls=%async_computation.10 | async-start | bytes 2949120 | tf_op jit(solution)/shard_map/reduce_scatter | solution.py:733
  518.5 31.7 %collective-permute-start.21 = (bf16[4,96,768]{2,1,0:T(8,128)(2,1)S(1)}, bf16[4,96,768]{2,1,0:T(8,128)(2,1)S(1)}, u32[]{:S(2)}, u32[]{:S(2)}) collective-permute-start(bf16[4,96,768]{2,1,0:T(8,128)(2,1)S(1)} %dynamic-slice_bitcast_fusion.11), channel_id=1, source_target_pairs={{0,4},{2,6},{4,0},{6,2},{8,12},{10,14},{12,8},{14,10},{16,20},{18,... | collective-permute-start | bytes 1769480 | tf_op jit(solution)/shard_map/ppermute | solution.py:719
  563.2 233.9 %reduce-scatter.12.cloned.1.call-start = ((), (), s32[]{:S(2)}) async-start(), calls=%async_computation.11 | async-start | bytes 2949120 | tf_op jit(solution)/shard_map/reduce_scatter | solution.py:733
  570.8 53.5 %collective-permute-start.25 = (bf16[4,96,3072]{2,1,0:T(8,128)(2,1)}, bf16[4,96,3072]{2,1,0:T(8,128)(2,1)}, u32[]{:S(2)}, u32[]{:S(2)}) collective-permute-start(bf16[4,96,3072]{2,1,0:T(8,128)(2,1)} %dynamic-slice_bitcast_fusion.4), channel_id=1, source_target_pairs={{0,4},{2,6},{4,0},{6,2},{8,12},{10,14},{12,8},{14,10},{16,20},{18,... | collective-permute-start | bytes 7077896 | tf_op jit(solution)/shard_map/ppermute | solution.py:719
  628.2 171.0 %reduce-scatter.14.cloned.1.call-start = ((), (), s32[]{:S(2)}) async-start(), calls=%async_computation.12 | async-start | bytes 2949120 | tf_op jit(solution)/shard_map/reduce_scatter | solution.py:733
  632.7 67.9 %collective-permute-start.12 = (bf16[8,96,2304]{2,1,0:T(8,128)(2,1)}, bf16[8,96,2304]{2,1,0:T(8,128)(2,1)}, u32[]{:S(2)}, u32[]{:S(2)}) collective-permute-start(bf16[8,96,2304]{2,1,0:T(8,128)(2,1)} %dynamic-slice_bitcast_fusion.2), channel_id=1, source_target_pairs={{0,2},{2,0},{4,6},{6,4},{8,10},{10,8},{12,14},{14,12},{16,18},{18,... | collective-permute-start | bytes 10616840 | tf_op jit(solution)/shard_map/ppermute | solution.py:719
  642.5 54.0 %collective-permute-start.27 = (bf16[4,96,3072]{2,1,0:T(8,128)(2,1)}, bf16[4,96,3072]{2,1,0:T(8,128)(2,1)}, u32[]{:S(2)}, u32[]{:S(2)}) collective-permute-start(bf16[4,96,3072]{2,1,0:T(8,128)(2,1)} %dynamic-slice_bitcast_fusion.3), channel_id=1, source_target_pairs={{0,4},{2,6},{4,0},{6,2},{8,12},{10,14},{12,8},{14,10},{16,20},{18,... | collective-permute-start | bytes 7077896 | tf_op jit(solution)/shard_map/ppermute | solution.py:719
  654.1 72.3 %collective-permute-start.9 = (bf16[512,1536]{1,0:T(8,128)(2,1)}, bf16[512,1536]{1,0:T(8,128)(2,1)}, u32[]{:S(2)}, u32[]{:S(2)}) collective-permute-start(bf16[512,1536]{1,0:T(8,128)(2,1)} %fusion.84), channel_id=1, source_target_pairs={{0,1},{1,0},{2,3},{3,2},{4,5},{5,4},{6,7},{7,6},{8,9},{9,8},{10,11... | collective-permute-start | bytes 4718600 | tf_op jit(solution)/shard_map/ppermute | solution.py:711
  700.5 100.9 %reduce-scatter.6.cloned.1.call-start = ((), (), s32[]{:S(2)}) async-start(), calls=%async_computation.8 | async-start | bytes 2211840 | tf_op jit(solution)/shard_map/reduce_scatter | solution.py:733
  707.7 40.4 %collective-permute-start.13 = (bf16[4,96,2304]{2,1,0:T(8,128)(2,1)}, bf16[4,96,2304]{2,1,0:T(8,128)(2,1)S(1)}, u32[]{:S(2)}, u32[]{:S(2)}) collective-permute-start(bf16[4,96,2304]{2,1,0:T(8,128)(2,1)} %dynamic-slice_bitcast_fusion.8), channel_id=1, source_target_pairs={{0,4},{2,6},{4,0},{6,2},{8,12},{10,14},{12,8},{14,10},{16,20},{18,... | collective-permute-start | bytes 5308424 | tf_op jit(solution)/shard_map/ppermute | solution.py:719
  720.2 37.6 %collective-permute-start.6 = (bf16[512,1536]{1,0:T(8,128)(2,1)}, bf16[512,1536]{1,0:T(8,128)(2,1)}, u32[]{:S(2)}, u32[]{:S(2)}) collective-permute-start(bf16[512,1536]{1,0:T(8,128)(2,1)} %fusion.87), channel_id=1, source_target_pairs={{0,1},{1,0},{2,3},{3,2},{4,5},{5,4},{6,7},{7,6},{8,9},{9,8},{10,11... | collective-permute-start | bytes 4718600 | tf_op jit(solution)/shard_map/ppermute | solution.py:711
  725.8 44.8 %collective-permute-start.11 = (bf16[64,768]{1,0:T(8,128)(2,1)}, bf16[64,768]{1,0:T(8,128)(2,1)}, u32[]{:S(2)}, u32[]{:S(2)}) collective-permute-start(bf16[64,768]{1,0:T(8,128)(2,1)} %constant_dynamic-slice_fusion), channel_id=1, source_target_pairs={{0,1},{1,0},{2,3},{3,2},{4,5},{5,4},{6,7},{7,6},{8,9},{9,8},{10,11... | collective-permute-start | bytes 294920 | tf_op jit(solution)/shard_map/ppermute | solution.py:711
  735.9 33.8 %collective-permute-start.28 = (f32[6,1536]{1,0:T(8,128)}, f32[6,1536]{1,0:T(8,128)}, u32[]{:S(2)}, u32[]{:S(2)}) collective-permute-start(f32[6,1536]{1,0:T(8,128)} %stack.27), channel_id=1, source_target_pairs={{0,1},{1,0},{2,3},{3,2},{4,5},{5,4},{6,7},{7,6},{8,9},{9,8},{10,11... | collective-permute-start | bytes 110600 | tf_op jit(solution)/shard_map/ppermute | solution.py:711
  (87 other events, 2148.7 us)
Sparse Core Ops, SparseCore 0:
  14.0 112.8 all-gather.3
  129.2 79.0 all-gather.5
  210.5 97.3 all-gather.7
  513.4 22.2 reduce-scatter.7
  563.3 47.6 reduce-scatter.9
  628.4 47.8 reduce-scatter.11
  700.6 47.8 reduce-scatter.13
  751.4 40.7 reduce-scatter.5

commit v2 on v1

--- a/solution.py
+++ b/solution.py
@@ -304,10 +304,210 @@
 QB = 256
 PAIR = 128
 QUAD = 256
+CUTS = 2
+
+
+def after(value, *ready):
+    return lax.optimization_barrier((value,) + ready)[0]
 
 
 def mm(left, right, dims):
     return lax.dot_general(left, right, dims, preferred_element_type=F32)
+
+
+LIGHT = pl.CostEstimate(flops=1024, transcendentals=0, bytes_accessed=1024)
+MIDDLE = pl.CostEstimate(flops=20_000_000_000, transcendentals=0, bytes_accessed=1024)
+HEAVY = pl.CostEstimate(flops=10**15, transcendentals=0, bytes_accessed=1024)
+
+
+def weight_kernel(side_ref, left_ref, right_ref, send_ref, keep_ref, *, shard):
+    total = mm(left_ref[...], right_ref[...], TN).astype(BF)
+    side = side_ref[0]
+    for parity in range(2):
+        even, odd = (keep_ref, send_ref) if parity == 0 else (send_ref, keep_ref)
+
+        @pl.when(side == parity)
+        def _():
+            for at in range(total.shape[0] // shard):
+                rows = total[at * shard : (at + 1) * shard, :]
+                (odd if at % 2 else even)[at // 2] = rows
+
+
+def weight_halves(side, left, right, shard, first=0, size=None):
+    depth, width = left.shape
+    size = size or right.shape[1]
+    tile = next(t for t in (768, 1152, 512, 384, 256, 128) if size % t == 0 and first % t == 0)
+    count = width // shard // 2
+    shape = jax.ShapeDtypeStruct((count, shard, size), BF)
+    out = pl.BlockSpec((count, shard, tile), lambda j, s: (0, 0, j))
+    return pl.pallas_call(
+        partial(weight_kernel, shard=shard),
+        out_shape=(shape, shape),
+        grid_spec=pltpu.PrefetchScalarGridSpec(
+            num_scalar_prefetch=1,
+            grid=(size // tile,),
+            in_specs=[
+                pl.BlockSpec((depth, width), lambda j, s: (0, 0)),
+                pl.BlockSpec((depth, tile), lambda j, s: (0, first // tile + j)),
+            ],
+            out_specs=[out, out],
+        ),
+        name="weight_halves",
+        cost_estimate=LIGHT,
+    )(side, left, right)
+
+
+def added(refs, at=slice(None)):
+    total = refs[0][at].astype(F32)
+    for ref in refs[1:]:
+        total = total + ref[at].astype(F32)
+    return total.astype(BF)
+
+
+def fold_kernel(side_ref, *refs):
+    side = side_ref[0]
+    refs[-2][...] = added(refs[:-2], pl.ds(1 - side, 1))
+    refs[-1][...] = added(refs[:-2], pl.ds(side, 1))
+
+
+def fold(side, *terms):
+    count, shard, size = terms[0].shape[0] // 2, terms[0].shape[1], terms[0].shape[2]
+    shape = jax.ShapeDtypeStruct((count, shard, size), BF)
+    whole = pl.BlockSpec((2, shard, size), lambda j, s: (j, 0, 0))
+    part = pl.BlockSpec((1, shard, size), lambda j, s: (j, 0, 0))
+    return pl.pallas_call(
+        fold_kernel,
+        out_shape=(shape, shape),
+        grid_spec=pltpu.PrefetchScalarGridSpec(
+            num_scalar_prefetch=1,
+            grid=(count,),
+            in_specs=[whole] * len(terms),
+            out_specs=[part, part],
+        ),
+        name="fold",
+        cost_estimate=LIGHT,
+    )(side, *terms)
+
+
+def totals_kernel(*refs, counts):
+    out_ref = refs[-1]
+    first, at = 0, 0
+    for count in counts:
+        size = refs[at].shape[2]
+        out_ref[:, :, first : first + size] = added(refs[at : at + count])
+        first, at = first + size, at + count
+
+
+def totals(groups):
+    count, shard = groups[0][0].shape[:2]
+    sizes = [terms[0].shape[2] for terms in groups]
+    spec = lambda size: pl.BlockSpec((2, shard, size), lambda j: (j, 0, 0))
+    return pl.pallas_call(
+        partial(totals_kernel, counts=[len(terms) for terms in groups]),
+        grid=(count // 2,),
+        out_shape=jax.ShapeDtypeStruct((count, shard, sum(sizes)), BF),
+        in_specs=[spec(size) for size, terms in zip(sizes, groups) for _ in terms],
+        out_specs=spec(sum(sizes)),
+        name="totals",
+        cost_estimate=LIGHT,
+    )(*[v for terms in groups for v in terms])
+
+
+def norm_sums_kernel(value_ref, *refs):
+    sums_ref = refs[-1]
+    incoming = refs[0][...]
+    for ref in refs[1:-1]:
+        incoming = incoming + ref[...]
+    centred, scale = stats_of(value_ref[...].astype(F32))
+
+    @pl.when(pl.program_id(0) == 0)
+    def _():
+        sums_ref[...] = jnp.zeros_like(sums_ref)
+
+    sums_ref[0:1, :] += jnp.sum(incoming * (centred * scale), axis=0, keepdims=True)
+    sums_ref[1:2, :] += jnp.sum(incoming, axis=0, keepdims=True)
+
+
+def norm_sums(value, incoming):
+    rows, width = value.shape
+    tile = 128
+    spec = pl.BlockSpec((tile, width), lambda j: (j, 0))
+    return pl.pallas_call(
+        norm_sums_kernel,
+        grid=(rows // tile,),
+        out_shape=jax.ShapeDtypeStruct((8, width), F32),
+        in_specs=[spec] * (1 + len(incoming)),
+        out_specs=pl.BlockSpec((8, width), lambda j: (0, 0)),
+        name="norm_sums",
+        cost_estimate=LIGHT,
+    )(value, *incoming)
+
+
+def norm_back_kernel(value_ref, gain_ref, base_ref, *refs, parts):
+    grad_ref, low_ref, sums_ref = refs[parts:]
+    incoming = refs[0][...].astype(F32)
+    for ref in refs[1:parts]:
+        incoming = incoming + ref[...].astype(F32)
+    centred, scale = stats_of(value_ref[...].astype(F32))
+    hat = centred * scale
+    scaled = incoming * gain_ref[...]
+    mean = jnp.mean(scaled, axis=-1, keepdims=True)
+    along = jnp.mean(scaled * hat, axis=-1, keepdims=True)
+    grad = base_ref[...].astype(F32) + scale * (scaled - mean - hat * along)
+    grad_ref[...] = grad
+    low_ref[...] = grad.astype(BF)
+
+    @pl.when(pl.program_id(0) == 0)
+    def _():
+        sums_ref[...] = jnp.zeros_like(sums_ref)
+
+    sums_ref[0:1, :] += jnp.sum(incoming * hat, axis=0, keepdims=True)
+    sums_ref[1:2, :] += jnp.sum(incoming, axis=0, keepdims=True)
+
+
+def norm_back_rows(value, gain, base, incoming, cost=LIGHT):
+    rows, width = value.shape
+    tile = 128
+    spec = pl.BlockSpec((tile, width), lambda j: (j, 0))
+    return pl.pallas_call(
+        partial(norm_back_kernel, parts=len(incoming)),
+        grid=(rows // tile,),
+        out_shape=(
+            jax.ShapeDtypeStruct((rows, width), F32),
+            jax.ShapeDtypeStruct((rows, width), BF),
+            jax.ShapeDtypeStruct((8, width), F32),
+        ),
+        in_specs=[spec, pl.BlockSpec((1, width), lambda j: (0, 0)), spec] + [spec] * len(incoming),
+        out_specs=[spec, spec, pl.BlockSpec((8, width), lambda j: (0, 0))],
+        name="norm_back",
+        cost_estimate=cost,
+    )(value, gain.reshape(1, width), base, *incoming)
+
+
+def product_kernel(left_ref, right_ref, out_ref, *, dims):
+    out_ref[...] = mm(left_ref[...], right_ref[...], dims).astype(out_ref.dtype)
+
+
+def product(left, right, dims, dtype, row=0, rows=None, first=0, size=None, cost=LIGHT):
+    rows = rows or left.shape[0]
+    depth = left.shape[1]
+    if dims is NN:
+        size = size or right.shape[1]
+        tile = next(t for t in (768, 512, 384, 256) if size % t == 0 and first % t == 0)
+        right_spec = pl.BlockSpec((depth, tile), lambda j: (0, first // tile + j))
+    else:
+        size = right.shape[0]
+        tile = 512
+        right_spec = pl.BlockSpec((tile, depth), lambda j: (j, first // depth))
+    return pl.pallas_call(
+        partial(product_kernel, dims=dims),
+        grid=(size // tile,),
+        out_shape=jax.ShapeDtypeStruct((rows, size), dtype),
+        in_specs=[pl.BlockSpec((rows, depth), lambda j: (row, 0)), right_spec],
+        out_specs=pl.BlockSpec((rows, tile), lambda j: (0, j)),
+        name="product",
+        cost_estimate=cost,
+    )(left, right)
 
 
 def lanes_of(width, head):
@@ -380,7 +580,10 @@
 def self_forward(t, qkv):
     length, width = qkv.shape
     pairs = width // (3 * PAIR)
-    spec = lambda part: pl.BlockSpec((length, PAIR), lambda j, s: (0, part * pairs + j))
+    cut = pairs // CUTS
+    spec = lambda part: pl.BlockSpec(
+        (length, PAIR), lambda j, r: (0, (3 * (j // cut) + part) * cut + j % cut)
+    )
     return pl.pallas_call(
         self_kernel,
         out_shape=(
@@ -398,11 +601,7 @@
             scratch_shapes=[pltpu.VMEM((length, PAIR), BF)] * 3,
         ),
         name="self_attend",
-        cost_estimate=pl.CostEstimate(
-            flops=16 * length * length * PAIR * pairs // 3,
-            transcendentals=length * length * pairs,
-            bytes_accessed=8 * length * PAIR * pairs,
-        ),
+        cost_estimate=LIGHT,
     )(t, qkv, qkv, qkv)
 
 
@@ -469,10 +668,13 @@
         out_ref[...] = dvb[...]
 
 
-def self_backward(t, qkv, mixed, d_mixed, lse):
-    length, width = qkv.shape
+def self_backward(t, qkv, mixed, d_mixed, lse, part):
+    length, width = qkv.shape[0], qkv.shape[1] // CUTS
     pairs = width // (3 * PAIR)
-    spec = lambda part: pl.BlockSpec((length, PAIR), lambda j, s, r: (0, part * pairs + j))
+    first = part * pairs
+    spec = lambda kind: pl.BlockSpec(
+        (length, PAIR), lambda j, s, r: (0, 3 * first + kind * pairs + j)
+    )
     return pl.pallas_call(
         self_back_kernel,
         out_shape=jax.ShapeDtypeStruct((length, width), BF),
@@ -483,9 +685,9 @@
                 spec(0),
                 spec(1),
                 spec(2),
-                pl.BlockSpec((length, PAIR), lambda j, s, r: (0, j)),
-                pl.BlockSpec((length, PAIR), lambda j, s, r: (0, j)),
-                pl.BlockSpec((1, 8, length), lambda j, s, r: (j, 0, 0)),
+                pl.BlockSpec((length, PAIR), lambda j, s, r: (0, first + j)),
+                pl.BlockSpec((length, PAIR), lambda j, s, r: (0, first + j)),
+                pl.BlockSpec((1, 8, length), lambda j, s, r: (first + j, 0, 0)),
             ],
             out_specs=pl.BlockSpec((length, PAIR), lambda j, s, r: (0, s * pairs + j)),
             scratch_shapes=[pltpu.VMEM((length, PAIR), BF)] * 5
@@ -493,11 +695,7 @@
             + [pltpu.VMEM((length, PAIR), BF)] * 2,
         ),
         name="self_attend_back",
-        cost_estimate=pl.CostEstimate(
-            flops=40 * length * length * PAIR * pairs // 3,
-            transcendentals=length * length * pairs,
-            bytes_accessed=16 * length * PAIR * pairs,
-        ),
+        cost_estimate=MIDDLE,
     )(t, qkv, qkv, qkv, mixed, d_mixed, lse)
 
 
@@ -550,9 +748,7 @@
             pl.BlockSpec((1, 8, rows), lambda j: (j, 0, 0)),
         ],
         name="cross_attend",
-        cost_estimate=pl.CostEstimate(
-            flops=4 * rows * QUAD * width, transcendentals=rows * width, bytes_accessed=4 * rows * width
-        ),
+        cost_estimate=LIGHT,
     )(query, key, value)
 
 
@@ -605,9 +801,7 @@
             pl.BlockSpec((keys, QUAD), lambda j: (0, j)),
         ],
         name="cross_attend_back",
-        cost_estimate=pl.CostEstimate(
-            flops=10 * rows * QUAD * width, transcendentals=rows * width, bytes_accessed=8 * rows * width
-        ),
+        cost_estimate=LIGHT,
     )(query, key, value, mixed, d_mixed, lse)
 
 
@@ -648,11 +842,7 @@
         out_specs=[out_spec, out_spec],
         input_output_aliases={4 + i: i for i in range(len(kept))},
         name="ffn_middle",
-        cost_estimate=pl.CostEstimate(
-            flops=4 * rows * width * hidden,
-            transcendentals=2 * rows * hidden,
-            bytes_accessed=4 * width * hidden + 4 * rows * hidden,
-        ),
+        cost_estimate=LIGHT,
     )(normed, grads, weights, weights, *kept)
 
 
@@ -699,11 +889,12 @@
     half = width // 2
     hidden = inner_weight.shape[1]
     shard = self_query.shape[0]
-    tensor = lax.axis_index("tensor")
-    place = lax.axis_index("dp")
-    core, column = place % 2, (place // 2) % 2
-    core_swap = [(i, i ^ 1) for i in range(groups)]
-    column_swap = [(i, i ^ 2) for i in range(groups)]
+    tensor = lax.axis_index("tensor").astype(jnp.uint32)
+    place = lax.axis_index("dp").astype(jnp.uint32)
+    one = jnp.uint32(1)
+    bits = [(place >> i) & one for i in range((groups - 1).bit_length())]
+    mine, theirs = tensor * jnp.uint32(half), (tensor ^ one) * jnp.uint32(half)
+    zero = jnp.uint32(0)
     lines = [[i + 4 * j for j in range(groups // 4)] for i in range(4)]
     t_ref = tensor.astype(jnp.int32).reshape(1)
 
@@ -713,60 +904,64 @@
     def gather(parts):
         return lax.all_gather(jnp.concatenate(parts, axis=1), "dp", axis=0, tiled=True)
 
-    def halved(value, bit, swap):
-        send = lax.dynamic_index_in_dim(value, 1 - bit, 1, False)
-        keep = lax.dynamic_index_in_dim(value, bit, 1, False)
-        got = lax.ppermute(send, "dp", swap)
-        return (keep.astype(F32) + got.astype(F32)).astype(BF)
-
-    def core_sum(grad):
-        cut = grad.reshape(groups // 2, 2, shard, grad.shape[1])
-        return halved(cut, core, core_swap)
-
-    def column_sum(grad):
-        cut = grad.reshape(groups // 4, 2, shard, grad.shape[-1])
-        return halved(cut, column, column_swap)
-
-    def line_sum(parts):
-        whole = jnp.concatenate(parts, axis=-1) if len(parts) > 1 else parts[0]
+    swaps = [[(i, i ^ (1 << level)) for i in range(groups)] for level in range(len(bits))]
+
+    def swap(send, level):
+        return lax.ppermute(send, "dp", swaps[level])
+
+    def line_sum(whole):
         whole = whole.reshape(-1, whole.shape[-1])
         return lax.psum_scatter(
             whole, "dp", scatter_dimension=0, tiled=True, axis_index_groups=lines
-        ).astype(F32)
-
-    def pair_sum(grad):
-        got = peer(grad[..., half:])
-        return (grad[..., :half].astype(F32) + got.astype(F32)).astype(BF)
-
-    inputs_peer = peer(inputs)
+        )
+
+    def line_step(send, keep, ready):
+        return fold(side_refs[3], after(keep, ready), swap(send, 2))
+
+    def line_end(send, keep):
+        for level in range(3, len(bits)):
+            got = swap(send, level)
+            if level + 1 < len(bits):
+                send, keep = fold(side_refs[level + 1], keep, got)
+        return (keep.astype(F32) + got.astype(F32)).reshape(shard, -1)
+
+    part = half // CUTS
+    pieces = [slice(i * part, (i + 1) * part) for i in range(CUTS)]
+    side_refs = [bit.astype(jnp.int32).reshape(1) for bit in bits]
+    start_x, side_refs, mine, theirs, t_ref = lax.optimization_barrier(
+        (inputs, side_refs, mine, theirs, t_ref)
+    )
     cross_two = jnp.concatenate([cross_query, cross_output.T], axis=1)
     cross_peer = peer(cross_two)
-    grads_peer = peer(cotangent)
-
-    first = gather([self_query, self_key, self_value, self_output.T, cross_key, cross_value])
-    second = gather(
-        [cross_query, cross_peer[:, :half], cross_two[:, half:], cross_peer[:, half:]]
-    )
-    third = gather([inner_weight, outer_weight.T])
+    first = gather(
+        [v[:, p] for p in pieces for v in (self_query, self_key, self_value)]
+        + [self_output.T, cross_key, cross_value]
+        + [cross_query, cross_peer[:, :half], cross_two[:, half:], cross_peer[:, half:]]
+    )
+    second = gather([inner_weight, outer_weight.T])
+    inputs_peer = peer(after(start_x, cross_peer))
+    grads_peer = peer(after(cotangent, inputs_peer))
     w_qkv = first[:, : 3 * half]
     w_self_out = first[:, 3 * half : 4 * half]
-    w_text = first[:, 4 * half :]
-    w_cross_query = second[:, :width]
-    w_cross_out = second[:, width:]
-    w_inner = third[:, :hidden]
-    w_outer = third[:, hidden:]
+    w_text = first[:, 4 * half : 6 * half]
+    w_cross_query = first[:, 6 * half : 8 * half]
+    w_cross_out = first[:, 8 * half :]
+    w_inner = second[:, :hidden]
+    w_outer = second[:, hidden:]
 
     start = jnp.concatenate([inputs, inputs_peer], axis=0).astype(F32)
     normed1 = norm_rows(start, norm_gains[0], norm_shifts[0]).astype(BF)
-    qkv = mm(normed1, w_qkv, NN).astype(BF)
     text = text_states.reshape(-1, width)
     text_own = mm(text, w_text, NN).astype(BF)
+    grads3 = jnp.concatenate([cotangent, grads_peer], axis=0)
+    normed1 = after(normed1, grads3, text_own)
+    qkv = mm(normed1, w_qkv, NN).astype(BF)
     text_peer = peer(text_own)
-    key2 = jnp.concatenate([text_own[:, :half], text_peer[:, :half]], axis=1)
-    value2 = jnp.concatenate([text_own[:, half:], text_peer[:, half:]], axis=1)
     mixed1, lse1 = self_forward(t_ref, qkv)
     away = peer(mm(mixed1[rows:], w_self_out, NT).astype(BF))
     home = mm(mixed1[:rows], w_self_out, NT)
+    key2 = jnp.concatenate([text_own[:, :half], text_peer[:, :half]], axis=1)
+    value2 = jnp.concatenate([text_own[:, half:], text_peer[:, half:]], axis=1)
     state1 = inputs.astype(F32) + home + away.astype(F32)
 
     normed2 = norm_rows(state1, norm_gains[1], norm_shifts[1]).astype(BF)
@@ -776,73 +971,159 @@
 
     normed3 = norm_rows(state2, norm_gains[2], norm_shifts[2]).astype(BF)
     normed3_peer = peer(normed3)
-    active, d_inner = ffn_middle(normed3, cotangent, third, 0, 2)
-    active, d_inner = ffn_middle(normed3_peer, grads_peer, third, 1, 2, (active, d_inner))
-    back3_away = peer(mm(d_inner[rows:], w_inner, NT).astype(BF))
-    grads3 = jnp.concatenate([cotangent, grads_peer], axis=0)
-    d_outer = column_sum(core_sum(mm(grads3, active, TN).astype(BF)))
-    outer_sum = line_sum([d_outer])
-    rows3 = jnp.concatenate([normed3, normed3_peer], axis=0)
-    d_innerw = column_sum(core_sum(mm(rows3, d_inner, TN).astype(BF)))
-    inner_sum = line_sum([d_innerw])
-    out_away = peer(mm(active[rows:], w_outer, NT).astype(BF))
-    output = (state2 + mm(active[:rows], w_outer, NT) + out_away.astype(F32)).astype(BF)
-
-    back3 = mm(d_inner[:rows], w_inner, NT) + back3_away.astype(F32)
-    d_state2, gain3, shift3 = norm_grad(state2, norm_gains[2], back3)
-    grad2 = cotangent.astype(F32) + d_state2
-    g2 = grad2.astype(BF)
-    d_mixed2 = mm(g2, w_cross_out, NN).astype(BF)
+    active, d_inner = ffn_middle(normed3, cotangent, second, 0, 2)
+    back3_home = product(d_inner, second, NT, F32, row=0, rows=rows)
+    out_home = product(active, second, NT, F32, row=0, rows=rows, first=hidden)
+    normed3_peer = after(normed3_peer, back3_home, out_home)
+    active, d_inner = ffn_middle(normed3_peer, grads_peer, second, 1, 2, (active, d_inner))
+    back3_part = product(d_inner, second, NT, BF, row=1, rows=rows)
+    back3_away = peer(back3_part)
+    d_outer = mm(after(grads3, back3_part), active, TN).astype(BF)
+    outer_sum = lax.psum_scatter(d_outer, "dp", scatter_dimension=0, tiled=True)
+    rows3 = jnp.concatenate([normed3, after(normed3_peer, d_outer)], axis=0)
+    last = rows3
+
+    def weight_core(left, right, first=0, size=None):
+        nonlocal last
+        send, keep = weight_halves(side_refs[0], after(left, last), right, shard, first, size)
+        last = send
+        return send, keep
+
+    inner = weight_core(rows3, d_inner)
+    inner_got = swap(inner[0], 0)
+
+    back3_away = after(back3_away, last)
+    grad2, g2, sums3 = norm_back_rows(
+        state2, norm_gains[2], cotangent, [back3_home, back3_away], HEAVY
+    )
+    d_mixed2 = product(g2, first, NN, BF, first=8 * half, size=width)
+    inner = fold(side_refs[1], after(inner[1], d_mixed2), inner_got)
+    inner_got = swap(inner[0], 1)
+    d_mixed2 = after(d_mixed2, inner[0])
     d_query2, d_key2, d_value2 = cross_backward(query2, key2, value2, mixed2, d_mixed2, lse2)
-    back2 = mm(d_query2, w_cross_query, NT)
-    d_state1, gain2, shift2 = norm_grad(state1, norm_gains[1], back2)
-    grad1 = grad2 + d_state1
-    g1 = grad1.astype(BF)
+    d_text_send = jnp.concatenate([d_key2[:, half:], d_value2[:, half:]], axis=1).astype(BF)
+    d_text_keep = jnp.concatenate([d_key2[:, :half], d_value2[:, :half]], axis=1)
+    d_text_peer = peer(d_text_send)
+    back2 = product(after(d_query2, d_text_send), first, NT, F32, first=6 * half)
+    grad1, g1, sums2 = norm_back_rows(state1, norm_gains[1], grad2, [back2])
     g1_peer = peer(g1)
 
-    d_text_send = jnp.concatenate([d_key2[:, half:], d_value2[:, half:]], axis=1)
-    d_text_keep = jnp.concatenate([d_key2[:, :half], d_value2[:, :half]], axis=1)
-    d_text = (d_text_keep + peer(d_text_send.astype(BF)).astype(F32)).astype(BF)
-    d_coutput = pair_sum(core_sum(mm(g2, mixed2, TN).astype(BF)))
-    d_cquery = pair_sum(core_sum(mm(normed2, d_query2, TN).astype(BF)))
-    d_ckv = core_sum(mm(text, d_text, TN).astype(BF))
-    cross_sum = line_sum([column_sum(v) for v in (d_coutput, d_cquery, d_ckv)])
-    text_terms = mm(d_text, w_text, NT).astype(BF)
-    text_keep = lax.dynamic_slice_in_dim(text_terms, tensor * half, half, 1)
-    text_send = lax.dynamic_slice_in_dim(text_terms, (1 - tensor) * half, half, 1)
-    text_grad = (text_keep.astype(F32) + peer(text_send).astype(F32)).reshape(1, -1, half)
-
-    grads1 = jnp.concatenate([g1, g1_peer], axis=0)
-    d_mixed1 = mm(grads1, w_self_out, NN).astype(BF)
-    d_soutput = column_sum(core_sum(mm(grads1, mixed1, TN).astype(BF)))
-    so_sum = line_sum([d_soutput])
-    d_qkv = self_backward(t_ref, qkv, mixed1, d_mixed1, lse1)
-    qkv_sum = line_sum([column_sum(core_sum(mm(normed1, d_qkv, TN).astype(BF)))])
-    back1_away = peer(mm(d_qkv[rows:], w_qkv, NT).astype(BF))
-    back1 = mm(d_qkv[:rows], w_qkv, NT) + back1_away.astype(F32)
-    d_start, gain1, shift1 = norm_grad(inputs.astype(F32), norm_gains[0], back1)
-    input_grad = grad1 + d_start
-
-    small = jnp.stack([gain1, gain2, gain3, shift1, shift2, shift3])
+    out_part = product(after(active, g1), second, NT, BF, row=1, rows=rows, first=hidden)
+    last = out_part
+
+    def two(left, right):
+        found = [weight_core(left, right, i * half, half) for i in range(2)]
+        return [(keep, swap(send, 0)) for send, keep in found]
+
+    co_own, co_away = two(g2, mixed2)
+    cq_own, cq_away = two(normed2, d_query2)
+    d_text = (d_text_keep + after(d_text_peer, last).astype(F32)).astype(BF)
+    kv = two(text, d_text)
+    text_terms = mm(after(d_text, last), w_text, NT).astype(BF)
+    text_keep, text_send = (
+        lax.dynamic_slice(
+            text_terms, (zero, at), (text_terms.shape[0], half), allow_negative_indices=False
+        )
+        for at in (mine, theirs)
+    )
+
+    grads1 = jnp.concatenate([g1, after(g1_peer, text_send, last)], axis=0)
+    d_mixed1 = product(grads1, first, NN, BF, first=3 * half, size=half)
+    co_send = totals([(after(co_away[0], d_mixed1), co_away[1])])
+    co_got = peer(co_send)
+    cq_send = totals([(after(cq_away[0], co_send), cq_away[1])])
+    cq_got = peer(cq_send)
+    kv = [fold(side_refs[1], after(keep, cq_send), got) for keep, got in kv]
+    kv = [(keep, swap(send, 1)) for send, keep in kv]
+    inner = fold(side_refs[2], after(inner[1], cq_send), inner_got)
+    found0 = self_backward(
+        t_ref, qkv, mixed1, after(d_mixed1, kv[0][0], kv[1][0], inner[0], outer_sum), lse1, 0
+    )
+    text_got = peer(after(text_send, found0))
+    out_away = peer(after(out_part, found0))
+    last = found0
+    qkv0 = weight_core(normed1, found0)
+    qkv0_got = swap(qkv0[0], 0)
+    so = weight_core(grads1, mixed1)
+    so_got = swap(so[0], 0)
+    kv_whole = totals([(after(kv[0][0], last), kv[0][1]), kv[1]])
+    co = fold(side_refs[1], after(co_own[0], kv_whole), co_own[1], co_got)
+    co_got = swap(co[0], 1)
+    cq = fold(side_refs[1], after(cq_own[0], co[0]), cq_own[1], cq_got)
+    cq_got = swap(cq[0], 1)
+    inner = line_step(*inner, cq[0])
+    away0 = product(after(found0, inner[0]), first, NT, F32, row=1, rows=rows, cost=HEAVY)
+    qkv0 = fold(side_refs[1], after(qkv0[1], away0), qkv0_got)
+    qkv0_got = swap(qkv0[0], 1)
+    so = fold(side_refs[1], after(so[1], qkv0[0]), so_got)
+    so_got = swap(so[0], 1)
+    found1 = self_backward(t_ref, qkv, mixed1, after(d_mixed1, so[0]), lse1, 1)
+    last = found1
+    qkv1 = weight_core(normed1, found1)
+    qkv1_got = swap(qkv1[0], 0)
+    whole = totals([(after(co[1], qkv1[0]), co_got), (kv_whole,)])
+    sum_a = line_sum(whole)
+    qkv0 = fold(side_refs[2], after(qkv0[1], whole), qkv0_got)
+    away1 = product(
+        after(found1, qkv0[0]),
+        first,
+        NT,
+        F32,
+        row=1,
+        rows=rows,
+        first=3 * part,
+        cost=HEAVY,
+    )
+    back1_part = (away0 + away1).astype(BF)
+    back1_away = peer(back1_part)
+    qkv1 = fold(side_refs[1], after(qkv1[1], back1_part), qkv1_got)
+    qkv1_got = swap(qkv1[0], 1)
+    cq = fold(side_refs[2], after(cq[1], qkv1[0]), cq_got)
+    so = fold(side_refs[2], after(so[1], cq[0]), so_got)
+    home0 = product(after(found0, so[0]), first, NT, F32, row=0, rows=rows)
+    qkv0 = line_step(*qkv0, home0)
+    home1 = product(after(found1, qkv0[0]), first, NT, F32, row=0, rows=rows, first=3 * part)
+    qkv1 = fold(side_refs[2], after(qkv1[1], home1), qkv1_got)
+    sums0 = norm_sums(after(inputs_peer, qkv1[0]), [away0, away1])
+    cq = line_step(*cq, sums0)
+    so = line_step(*so, cq[0])
+    sums1 = sums0 + norm_sums(after(inputs, so[0], sum_a), [home0, home1])
+    qkv1 = line_step(*qkv1, sums1)
+    input_grad, _, _ = norm_back_rows(
+        inputs, norm_gains[0], grad1, [home0, home1, after(back1_away, qkv1[0])]
+    )
+    inner_sum = line_end(inner[0], after(inner[1], home0))
+    qkv0_sum, cq_sum, so_sum, qkv1_sum = (line_end(*v) for v in (qkv0, cq, so, qkv1))
+    output = (state2 + out_home + after(out_away, last).astype(F32)).astype(BF)
+    text_grad = text_keep.astype(F32) + after(text_got, last).astype(F32)
+    text_grad = text_grad.reshape(1, -1, half)
+    qkv_sums = [qkv0_sum, qkv1_sum]
+
+    small = jnp.stack([v[i] for i in range(2) for v in (sums1, sums2, sums3)])
+    small = after(small, back1_away)
     small = small + peer(small)
     bit = 1
     while bit < groups:
         small = small + lax.ppermute(small, "dp", [(i, i ^ bit) for i in range(groups)])
         bit *= 2
+
+    def joined(kind):
+        return jnp.concatenate([v[:, kind * part : (kind + 1) * part] for v in qkv_sums], axis=1)
+
     return (
         output,
         input_grad,
         text_grad,
-        qkv_sum[:, :half],
-        qkv_sum[:, half : 2 * half],
-        qkv_sum[:, 2 * half :],
+        joined(0),
+        joined(1),
+        joined(2),
         so_sum.T,
-        cross_sum[:, half : 2 * half],
-        cross_sum[:, 2 * half : 3 * half],
-        cross_sum[:, 3 * half :],
-        cross_sum[:, :half].T,
-        inner_sum,
-        outer_sum.T,
+        cq_sum,
+        sum_a[:, half : 2 * half].astype(F32),
+        sum_a[:, 2 * half :].astype(F32),
+        sum_a[:, :half].astype(F32).T,
+        inner_sum.astype(F32),
+        outer_sum.astype(F32).T,
         small[:3],
         small[3:],
     )
@@ -853,12 +1134,13 @@
     width = inputs.shape[1]
     return (
         sides == 2
-        and groups >= 4
+        and groups >= 16
         and groups & (groups - 1) == 0
         and text_states.shape[0] == groups
         and text_states.shape[1] == TEXT
         and inputs.shape[0] == groups * LEN
         and width % (2 * QUAD) == 0
+        and width % (2 * CUTS * PAIR) == 0
         and width % (32 * groups) in (0, 16 * groups)
         and inner_weight.shape[1] % (2 * FF_STEP) == 0
     )

time: 819 us -> 752 us (0.918)
  Pallas kernels: 109 us -> 362 us
  waiting for transfers between devices: 362 us -> 192 us
  matrix products: 172 us -> 53.6 us
  other arithmetic: 70.3 us -> 32.2 us
  starting transfers between devices: 33.7 us -> 42.3 us
    pallas_call x0 -> x48, Pallas kernels: none -> 252 us  [the longest x11 82.4 us: product(): pl.pallas_call(partial(product_kernel, dims=dims), grid=(size // tile,),...]
    dot_general x23 -> x8, matrix products: 172 us -> 53.6 us  [mm(): return lax.dot_general(left, right, dims, preferred_element_type=F32)]
    ppermute x15, waiting for transfers between devices: 178 us -> 112 us  [peer(): return lax.ppermute(value, 'tensor', [(0, 1), (1, 0)])]
    all_gather x3 -> x2, waiting for transfers between devices: 97.9 us -> 45.7 us  [gather(): lax.all_gather(jnp.concatenate(parts, axis=1), 'dp', axis=0, tiled=True)]
    ppermute x14 -> x28, waiting for transfers between devices: 74 us -> 32.7 us  [swap(): return lax.ppermute(send, 'dp', swaps[level])]
    convert_element_type x19 -> x5, other arithmetic: 46.3 us -> 10.5 us  [the longest x1 3.69 us: on_pair(): back1_part = (away0 + away1).astype(BF)]
    squeeze x14 -> x0, local copies, waits for them, and re-layouts: 20.6 us -> none  [halved(): send = lax.dynamic_index_in_dim(value, 1 - bit, 1, False)]
    unnamed x161 -> x114, local copies, waits for them, and re-layouts: 14.7 us -> 33.7 us
  transfers between devices with their start and end apart: 41 -> 51, of which waited for: 18 -> 13; matrix products, arithmetic and copies ran while one was open for 32% -> 15% of each run, Pallas kernels for 11% -> 45%
where the time goes in v2:
time: 752 us; the launch traced here: 739 us
  Pallas kernels  362 us (48%)
  waiting for transfers between devices  192 us (26%)
  matrix products  53.6 us (7%)
  local copies, waits for them, and re-layouts  42.8 us (6%)
  starting transfers between devices  42.3 us (6%)
  other arithmetic  32.2 us (4%)
  between operations  14.7 us (2%)
    ppermute x15, waiting for transfers between devices, peer(): return lax.ppermute(value, 'tensor', [(0, 1), (1, 0)])  112 us
    pallas_call x11, Pallas kernels, product(): pl.pallas_call(partial(product_kernel, dims=dims), grid=(size // tile,),...  82.4 us
    pallas_call x10, Pallas kernels, weight_halves(): pl.pallas_call(partial(weight_kernel, shard=shard), out_shape=(shape, sha...  67.4 us
    pallas_call x18, Pallas kernels, fold(): pl.pallas_call(fold_kernel, out_shape=(shape, shape), grid_spec=pltpu.Pre...  55.8 us
    dot_general x8, matrix products, mm(): return lax.dot_general(left, right, dims, preferred_element_type=F32)  53.6 us
    all_gather x2, waiting for transfers between devices, gather(): lax.all_gather(jnp.concatenate(parts, axis=1), 'dp', axis=0, tiled=True)  45.7 us
    pallas_call x2, Pallas kernels, self_backward(): pl.pallas_call(self_back_kernel, out_shape=jax.ShapeDtypeStruct((length,...  40.1 us
    pallas_call x2, Pallas kernels, ffn_middle(): pl.pallas_call(ffn_kernel, grid=(steps,), out_shape=(out_shape, out_shape...  33.8 us
  transfers between devices with their start and end apart: 51, of which 13 were waited for; matrix products, arithmetic and copies ran while one was open for 15% of the time, Pallas kernels for 45%

profile of v2, /device:TPU:0, one launch (start us, length us, event | category | flops | bytes accessed | tf_op | source)
XLA Modules:
  0.0 739.2 jit_solution(292438172070196384)
XLA Ops:
  34.3 33.9 %collective-permute-done.1.value_ref = bf16[512,1536]{1,0:T(8,128)(2,1)S(1)} collective-permute-done((bf16[512,1536]{1,0:T(8,128)(2,1)S(1)}, bf16[512,1536]{1,0:T(8,128)(2,1)S(1)}, u32[]{:S(2)}, u32[]{:S(2)}) %collective-permute-start.1) | collective-permute-done | bytes 1572896 | tf_op jit(solution)/shard_map/ppermute | solution.py:902
  74.9 28.5 %collective-permute-done.2.g_ref = bf16[512,1536]{1,0:T(8,128)(2,1)S(1)} collective-permute-done((bf16[512,1536]{1,0:T(8,128)(2,1)S(1)}, bf16[512,1536]{1,0:T(8,128)(2,1)S(1)}, u32[]{:S(2)}, u32[]{:S(2)}) %collective-permute-start.2) | collective-permute-done | bytes 1572896 | tf_op jit(solution)/shard_map/ppermute | solution.py:902
  105.8 45.7 %all-gather.3.cloned.1.call-done.right_ref = bf16[1536,7680]{1,0:T(8,128)(2,1)} async-done(((bf16[96,7680]{1,0:T(8,128)(2,1)}), bf16[1536,7680]{1,0:T(8,128)(2,1)}) %all-gather.3.cloned.1.call-update) | async-done | bytes 23592976 | tf_op jit(solution)/shard_map/all_gather | solution.py:905
  154.9 12.1 %fusion.8.q_ref.k_ref.v_ref = bf16[1024,2304]{1,0:T(8,128)(2,1)} fusion(bf16[1024,1536]{1,0:T(8,128)(2,1)S(1)} %copy-done.1, bf16[1536,7680]{1,0:T(8,128)(2,1)} %all-gather.3.cloned.1.call-done.right_ref), kind=kOutput, calls=%fused_computation.11 | convolution fusion | flops 7250116608 | bytes 14942208 | tf_op jit(solution)/shard_map/dot_general | solution.py:315
  166.9 21.0 %self_attend.1 = (bf16[1024,768]{1,0:T(8,128)(2,1)}, f32[6,8,1024]{2,1,0:T(8,128)}) custom-call(s32[1]{0:T(128)} %bitcast.4.t_ref, bf16[1024,2304]{1,0:T(8,128)(2,1)} %fusion.8.q_ref.k_ref.v_ref, bf16[1024,2304]{1,0:T(8,128)(2,1)} %fusion.8.q_ref.k_ref.v_ref, bf16[1024,2304]{1,0:T(8,128)(2,1)} %fusion.8.q_ref.k_ref.v_ref), custom_call_target="tpu_custom_call" | custom-call | flops 1024 | bytes 1024 | tf_op jit(solution)/shard_map/self_attend/pallas_call | solution.py:587
  193.7 38.6 %collective-permute-done.4 = bf16[64,1536]{1,0:T(8,128)(2,1)S(1)} collective-permute-done((bf16[64,1536]{1,0:T(8,128)(2,1)S(1)}, bf16[64,1536]{1,0:T(8,128)(2,1)S(1)}, u32[]{:S(2)}, u32[]{:S(2)}) %collective-permute-start.4) | collective-permute-done | bytes 196640 | tf_op jit(solution)/shard_map/ppermute | solution.py:902
  238.8 6.7 fusion.23.q_ref
  245.5 6.8 cross_attend.1
  260.6 17.0 %ffn_middle.2 = (bf16[1024,3072]{1,0:T(8,128)(2,1)}, bf16[1024,3072]{1,0:T(8,128)(2,1)}) custom-call(bf16[512,1536]{1,0:T(8,128)(2,1)} %copy-done.8, bf16[512,1536]{1,0:T(8,128)(2,1)} %base_ref.1, bf16[1536,6144]{1,0:T(8,128)(2,1)} %all-gather.5.cloned.1.call-done.wi_ref.wo_ref.right_ref, bf16[1536,6144]{1,0:T(8,128)(2,1)} %all-gather.5.cloned.1.call-done.wi_ref.wo_ref.right_ref), custom_call_target="tpu_custom_call" | custom-call | flops 1024 | bytes 1024 | tf_op jit(solution)/shard_map/ffn_middle/pallas_call | solution.py:831
  277.6 9.8 %product.11 = f32[512,1536]{1,0:T(8,128)} custom-call(bf16[1024,3072]{1,0:T(8,128)(2,1)} %get-tuple-element.163.left_ref.refs_0_, bf16[1536,6144]{1,0:T(8,128)(2,1)} %all-gather.5.cloned.1.call-done.wi_ref.wo_ref.right_ref), custom_call_target="tpu_custom_call" | custom-call | flops 1024 | bytes 1024 | tf_op jit(solution)/shard_map/product/pallas_call | solution.py:502
  287.3 9.8 %product.12.refs_0_ = f32[512,1536]{1,0:T(8,128)} custom-call(bf16[1024,3072]{1,0:T(8,128)(2,1)} %get-tuple-element.164.left_ref.refs_1_, bf16[1536,6144]{1,0:T(8,128)(2,1)} %all-gather.5.cloned.1.call-done.wi_ref.wo_ref.right_ref), custom_call_target="tpu_custom_call" | custom-call | flops 1024 | bytes 1024 | tf_op jit(solution)/shard_map/product/pallas_call | solution.py:502
  298.3 16.9 %ffn_middle.3 = (bf16[1024,3072]{1,0:T(8,128)(2,1)}, bf16[1024,3072]{1,0:T(8,128)(2,1)}) custom-call(bf16[512,1536]{1,0:T(8,128)(2,1)} %copy-done.15, bf16[512,1536]{1,0:T(8,128)(2,1)} %copy-done.14, bf16[1536,6144]{1,0:T(8,128)(2,1)} %all-gather.5.cloned.1.call-done.wi_ref.wo_ref.right_ref, ...), custom_call_target="tpu_custom_call", output_to_operand_aliasing={{0}: (4, {}), {1}: (5, {})} | custom-call | flops 1024 | bytes 1024 | tf_op jit(solution)/shard_map/ffn_middle/pallas_call | solution.py:831
  315.2 9.4 %product.13 = bf16[512,1536]{1,0:T(8,128)(2,1)} custom-call(bf16[1024,3072]{1,0:T(8,128)(2,1)} %get-tuple-element.167.left_ref.right_ref, bf16[1536,6144]{1,0:T(8,128)(2,1)} %all-gather.5.cloned.1.call-done.wi_ref.wo_ref.right_ref), custom_call_target="tpu_custom_call" | custom-call | flops 1024 | bytes 1024 | tf_op jit(solution)/shard_map/product/pallas_call | solution.py:502
  325.8 15.2 %convolution_convert_fusion = bf16[1536,3072]{1,0:T(8,128)(2,1)} fusion(bf16[1024,1536]{1,0:T(8,128)(2,1)} %constant_dynamic-update-slice_fusion, bf16[1024,3072]{1,0:T(8,128)(2,1)} %get-tuple-element.186.left_ref), kind=kOutput, calls=%fused_computation | convolution fusion | flops 9668395008 | bytes 18874368 | tf_op jit(solution)/shard_map/dot_general | solution.py:315
  344.7 16.1 %weight_halves.10 = (bf16[8,96,3072]{2,1,0:T(8,128)(2,1)}, bf16[8,96,3072]{2,1,0:T(8,128)(2,1)}) custom-call(s32[1]{0:T(128)} %bitcast.side_ref, bf16[1024,1536]{1,0:T(8,128)(2,1)} %pad_maximum_fusion.1.left_ref, bf16[1024,3072]{1,0:T(8,128)(2,1)} %get-tuple-element.167.left_ref.right_ref), custom_call_target="tpu_custom_call" | custom-call | flops 1024 | bytes 1024 | tf_op jit(solution)/shard_map/weight_halves/pallas_call | solution.py:343
  360.8 7.6 %norm_back.3 = (f32[512,1536]{1,0:T(8,128)}, bf16[512,1536]{1,0:T(8,128)(2,1)}, f32[8,1536]{1,0:T(8,128)}) custom-call(f32[512,1536]{1,0:T(8,128)} %copy-done.2, f32[1,1536]{1,0:T(1,128)} %get-tuple-element.325.gain_ref, bf16[512,1536]{1,0:T(8,128)(2,1)} %base_ref.1, f32[512,1536]{1,0:T(8,128)} %product.12.refs_0_, ...), custom_call_target="tpu_custom_call" | custom-call | flops 999999986991104 | bytes 1024 | tf_op jit(solution)/shard_map/norm_back/pallas_call | solution.py:472
  374.3 6.4 fold.18
  380.7 7.3 cross_attend_back.1
  389.9 6.8 product.15.refs_0_
  396.7 7.3 norm_back.4
  407.5 9.6 %product.16 = bf16[512,1536]{1,0:T(8,128)(2,1)} custom-call(bf16[1024,3072]{1,0:T(8,128)(2,1)} %get-tuple-element.186.left_ref, bf16[1536,6144]{1,0:T(8,128)(2,1)} %all-gather.5.cloned.1.call-done.wi_ref.wo_ref.right_ref), custom_call_target="tpu_custom_call" | custom-call | flops 1024 | bytes 1024 | tf_op jit(solution)/shard_map/product/pallas_call | solution.py:502
  436.5 8.9 %collective-permute-done.9 = bf16[64,1536]{1,0:T(8,128)(2,1)S(1)} collective-permute-done((bf16[64,1536]{1,0:T(8,128)(2,1)S(1)}, bf16[64,1536]{1,0:T(8,128)(2,1)S(1)}, u32[]{:S(2)}, u32[]{:S(2)}) %collective-permute-start.9) | collective-permute-done | bytes 196640 | tf_op jit(solution)/shard_map/ppermute | solution.py:902
  463.8 6.4 product.17.do_ref
  498.7 10.9 %collective-permute-done.17.refs_3_ = bf16[4,96,768]{2,1,0:T(8,128)(2,1)} collective-permute-done((bf16[4,96,768]{2,1,0:T(8,128)(2,1)}, bf16[4,96,768]{2,1,0:T(8,128)(2,1)}, u32[]{:S(2)}, u32[]{:S(2)}) %collective-permute-start.17) | collective-permute-done | bytes 589856 | tf_op jit(solution)/shard_map/ppermute | solution.py:910
  511.1 20.0 %self_attend_back.2.right_ref.left_ref = bf16[1024,1152]{1,0:T(8,128)(2,1)} custom-call(s32[1]{0:T(128)} %bitcast.4.t_ref, bf16[1024,2304]{1,0:T(8,128)(2,1)} %fusion.8.q_ref.k_ref.v_ref, bf16[1024,2304]{1,0:T(8,128)(2,1)} %fusion.8.q_ref.k_ref.v_ref, bf16[1024,2304]{1,0:T(8,128)(2,1)} %fusion.8.q_ref.k_ref.v_ref, ...), custom_call_target="tpu_custom_call" | custom-call | flops 20000000000 | bytes 1024 | tf_op jit(solution)/shard_map/self_attend_back/pallas_call | solution.py:678
  531.1 9.2 %weight_halves.17 = (bf16[8,96,1152]{2,1,0:T(8,128)(2,1)}, bf16[8,96,1152]{2,1,0:T(8,128)(2,1)}) custom-call(s32[1]{0:T(128)} %bitcast.side_ref, bf16[1024,1536]{1,0:T(8,128)(2,1)} %fusion.7.left_ref, bf16[1024,1152]{1,0:T(8,128)(2,1)} %self_attend_back.2.right_ref.left_ref), custom_call_target="tpu_custom_call" | custom-call | flops 1024 | bytes 1024 | tf_op jit(solution)/shard_map/weight_halves/pallas_call | solution.py:343
  540.3 6.7 weight_halves.18
  566.3 6.2 product.18.refs_0_
  582.9 20.1 %self_attend_back.3.right_ref.left_ref = bf16[1024,1152]{1,0:T(8,128)(2,1)} custom-call(s32[1]{0:T(128)} %bitcast.4.t_ref, bf16[1024,2304]{1,0:T(8,128)(2,1)} %fusion.8.q_ref.k_ref.v_ref, bf16[1024,2304]{1,0:T(8,128)(2,1)} %fusion.8.q_ref.k_ref.v_ref, bf16[1024,2304]{1,0:T(8,128)(2,1)} %fusion.8.q_ref.k_ref.v_ref, ...), custom_call_target="tpu_custom_call" | custom-call | flops 20000000000 | bytes 1024 | tf_op jit(solution)/shard_map/self_attend_back/pallas_call | solution.py:678
  603.0 9.3 %weight_halves.19 = (bf16[8,96,1152]{2,1,0:T(8,128)(2,1)}, bf16[8,96,1152]{2,1,0:T(8,128)(2,1)}) custom-call(s32[1]{0:T(128)} %bitcast.side_ref, bf16[1024,1536]{1,0:T(8,128)(2,1)} %fusion.7.left_ref, bf16[1024,1152]{1,0:T(8,128)(2,1)} %self_attend_back.3.right_ref.left_ref), custom_call_target="tpu_custom_call" | custom-call | flops 1024 | bytes 1024 | tf_op jit(solution)/shard_map/weight_halves/pallas_call | solution.py:343
  619.8 6.4 product.19.refs_1_
  719.2 8.2 %norm_back.5 = (f32[512,1536]{1,0:T(8,128)}, bf16[512,1536]{1,0:T(8,128)(2,1)}, f32[8,1536]{1,0:T(8,128)}) custom-call(bf16[512,1536]{1,0:T(8,128)(2,1)} %value_ref.2, f32[1,1536]{1,0:T(1,128)} %get-tuple-element.324.gain_ref, f32[512,1536]{1,0:T(8,128)} %get-tuple-element.248.base_ref, f32[512,1536]{1,0:T(8,128)} %product.20.refs_0_, ...), custom_call_target="tpu_custom_call" | custom-call | flops 1024 | bytes 1024 | tf_op jit(solution)/shard_map/norm_back/pallas_call | solution.py:472
  (308 shorter events, 279.7 us)
Async XLA Ops:
  7.2 144.2 %all-gather.3.cloned.1.call-start = ((), (), s32[]{:S(2)}) async-start(), calls=%async_computation.2 | async-start | bytes 25067520 | tf_op jit(solution)/shard_map/all_gather | solution.py:905
  29.9 230.7 %all-gather.5.cloned.1.call-start = ((), (), s32[]{:S(2)}) async-start(), calls=%async_computation.3 | async-start | bytes 20054016 | tf_op jit(solution)/shard_map/all_gather | solution.py:905
  32.3 462.8 %reduce-scatter.3.cloned.1.call-start = ((), (), s32[]{:S(2)}) async-start(), calls=%async_computation.4 | async-start | bytes 10027008 | tf_op jit(solution)/shard_map/reduce_scatter | solution.py:982
  32.4 35.9 %collective-permute-start.1 = (bf16[512,1536]{1,0:T(8,128)(2,1)S(1)}, bf16[512,1536]{1,0:T(8,128)(2,1)S(1)}, u32[]{:S(2)}, u32[]{:S(2)}) collective-permute-start(bf16[512,1536]{1,0:T(8,128)(2,1)S(1)} %copy-done), channel_id=1, source_target_pairs={{0,1},{1,0},{2,3},{3,2},{4,5},{5,4},{6,7},{7,6},{8,9},{9,8},{10,11... | collective-permute-start | bytes 4718600 | tf_op jit(solution)/shard_map/ppermute | solution.py:902
  68.3 35.1 %collective-permute-start.2 = (bf16[512,1536]{1,0:T(8,128)(2,1)S(1)}, bf16[512,1536]{1,0:T(8,128)(2,1)S(1)}, u32[]{:S(2)}, u32[]{:S(2)}) collective-permute-start(bf16[512,1536]{1,0:T(8,128)(2,1)S(1)} %copy-done.13), channel_id=1, source_target_pairs={{0,1},{1,0},{2,3},{3,2},{4,5},{5,4},{6,7},{7,6},{8,9},{9,8},{10,11... | collective-permute-start | bytes 4718600 | tf_op jit(solution)/shard_map/ppermute | solution.py:902
  191.6 41.5 %collective-permute-start.3 = (bf16[512,1536]{1,0:T(8,128)(2,1)S(1)}, bf16[512,1536]{1,0:T(8,128)(2,1)S(1)}, u32[]{:S(2)}, u32[]{:S(2)}) collective-permute-start(bf16[512,1536]{1,0:T(8,128)(2,1)S(1)} %convolution_convert_fusion.1), channel_id=1, source_target_pairs={{0,1},{1,0},{2,3},{3,2},{4,5},{5,4},{6,7},{7,6},{8,9},{9,8},{10,11... | collective-permute-start | bytes 4718600 | tf_op jit(solution)/shard_map/ppermute | solution.py:902
  193.1 39.2 %collective-permute-start.4 = (bf16[64,1536]{1,0:T(8,128)(2,1)S(1)}, bf16[64,1536]{1,0:T(8,128)(2,1)S(1)}, u32[]{:S(2)}, u32[]{:S(2)}) collective-permute-start(bf16[64,1536]{1,0:T(8,128)(2,1)S(1)} %fusion.32), channel_id=1, source_target_pairs={{0,1},{1,0},{2,3},{3,2},{4,5},{5,4},{6,7},{7,6},{8,9},{9,8},{10,11... | collective-permute-start | bytes 589832 | tf_op jit(solution)/shard_map/ppermute | solution.py:902
  259.1 38.0 %collective-permute-start.5 = (bf16[512,1536]{1,0:T(8,128)(2,1)S(1)}, bf16[512,1536]{1,0:T(8,128)(2,1)S(1)}, u32[]{:S(2)}, u32[]{:S(2)}) collective-permute-start(bf16[512,1536]{1,0:T(8,128)(2,1)S(1)} %add_convert_fusion.2.n_ref), channel_id=1, source_target_pairs={{0,1},{1,0},{2,3},{3,2},{4,5},{5,4},{6,7},{7,6},{8,9},{9,8},{10,11... | collective-permute-start | bytes 4718600 | tf_op jit(solution)/shard_map/ppermute | solution.py:902
  324.7 36.1 %collective-permute-start.6 = (bf16[512,1536]{1,0:T(8,128)(2,1)}, bf16[512,1536]{1,0:T(8,128)(2,1)}, u32[]{:S(2)}, u32[]{:S(2)}) collective-permute-start(bf16[512,1536]{1,0:T(8,128)(2,1)} %product.13), channel_id=1, source_target_pairs={{0,1},{1,0},{2,3},{3,2},{4,5},{5,4},{6,7},{7,6},{8,9},{9,8},{10,11... | collective-permute-start | bytes 4718600 | tf_op jit(solution)/shard_map/ppermute | solution.py:902
  341.0 341.4 %reduce-scatter.5.cloned.1.call-start = ((), (), s32[]{:S(2)}) async-start(), calls=%async_computation.5 | async-start | bytes 2211840 | tf_op jit(solution)/shard_map/reduce_scatter | solution.py:914
  404.1 49.3 %collective-permute-start.8 = (bf16[512,1536]{1,0:T(8,128)(2,1)}, bf16[512,1536]{1,0:T(8,128)(2,1)S(1)}, u32[]{:S(2)}, u32[]{:S(2)}) collective-permute-start(bf16[512,1536]{1,0:T(8,128)(2,1)} %get-tuple-element.185), channel_id=1, source_target_pairs={{0,1},{1,0},{2,3},{3,2},{4,5},{5,4},{6,7},{7,6},{8,9},{9,8},{10,11... | collective-permute-start | bytes 4718600 | tf_op jit(solution)/shard_map/ppermute | solution.py:902
  405.3 40.1 %collective-permute-start.9 = (bf16[64,1536]{1,0:T(8,128)(2,1)S(1)}, bf16[64,1536]{1,0:T(8,128)(2,1)S(1)}, u32[]{:S(2)}, u32[]{:S(2)}) collective-permute-start(bf16[64,1536]{1,0:T(8,128)(2,1)S(1)} %pad_maximum_fusion.9), channel_id=1, source_target_pairs={{0,1},{1,0},{2,3},{3,2},{4,5},{5,4},{6,7},{7,6},{8,9},{9,8},{10,11... | collective-permute-start | bytes 589832 | tf_op jit(solution)/shard_map/ppermute | solution.py:902
  406.2 84.4 %collective-permute-start.14 = (bf16[4,96,3072]{2,1,0:T(8,128)(2,1)}, bf16[4,96,3072]{2,1,0:T(8,128)(2,1)}, u32[]{:S(2)}, u32[]{:S(2)}) collective-permute-start(bf16[4,96,3072]{2,1,0:T(8,128)(2,1)} %get-tuple-element.178), channel_id=1, source_target_pairs={{0,4},{2,6},{4,0},{6,2},{8,12},{10,14},{12,8},{14,10},{16,20},{18,... | collective-permute-start | bytes 7077896 | tf_op jit(solution)/shard_map/ppermute | solution.py:910
  426.6 43.7 %collective-permute-start.10 = (bf16[8,96,768]{2,1,0:T(8,128)(2,1)}, bf16[8,96,768]{2,1,0:T(8,128)(2,1)}, u32[]{:S(2)}, u32[]{:S(2)}) collective-permute-start(bf16[8,96,768]{2,1,0:T(8,128)(2,1)} %get-tuple-element.190), channel_id=1, source_target_pairs={{0,2},{2,0},{4,6},{6,4},{8,10},{10,8},{12,14},{14,12},{16,18},{18,... | collective-permute-start | bytes 3538952 | tf_op jit(solution)/shard_map/ppermute | solution.py:910
  435.9 38.1 %collective-permute-start.11 = (bf16[8,96,768]{2,1,0:T(8,128)(2,1)}, bf16[8,96,768]{2,1,0:T(8,128)(2,1)}, u32[]{:S(2)}, u32[]{:S(2)}) collective-permute-start(bf16[8,96,768]{2,1,0:T(8,128)(2,1)} %get-tuple-element.194), channel_id=1, source_target_pairs={{0,2},{2,0},{4,6},{6,4},{8,10},{10,8},{12,14},{14,12},{16,18},{18,... | collective-permute-start | bytes 3538952 | tf_op jit(solution)/shard_map/ppermute | solution.py:910
  449.5 28.2 %collective-permute-start.12 = (bf16[8,96,768]{2,1,0:T(8,128)(2,1)}, bf16[8,96,768]{2,1,0:T(8,128)(2,1)}, u32[]{:S(2)}, u32[]{:S(2)}) collective-permute-start(bf16[8,96,768]{2,1,0:T(8,128)(2,1)} %get-tuple-element.197), channel_id=1, source_target_pairs={{0,2},{2,0},{4,6},{6,4},{8,10},{10,8},{12,14},{14,12},{16,18},{18,... | collective-permute-start | bytes 3538952 | tf_op jit(solution)/shard_map/ppermute | solution.py:910
  454.6 28.0 %collective-permute-start.13 = (bf16[8,96,768]{2,1,0:T(8,128)(2,1)}, bf16[8,96,768]{2,1,0:T(8,128)(2,1)}, u32[]{:S(2)}, u32[]{:S(2)}) collective-permute-start(bf16[8,96,768]{2,1,0:T(8,128)(2,1)} %get-tuple-element.199), channel_id=1, source_target_pairs={{0,2},{2,0},{4,6},{6,4},{8,10},{10,8},{12,14},{14,12},{16,18},{18,... | collective-permute-start | bytes 3538952 | tf_op jit(solution)/shard_map/ppermute | solution.py:910
  488.6 61.0 %collective-permute-start.18 = (bf16[8,96,768]{2,1,0:T(8,128)(2,1)}, bf16[8,96,768]{2,1,0:T(8,128)(2,1)}, u32[]{:S(2)}, u32[]{:S(2)}) collective-permute-start(bf16[8,96,768]{2,1,0:T(8,128)(2,1)} %get-tuple-element.188), channel_id=1, source_target_pairs={{0,2},{2,0},{4,6},{6,4},{8,10},{10,8},{12,14},{14,12},{16,18},{18,... | collective-permute-start | bytes 3538952 | tf_op jit(solution)/shard_map/ppermute | solution.py:910
  488.6 64.9 %collective-permute-start.20 = (bf16[8,96,768]{2,1,0:T(8,128)(2,1)}, bf16[8,96,768]{2,1,0:T(8,128)(2,1)}, u32[]{:S(2)}, u32[]{:S(2)}) collective-permute-start(bf16[8,96,768]{2,1,0:T(8,128)(2,1)} %get-tuple-element.192), channel_id=1, source_target_pairs={{0,2},{2,0},{4,6},{6,4},{8,10},{10,8},{12,14},{14,12},{16,18},{18,... | collective-permute-start | bytes 3538952 | tf_op jit(solution)/shard_map/ppermute | solution.py:910
  490.6 62.9 %collective-permute-start.21 = (bf16[8,96,768]{2,1,0:T(8,128)(2,1)S(1)}, bf16[8,96,768]{2,1,0:T(8,128)(2,1)}, u32[]{:S(2)}, u32[]{:S(2)}) collective-permute-start(bf16[8,96,768]{2,1,0:T(8,128)(2,1)S(1)} %copy-done.25), channel_id=1, source_target_pairs={{0,1},{1,0},{2,3},{3,2},{4,5},{5,4},{6,7},{7,6},{8,9},{9,8},{10,11... | collective-permute-start | bytes 3538952 | tf_op jit(solution)/shard_map/ppermute | solution.py:902
  497.9 51.8 %collective-permute-start.19 = (bf16[8,96,768]{2,1,0:T(8,128)(2,1)S(1)}, bf16[8,96,768]{2,1,0:T(8,128)(2,1)}, u32[]{:S(2)}, u32[]{:S(2)}) collective-permute-start(bf16[8,96,768]{2,1,0:T(8,128)(2,1)S(1)} %copy-done.26), channel_id=1, source_target_pairs={{0,1},{1,0},{2,3},{3,2},{4,5},{5,4},{6,7},{7,6},{8,9},{9,8},{10,11... | collective-permute-start | bytes 3538952 | tf_op jit(solution)/shard_map/ppermute | solution.py:902
  509.6 47.8 %collective-permute-start.22 = (bf16[2,96,3072]{2,1,0:T(8,128)(2,1)}, bf16[2,96,3072]{2,1,0:T(8,128)(2,1)S(1)}, u32[]{:S(2)}, u32[]{:S(2)}) collective-permute-start(bf16[2,96,3072]{2,1,0:T(8,128)(2,1)} %get-tuple-element.216), channel_id=1, source_target_pairs={{0,8},{2,10},{4,12},{6,14},{8,0},{10,2},{12,4},{14,6},{16,24},{18,... | collective-permute-start | bytes 3538952 | tf_op jit(solution)/shard_map/ppermute | solution.py:910
  561.3 98.5 %collective-permute-start.41 = (bf16[1,96,3072]{2,1,0:T(8,128)(2,1)}, bf16[1,96,3072]{2,1,0:T(8,128)(2,1)}, u32[]{:S(2)}, u32[]{:S(2)}) collective-permute-start(bf16[1,96,3072]{2,1,0:T(8,128)(2,1)} %get-tuple-element.238), channel_id=1, source_target_pairs={{0,16},{2,18},{4,20},{6,22},{8,24},{10,26},{12,28},{14,30},{16,0},... | collective-permute-start | bytes 1769480 | tf_op jit(solution)/shard_map/ppermute | solution.py:910
  563.7 73.5 %collective-permute-start.28 = (bf16[4,96,768]{2,1,0:T(8,128)(2,1)}, bf16[4,96,768]{2,1,0:T(8,128)(2,1)}, u32[]{:S(2)}, u32[]{:S(2)}) collective-permute-start(bf16[4,96,768]{2,1,0:T(8,128)(2,1)} %get-tuple-element.236), channel_id=1, source_target_pairs={{0,4},{2,6},{4,0},{6,2},{8,12},{10,14},{12,8},{14,10},{16,20},{18,... | collective-permute-start | bytes 1769480 | tf_op jit(solution)/shard_map/ppermute | solution.py:910
  564.1 48.2 %collective-permute-start.25 = (bf16[4,96,768]{2,1,0:T(8,128)(2,1)}, bf16[4,96,768]{2,1,0:T(8,128)(2,1)}, u32[]{:S(2)}, u32[]{:S(2)}) collective-permute-start(bf16[4,96,768]{2,1,0:T(8,128)(2,1)} %get-tuple-element.234), channel_id=1, source_target_pairs={{0,4},{2,6},{4,0},{6,2},{8,12},{10,14},{12,8},{14,10},{16,20},{18,... | collective-permute-start | bytes 1769480 | tf_op jit(solution)/shard_map/ppermute | solution.py:910
  573.6 42.1 %collective-permute-start.15 = (bf16[512,1536]{1,0:T(8,128)(2,1)S(1)}, bf16[512,1536]{1,0:T(8,128)(2,1)S(1)}, u32[]{:S(2)}, u32[]{:S(2)}) collective-permute-start(bf16[512,1536]{1,0:T(8,128)(2,1)S(1)} %copy-done.19), channel_id=1, source_target_pairs={{0,1},{1,0},{2,3},{3,2},{4,5},{5,4},{6,7},{7,6},{8,9},{9,8},{10,11... | collective-permute-start | bytes 4718600 | tf_op jit(solution)/shard_map/ppermute | solution.py:902
  578.6 38.9 %collective-permute-start.26 = (bf16[4,96,1152]{2,1,0:T(8,128)(2,1)}, bf16[4,96,1152]{2,1,0:T(8,128)(2,1)}, u32[]{:S(2)}, u32[]{:S(2)}) collective-permute-start(bf16[4,96,1152]{2,1,0:T(8,128)(2,1)} %get-tuple-element.241), channel_id=1, source_target_pairs={{0,4},{2,6},{4,0},{6,2},{8,12},{10,14},{12,8},{14,10},{16,20},{18,... | collective-permute-start | bytes 2654216 | tf_op jit(solution)/shard_map/ppermute | solution.py:910
  629.9 27.2 %collective-permute-start.30 = (bf16[2,96,1152]{2,1,0:T(8,128)(2,1)}, bf16[2,96,1152]{2,1,0:T(8,128)(2,1)S(1)}, u32[]{:S(2)}, u32[]{:S(2)}) collective-permute-start(bf16[2,96,1152]{2,1,0:T(8,128)(2,1)} %get-tuple-element.256), channel_id=1, source_target_pairs={{0,8},{2,10},{4,12},{6,14},{8,0},{10,2},{12,4},{14,6},{16,24},{18,... | collective-permute-start | bytes 1327112 | tf_op jit(solution)/shard_map/ppermute | solution.py:910
  630.3 58.7 %collective-permute-start.31 = (bf16[512,1536]{1,0:T(8,128)(2,1)}, bf16[512,1536]{1,0:T(8,128)(2,1)S(1)}, u32[]{:S(2)}, u32[]{:S(2)}) collective-permute-start(bf16[512,1536]{1,0:T(8,128)(2,1)} %add_convert_fusion), channel_id=1, source_target_pairs={{0,1},{1,0},{2,3},{3,2},{4,5},{5,4},{6,7},{7,6},{8,9},{9,8},{10,11... | collective-permute-start | bytes 4718600 | tf_op jit(solution)/shard_map/ppermute | solution.py:902
  637.2 32.9 %collective-permute-start.32 = (bf16[4,96,1152]{2,1,0:T(8,128)(2,1)}, bf16[4,96,1152]{2,1,0:T(8,128)(2,1)S(1)}, u32[]{:S(2)}, u32[]{:S(2)}) collective-permute-start(bf16[4,96,1152]{2,1,0:T(8,128)(2,1)} %get-tuple-element.259), channel_id=1, source_target_pairs={{0,4},{2,6},{4,0},{6,2},{8,12},{10,14},{12,8},{14,10},{16,20},{18,... | collective-permute-start | bytes 2654216 | tf_op jit(solution)/shard_map/ppermute | solution.py:910
  643.8 36.8 %collective-permute-start.34 = (bf16[2,96,768]{2,1,0:T(8,128)(2,1)}, bf16[2,96,768]{2,1,0:T(8,128)(2,1)}, u32[]{:S(2)}, u32[]{:S(2)}) collective-permute-start(bf16[2,96,768]{2,1,0:T(8,128)(2,1)} %get-tuple-element.263), channel_id=1, source_target_pairs={{0,8},{2,10},{4,12},{6,14},{8,0},{10,2},{12,4},{14,6},{16,24},{18,... | collective-permute-start | bytes 884744 | tf_op jit(solution)/shard_map/ppermute | solution.py:910
  659.8 30.1 %collective-permute-start.37 = (bf16[1,96,1152]{2,1,0:T(8,128)(2,1)}, bf16[1,96,1152]{2,1,0:T(8,128)(2,1)S(1)}, u32[]{:S(2)}, u32[]{:S(2)}) collective-permute-start(bf16[1,96,1152]{2,1,0:T(8,128)(2,1)} %get-tuple-element.267), channel_id=1, source_target_pairs={{0,16},{2,18},{4,20},{6,22},{8,24},{10,26},{12,28},{14,30},{16,0},... | collective-permute-start | bytes 663560 | tf_op jit(solution)/shard_map/ppermute | solution.py:910
  (69 other events, 758.7 us)
Sparse Core Ops, SparseCore 0:
  30.0 121.3 all-gather.2
  153.6 98.8 all-gather.4
  341.2 125.7 reduce-scatter.2
  617.5 54.3 reduce-scatter.4

commit v3 on v2

--- a/solution.py
+++ b/solution.py
@@ -364,29 +364,45 @@
     return total.astype(BF)
 
 
-def fold_kernel(side_ref, *refs):
+def pairs_per_step(count, row_bytes):
+    while count > 1 and count % 2 == 0 and count * row_bytes > 5_000_000:
+        count //= 2
+    return count
+
+
+def fold_kernel(side_ref, *refs, counts):
+    send_ref, keep_ref = refs[-2:]
     side = side_ref[0]
-    refs[-2][...] = added(refs[:-2], pl.ds(1 - side, 1))
-    refs[-1][...] = added(refs[:-2], pl.ds(side, 1))
-
-
-def fold(side, *terms):
-    count, shard, size = terms[0].shape[0] // 2, terms[0].shape[1], terms[0].shape[2]
-    shape = jax.ShapeDtypeStruct((count, shard, size), BF)
-    whole = pl.BlockSpec((2, shard, size), lambda j, s: (j, 0, 0))
-    part = pl.BlockSpec((1, shard, size), lambda j, s: (j, 0, 0))
+    first, at = 0, 0
+    for count in counts:
+        terms = refs[at : at + count]
+        size = terms[0].shape[2]
+        for pair in range(keep_ref.shape[0]):
+            for out_ref, bit in ((send_ref, 1 - side), (keep_ref, side)):
+                out_ref[pair, :, first : first + size] = added(terms, 2 * pair + bit)
+        first, at = first + size, at + count
+
+
+def fold(side, *groups, cost=None):
+    count, shard = groups[0][0].shape[0] // 2, groups[0][0].shape[1]
+    sizes = [terms[0].shape[2] for terms in groups]
+    row = sum(4 * shard * size * (len(terms) + 1) for size, terms in zip(sizes, groups))
+    per = pairs_per_step(count, row)
+    shape = jax.ShapeDtypeStruct((count, shard, sum(sizes)), BF)
+    spec = lambda size: pl.BlockSpec((2 * per, shard, size), lambda j, s: (j, 0, 0))
+    part = pl.BlockSpec((per, shard, sum(sizes)), lambda j, s: (j, 0, 0))
     return pl.pallas_call(
-        fold_kernel,
+        partial(fold_kernel, counts=[len(terms) for terms in groups]),
         out_shape=(shape, shape),
         grid_spec=pltpu.PrefetchScalarGridSpec(
             num_scalar_prefetch=1,
-            grid=(count,),
-            in_specs=[whole] * len(terms),
+            grid=(count // per,),
+            in_specs=[spec(size) for size, terms in zip(sizes, groups) for _ in terms],
             out_specs=[part, part],
         ),
         name="fold",
-        cost_estimate=LIGHT,
-    )(side, *terms)
+        cost_estimate=cost or LIGHT,
+    )(side, *[v for terms in groups for v in terms])
 
 
 def totals_kernel(*refs, counts):
@@ -398,13 +414,15 @@
         first, at = first + size, at + count
 
 
-def totals(groups):
+def totals(*groups):
     count, shard = groups[0][0].shape[:2]
     sizes = [terms[0].shape[2] for terms in groups]
-    spec = lambda size: pl.BlockSpec((2, shard, size), lambda j: (j, 0, 0))
+    row = sum(2 * shard * size * (len(terms) + 1) for size, terms in zip(sizes, groups))
+    per = pairs_per_step(count, row)
+    spec = lambda size: pl.BlockSpec((per, shard, size), lambda j: (j, 0, 0))
     return pl.pallas_call(
         partial(totals_kernel, counts=[len(terms) for terms in groups]),
-        grid=(count // 2,),
+        grid=(count // per,),
         out_shape=jax.ShapeDtypeStruct((count, shard, sum(sizes)), BF),
         in_specs=[spec(size) for size, terms in zip(sizes, groups) for _ in terms],
         out_specs=spec(sum(sizes)),
@@ -413,11 +431,31 @@
     )(*[v for terms in groups for v in terms])
 
 
+def pack_kernel(*refs, parts):
+    out_ref = refs[-1]
+    first = 0
+    for which, begin, end, turned in parts:
+        ref = refs[which]
+        value = ref[begin:end, :].T if turned else ref[:, begin:end]
+        out_ref[:, first : first + end - begin] = value
+        first += end - begin
+
+
+def pack(arrays, parts):
+    shard = arrays[0].shape[0]
+    return pl.pallas_call(
+        partial(pack_kernel, parts=parts),
+        out_shape=jax.ShapeDtypeStruct((shard, sum(end - begin for _, begin, end, _ in parts)), BF),
+        name="pack",
+        cost_estimate=LIGHT,
+    )(*arrays)
+
+
 def norm_sums_kernel(value_ref, *refs):
     sums_ref = refs[-1]
-    incoming = refs[0][...]
+    incoming = refs[0][...].astype(F32)
     for ref in refs[1:-1]:
-        incoming = incoming + ref[...]
+        incoming = incoming + ref[...].astype(F32)
     centred, scale = stats_of(value_ref[...].astype(F32))
 
     @pl.when(pl.program_id(0) == 0)
@@ -430,7 +468,7 @@
 
 def norm_sums(value, incoming):
     rows, width = value.shape
-    tile = 128
+    tile = 256 if rows % 256 == 0 else 128
     spec = pl.BlockSpec((tile, width), lambda j: (j, 0))
     return pl.pallas_call(
         norm_sums_kernel,
@@ -467,7 +505,7 @@
 
 def norm_back_rows(value, gain, base, incoming, cost=LIGHT):
     rows, width = value.shape
-    tile = 128
+    tile = 256 if rows % 256 == 0 else 128
     spec = pl.BlockSpec((tile, width), lambda j: (j, 0))
     return pl.pallas_call(
         partial(norm_back_kernel, parts=len(incoming)),
@@ -482,6 +520,30 @@
         name="norm_back",
         cost_estimate=cost,
     )(value, gain.reshape(1, width), base, *incoming)
+
+
+def joint_kernel(*refs):
+    right_ref, out_ref = refs[-2:]
+    depth = refs[0].shape[1]
+    total = None
+    for i, ref in enumerate(refs[:-2]):
+        term = mm(ref[...], right_ref[:, i * depth : (i + 1) * depth], NT)
+        total = term if total is None else total + term
+    out_ref[...] = total.astype(out_ref.dtype)
+
+
+def joint_product(lefts, right, dtype, row, rows, cost):
+    depth, size, tile = lefts[0].shape[1], right.shape[0], 512
+    return pl.pallas_call(
+        joint_kernel,
+        grid=(size // tile,),
+        out_shape=jax.ShapeDtypeStruct((rows, size), dtype),
+        in_specs=[pl.BlockSpec((rows, depth), lambda j: (row, 0))] * len(lefts)
+        + [pl.BlockSpec((tile, depth * len(lefts)), lambda j: (j, 0))],
+        out_specs=pl.BlockSpec((rows, tile), lambda j: (0, j)),
+        name="joint_product",
+        cost_estimate=cost,
+    )(*lefts, right)
 
 
 def product_kernel(left_ref, right_ref, out_ref, *, dims):
@@ -901,8 +963,8 @@
     def peer(value):
         return lax.ppermute(value, "tensor", [(0, 1), (1, 0)])
 
-    def gather(parts):
-        return lax.all_gather(jnp.concatenate(parts, axis=1), "dp", axis=0, tiled=True)
+    def gather(packed):
+        return lax.all_gather(packed, "dp", axis=0, tiled=True)
 
     swaps = [[(i, i ^ (1 << level)) for i in range(groups)] for level in range(len(bits))]
 
@@ -916,13 +978,13 @@
         )
 
     def line_step(send, keep, ready):
-        return fold(side_refs[3], after(keep, ready), swap(send, 2))
+        return fold(side_refs[3], (after(keep, ready), swap(send, 2)))
 
     def line_end(send, keep):
         for level in range(3, len(bits)):
             got = swap(send, level)
             if level + 1 < len(bits):
-                send, keep = fold(side_refs[level + 1], keep, got)
+                send, keep = fold(side_refs[level + 1], (keep, got))
         return (keep.astype(F32) + got.astype(F32)).reshape(shard, -1)
 
     part = half // CUTS
@@ -933,12 +995,17 @@
     )
     cross_two = jnp.concatenate([cross_query, cross_output.T], axis=1)
     cross_peer = peer(cross_two)
+    taken = [(which, p.start, p.stop, False) for p in pieces for which in range(3)]
+    taken += [(3, 0, half, True), (4, 0, half, False), (5, 0, half, False)]
+    taken += [(6, 0, half, False), (7, 0, half, False), (6, half, width, False), (7, half, width, False)]
     first = gather(
-        [v[:, p] for p in pieces for v in (self_query, self_key, self_value)]
-        + [self_output.T, cross_key, cross_value]
-        + [cross_query, cross_peer[:, :half], cross_two[:, half:], cross_peer[:, half:]]
-    )
-    second = gather([inner_weight, outer_weight.T])
+        pack(
+            [self_query, self_key, self_value, self_output, cross_key, cross_value]
+            + [cross_two, cross_peer],
+            taken,
+        )
+    )
+    second = gather(pack([inner_weight, outer_weight], [(0, 0, hidden, False), (1, 0, hidden, True)]))
     inputs_peer = peer(after(start_x, cross_peer))
     grads_peer = peer(after(cotangent, inputs_peer))
     w_qkv = first[:, : 3 * half]
@@ -997,7 +1064,7 @@
         state2, norm_gains[2], cotangent, [back3_home, back3_away], HEAVY
     )
     d_mixed2 = product(g2, first, NN, BF, first=8 * half, size=width)
-    inner = fold(side_refs[1], after(inner[1], d_mixed2), inner_got)
+    inner = fold(side_refs[1], (after(inner[1], d_mixed2), inner_got))
     inner_got = swap(inner[0], 1)
     d_mixed2 = after(d_mixed2, inner[0])
     d_query2, d_key2, d_value2 = cross_backward(query2, key2, value2, mixed2, d_mixed2, lse2)
@@ -1019,7 +1086,15 @@
     cq_own, cq_away = two(normed2, d_query2)
     d_text = (d_text_keep + after(d_text_peer, last).astype(F32)).astype(BF)
     kv = two(text, d_text)
-    text_terms = mm(after(d_text, last), w_text, NT).astype(BF)
+    grads1 = jnp.concatenate([g1, after(g1_peer, last)], axis=0)
+    d_mixed1 = product(grads1, first, NN, BF, first=3 * half, size=half)
+    co_send = totals((after(co_away[0], d_mixed1), co_away[1]))
+    co_got = peer(co_send)
+    cq_send = totals((after(cq_away[0], co_send), cq_away[1]))
+    cq_got = peer(cq_send)
+    inner = fold(side_refs[2], (after(inner[1], cq_send), inner_got))
+    found0 = self_backward(t_ref, qkv, mixed1, after(d_mixed1, inner[0], outer_sum), lse1, 0)
+    text_terms = mm(after(d_text, found0), w_text, NT).astype(BF)
     text_keep, text_send = (
         lax.dynamic_slice(
             text_terms, (zero, at), (text_terms.shape[0], half), allow_negative_indices=False
@@ -1027,73 +1102,49 @@
         for at in (mine, theirs)
     )
 
-    grads1 = jnp.concatenate([g1, after(g1_peer, text_send, last)], axis=0)
-    d_mixed1 = product(grads1, first, NN, BF, first=3 * half, size=half)
-    co_send = totals([(after(co_away[0], d_mixed1), co_away[1])])
-    co_got = peer(co_send)
-    cq_send = totals([(after(cq_away[0], co_send), cq_away[1])])
-    cq_got = peer(cq_send)
-    kv = [fold(side_refs[1], after(keep, cq_send), got) for keep, got in kv]
-    kv = [(keep, swap(send, 1)) for send, keep in kv]
-    inner = fold(side_refs[2], after(inner[1], cq_send), inner_got)
-    found0 = self_backward(
-        t_ref, qkv, mixed1, after(d_mixed1, kv[0][0], kv[1][0], inner[0], outer_sum), lse1, 0
-    )
-    text_got = peer(after(text_send, found0))
+    text_got = peer(text_send)
     out_away = peer(after(out_part, found0))
     last = found0
     qkv0 = weight_core(normed1, found0)
     qkv0_got = swap(qkv0[0], 0)
     so = weight_core(grads1, mixed1)
     so_got = swap(so[0], 0)
-    kv_whole = totals([(after(kv[0][0], last), kv[0][1]), kv[1]])
-    co = fold(side_refs[1], after(co_own[0], kv_whole), co_own[1], co_got)
-    co_got = swap(co[0], 1)
-    cq = fold(side_refs[1], after(cq_own[0], co[0]), cq_own[1], cq_got)
-    cq_got = swap(cq[0], 1)
-    inner = line_step(*inner, cq[0])
-    away0 = product(after(found0, inner[0]), first, NT, F32, row=1, rows=rows, cost=HEAVY)
-    qkv0 = fold(side_refs[1], after(qkv0[1], away0), qkv0_got)
-    qkv0_got = swap(qkv0[0], 1)
-    so = fold(side_refs[1], after(so[1], qkv0[0]), so_got)
-    so_got = swap(so[0], 1)
-    found1 = self_backward(t_ref, qkv, mixed1, after(d_mixed1, so[0]), lse1, 1)
+    kv = fold(side_refs[1], *[(after(keep, last), got) for keep, got in kv])
+    kv_got = swap(kv[0], 1)
+    cross = fold(
+        side_refs[1],
+        (after(co_own[0], kv[0]), co_own[1], co_got),
+        (cq_own[0], cq_own[1], cq_got),
+    )
+    cross_got = swap(cross[0], 1)
+    inner_first = after(inner[1], cross[0]), swap(inner[0], 2)
+    inner = fold(side_refs[3], inner_first, cost=HEAVY)
+    most = fold(side_refs[1], (after(qkv0[1], inner[0]), qkv0_got), (so[1], so_got))
+    most_got = swap(most[0], 1)
+    kv = totals((after(kv[1], most[0]), kv_got))
+    found1 = self_backward(t_ref, qkv, mixed1, after(d_mixed1, kv), lse1, 1)
     last = found1
     qkv1 = weight_core(normed1, found1)
     qkv1_got = swap(qkv1[0], 0)
-    whole = totals([(after(co[1], qkv1[0]), co_got), (kv_whole,)])
-    sum_a = line_sum(whole)
-    qkv0 = fold(side_refs[2], after(qkv0[1], whole), qkv0_got)
-    away1 = product(
-        after(found1, qkv0[0]),
-        first,
-        NT,
-        F32,
-        row=1,
-        rows=rows,
-        first=3 * part,
-        cost=HEAVY,
-    )
-    back1_part = (away0 + away1).astype(BF)
+    cross = totals((after(cross[1], qkv1[0]), cross_got), (kv,))
+    cross_sum = line_sum(cross)
+    most = fold(side_refs[2], (after(most[1], cross), most_got))
+    back1_part = joint_product([found0, after(found1, most[0])], first, BF, 1, rows, HEAVY)
     back1_away = peer(back1_part)
-    qkv1 = fold(side_refs[1], after(qkv1[1], back1_part), qkv1_got)
+    qkv1 = fold(side_refs[1], (after(qkv1[1], back1_part), qkv1_got))
     qkv1_got = swap(qkv1[0], 1)
-    cq = fold(side_refs[2], after(cq[1], qkv1[0]), cq_got)
-    so = fold(side_refs[2], after(so[1], cq[0]), so_got)
-    home0 = product(after(found0, so[0]), first, NT, F32, row=0, rows=rows)
-    qkv0 = line_step(*qkv0, home0)
-    home1 = product(after(found1, qkv0[0]), first, NT, F32, row=0, rows=rows, first=3 * part)
-    qkv1 = fold(side_refs[2], after(qkv1[1], home1), qkv1_got)
-    sums0 = norm_sums(after(inputs_peer, qkv1[0]), [away0, away1])
-    cq = line_step(*cq, sums0)
-    so = line_step(*so, cq[0])
-    sums1 = sums0 + norm_sums(after(inputs, so[0], sum_a), [home0, home1])
+    back1_home = joint_product([found0, after(found1, qkv1[0])], first, F32, 0, rows, LIGHT)
+    most = line_step(*most, back1_home)
+    sums0 = norm_sums(after(inputs_peer, most[0]), [back1_part])
+    qkv1 = fold(side_refs[2], (after(qkv1[1], sums0), qkv1_got))
+    sums1 = sums0 + norm_sums(after(inputs, qkv1[0], cross_sum), [back1_home])
     qkv1 = line_step(*qkv1, sums1)
     input_grad, _, _ = norm_back_rows(
-        inputs, norm_gains[0], grad1, [home0, home1, after(back1_away, qkv1[0])]
-    )
-    inner_sum = line_end(inner[0], after(inner[1], home0))
-    qkv0_sum, cq_sum, so_sum, qkv1_sum = (line_end(*v) for v in (qkv0, cq, so, qkv1))
+        inputs, norm_gains[0], grad1, [back1_home, after(back1_away, qkv1[0])]
+    )
+    inner_sum = line_end(inner[0], after(inner[1], back1_home))
+    most_sum, qkv1_sum = line_end(*most), line_end(*qkv1)
+    qkv0_sum, so_sum = most_sum[:, : 3 * part], most_sum[:, 3 * part :]
     output = (state2 + out_home + after(out_away, last).astype(F32)).astype(BF)
     text_grad = text_keep.astype(F32) + after(text_got, last).astype(F32)
     text_grad = text_grad.reshape(1, -1, half)
@@ -1118,10 +1169,10 @@
         joined(1),
         joined(2),
         so_sum.T,
-        cq_sum,
-        sum_a[:, half : 2 * half].astype(F32),
-        sum_a[:, 2 * half :].astype(F32),
-        sum_a[:, :half].astype(F32).T,
+        cross_sum[:, half : 2 * half].astype(F32),
+        cross_sum[:, 2 * half : 3 * half].astype(F32),
+        cross_sum[:, 3 * half :].astype(F32),
+        cross_sum[:, :half].astype(F32).T,
         inner_sum.astype(F32),
         outer_sum.astype(F32).T,
         small[:3],

time: 752 us -> 716 us (0.952)
  Pallas kernels: 362 us -> 335 us
  waiting for transfers between devices: 192 us -> 208 us
  local copies, waits for them, and re-layouts: 42.8 us -> 26.9 us
    pallas_call x11 -> x7, Pallas kernels: 82.4 us -> 57.7 us  [product(): pl.pallas_call(partial(product_kernel, dims=dims), grid=(size // tile,),...]
    unnamed x114 -> x92, local copies, waits for them, and re-layouts: 33.7 us -> 17.6 us
    ppermute x28 -> x21, starting transfers between devices: 22.9 us -> 12.7 us  [swap(): return lax.ppermute(send, 'dp', swaps[level])]
    ppermute x28 -> x21, waiting for transfers between devices: 32.7 us -> 38.6 us  [swap(): return lax.ppermute(send, 'dp', swaps[level])]
    pallas_call x18 -> x15, Pallas kernels: 55.8 us -> 60 us  [the longest x11 38 us: fold(): pl.pallas_call(partial(fold_kernel, counts=[len(terms) for terms in group...]
  transfers between devices with their start and end apart: 51 -> 44, of which waited for: 13 -> 17; matrix products, arithmetic and copies ran while one was open for 15% -> 13% of each run, Pallas kernels for 45% -> 44%
where the time goes in v3:
time: 716 us; the launch traced here: 704 us
  Pallas kernels  335 us (47%)
  waiting for transfers between devices  208 us (29%)
  matrix products  53.5 us (7%)
  starting transfers between devices  38.2 us (5%)
  other arithmetic  27.3 us (4%)
  local copies, waits for them, and re-layouts  26.9 us (4%)
  between operations  14.7 us (2%)
    ppermute x15, waiting for transfers between devices, peer(): return lax.ppermute(value, 'tensor', [(0, 1), (1, 0)])  119 us
    pallas_call x10, Pallas kernels, weight_halves(): pl.pallas_call(partial(weight_kernel, shard=shard), out_shape=(shape, sha...  67.6 us
    pallas_call x7, Pallas kernels, product(): pl.pallas_call(partial(product_kernel, dims=dims), grid=(size // tile,),...  57.7 us
    dot_general x8, matrix products, mm(): return lax.dot_general(left, right, dims, preferred_element_type=F32)  53.5 us
    all_gather x2, waiting for transfers between devices, gather(): return lax.all_gather(packed, 'dp', axis=0, tiled=True)  44.8 us
    pallas_call x2, Pallas kernels, self_backward(): pl.pallas_call(self_back_kernel, out_shape=jax.ShapeDtypeStruct((length,...  40 us
    ppermute x21, waiting for transfers between devices, swap(): return lax.ppermute(send, 'dp', swaps[level])  38.6 us
    pallas_call x11, Pallas kernels, fold(): pl.pallas_call(partial(fold_kernel, counts=[len(terms) for terms in group...  38 us
  transfers between devices with their start and end apart: 44, of which 17 were waited for; matrix products, arithmetic and copies ran while one was open for 13% of the time, Pallas kernels for 44%

profile of v3, /device:TPU:0, one launch (start us, length us, event | category | flops | bytes accessed | tf_op | source)
XLA Modules:
  0.0 704.1 jit_solution(15419957683942233880)
XLA Ops:
  30.6 31.9 %collective-permute-done.1.value_ref = bf16[512,1536]{1,0:T(8,128)(2,1)S(1)} collective-permute-done((bf16[512,1536]{1,0:T(8,128)(2,1)S(1)}, bf16[512,1536]{1,0:T(8,128)(2,1)S(1)}, u32[]{:S(2)}, u32[]{:S(2)}) %collective-permute-start.1) | collective-permute-done | bytes 1572896 | tf_op jit(solution)/shard_map/ppermute | solution.py:964
  70.3 27.0 %collective-permute-done.2.g_ref = bf16[512,1536]{1,0:T(8,128)(2,1)S(1)} collective-permute-done((bf16[512,1536]{1,0:T(8,128)(2,1)S(1)}, bf16[512,1536]{1,0:T(8,128)(2,1)S(1)}, u32[]{:S(2)}, u32[]{:S(2)}) %collective-permute-start.2) | collective-permute-done | bytes 1572896 | tf_op jit(solution)/shard_map/ppermute | solution.py:964
  99.7 44.8 %all-gather.3.cloned.1.call-done.right_ref.refs_2_ = bf16[1536,7680]{1,0:T(8,128)(2,1)} async-done(((bf16[96,7680]{1,0:T(8,128)(2,1)}), bf16[1536,7680]{1,0:T(8,128)(2,1)}) %all-gather.3.cloned.1.call-update) | async-done | bytes 23592976 | tf_op jit(solution)/shard_map/all_gather | solution.py:967
  147.9 12.1 %fusion.8.q_ref.k_ref.v_ref = bf16[1024,2304]{1,0:T(8,128)(2,1)} fusion(bf16[1024,1536]{1,0:T(8,128)(2,1)S(1)} %copy-done.1, bf16[1536,7680]{1,0:T(8,128)(2,1)} %all-gather.3.cloned.1.call-done.right_ref.refs_2_), kind=kOutput, calls=%fused_computation.11 | convolution fusion | flops 7250116608 | bytes 14942208 | tf_op jit(solution)/shard_map/dot_general | solution.py:315
  160.0 21.0 %self_attend.1 = (bf16[1024,768]{1,0:T(8,128)(2,1)}, f32[6,8,1024]{2,1,0:T(8,128)}) custom-call(s32[1]{0:T(128)} %bitcast.4.t_ref, bf16[1024,2304]{1,0:T(8,128)(2,1)} %fusion.8.q_ref.k_ref.v_ref, bf16[1024,2304]{1,0:T(8,128)(2,1)} %fusion.8.q_ref.k_ref.v_ref, bf16[1024,2304]{1,0:T(8,128)(2,1)} %fusion.8.q_ref.k_ref.v_ref), custom_call_target="tpu_custom_call" | custom-call | flops 1024 | bytes 1024 | tf_op jit(solution)/shard_map/self_attend/pallas_call | solution.py:649
  186.8 38.6 %collective-permute-done.4 = bf16[64,1536]{1,0:T(8,128)(2,1)S(1)} collective-permute-done((bf16[64,1536]{1,0:T(8,128)(2,1)S(1)}, bf16[64,1536]{1,0:T(8,128)(2,1)S(1)}, u32[]{:S(2)}, u32[]{:S(2)}) %collective-permute-start.4) | collective-permute-done | bytes 196640 | tf_op jit(solution)/shard_map/ppermute | solution.py:964
  231.9 6.7 fusion.23.q_ref
  238.6 6.8 cross_attend.1
  253.7 17.0 %ffn_middle.2 = (bf16[1024,3072]{1,0:T(8,128)(2,1)}, bf16[1024,3072]{1,0:T(8,128)(2,1)}) custom-call(bf16[512,1536]{1,0:T(8,128)(2,1)} %copy-done.8, bf16[512,1536]{1,0:T(8,128)(2,1)} %base_ref.1, bf16[1536,6144]{1,0:T(8,128)(2,1)} %all-gather.5.cloned.1.call-done.wi_ref.wo_ref.right_ref, bf16[1536,6144]{1,0:T(8,128)(2,1)} %all-gather.5.cloned.1.call-done.wi_ref.wo_ref.right_ref), custom_call_target="tpu_custom_call" | custom-call | flops 1024 | bytes 1024 | tf_op jit(solution)/shard_map/ffn_middle/pallas_call | solution.py:893
  270.7 9.8 %product.7 = f32[512,1536]{1,0:T(8,128)} custom-call(bf16[1024,3072]{1,0:T(8,128)(2,1)} %get-tuple-element.140.left_ref.refs_0_, bf16[1536,6144]{1,0:T(8,128)(2,1)} %all-gather.5.cloned.1.call-done.wi_ref.wo_ref.right_ref), custom_call_target="tpu_custom_call" | custom-call | flops 1024 | bytes 1024 | tf_op jit(solution)/shard_map/product/pallas_call | solution.py:564
  280.4 9.9 %product.8.refs_0_ = f32[512,1536]{1,0:T(8,128)} custom-call(bf16[1024,3072]{1,0:T(8,128)(2,1)} %get-tuple-element.141.left_ref.refs_1_, bf16[1536,6144]{1,0:T(8,128)(2,1)} %all-gather.5.cloned.1.call-done.wi_ref.wo_ref.right_ref), custom_call_target="tpu_custom_call" | custom-call | flops 1024 | bytes 1024 | tf_op jit(solution)/shard_map/product/pallas_call | solution.py:564
  291.5 16.9 %ffn_middle.3 = (bf16[1024,3072]{1,0:T(8,128)(2,1)}, bf16[1024,3072]{1,0:T(8,128)(2,1)}) custom-call(bf16[512,1536]{1,0:T(8,128)(2,1)} %copy-done.13, bf16[512,1536]{1,0:T(8,128)(2,1)} %copy-done.12, bf16[1536,6144]{1,0:T(8,128)(2,1)} %all-gather.5.cloned.1.call-done.wi_ref.wo_ref.right_ref, ...), custom_call_target="tpu_custom_call", output_to_operand_aliasing={{0}: (4, {}), {1}: (5, {})} | custom-call | flops 1024 | bytes 1024 | tf_op jit(solution)/shard_map/ffn_middle/pallas_call | solution.py:893
  308.3 9.4 %product.9 = bf16[512,1536]{1,0:T(8,128)(2,1)} custom-call(bf16[1024,3072]{1,0:T(8,128)(2,1)} %get-tuple-element.144.left_ref.right_ref, bf16[1536,6144]{1,0:T(8,128)(2,1)} %all-gather.5.cloned.1.call-done.wi_ref.wo_ref.right_ref), custom_call_target="tpu_custom_call" | custom-call | flops 1024 | bytes 1024 | tf_op jit(solution)/shard_map/product/pallas_call | solution.py:564
  318.8 15.3 %convolution_convert_fusion = bf16[1536,3072]{1,0:T(8,128)(2,1)} fusion(bf16[1024,1536]{1,0:T(8,128)(2,1)} %constant_dynamic-update-slice_fusion, bf16[1024,3072]{1,0:T(8,128)(2,1)} %get-tuple-element.163.left_ref), kind=kOutput, calls=%fused_computation | convolution fusion | flops 9668395008 | bytes 18874368 | tf_op jit(solution)/shard_map/dot_general | solution.py:315
  337.9 16.1 %weight_halves.10 = (bf16[8,96,3072]{2,1,0:T(8,128)(2,1)}, bf16[8,96,3072]{2,1,0:T(8,128)(2,1)}) custom-call(s32[1]{0:T(128)} %bitcast.side_ref, bf16[1024,1536]{1,0:T(8,128)(2,1)} %pad_maximum_fusion.1.left_ref, bf16[1024,3072]{1,0:T(8,128)(2,1)} %get-tuple-element.144.left_ref.right_ref), custom_call_target="tpu_custom_call" | custom-call | flops 1024 | bytes 1024 | tf_op jit(solution)/shard_map/weight_halves/pallas_call | solution.py:343
  354.0 7.3 %norm_back.3 = (f32[512,1536]{1,0:T(8,128)}, bf16[512,1536]{1,0:T(8,128)(2,1)}, f32[8,1536]{1,0:T(8,128)}) custom-call(f32[512,1536]{1,0:T(8,128)} %copy-done.2, f32[1,1536]{1,0:T(1,128)} %get-tuple-element.280.gain_ref, bf16[512,1536]{1,0:T(8,128)(2,1)} %base_ref.1, f32[512,1536]{1,0:T(8,128)} %product.8.refs_0_, ...), custom_call_target="tpu_custom_call" | custom-call | flops 999999986991104 | bytes 1024 | tf_op jit(solution)/shard_map/norm_back/pallas_call | solution.py:510
  373.5 7.4 %cross_attend_back.1 = (bf16[512,1536]{1,0:T(8,128)(2,1)}, f32[64,1536]{1,0:T(8,128)}, f32[64,1536]{1,0:T(8,128)}) custom-call(bf16[512,1536]{1,0:T(8,128)(2,1)} %fusion.23.q_ref, bf16[64,1536]{1,0:T(8,128)(2,1)} %get-tuple-element.286.k_ref, bf16[64,1536]{1,0:T(8,128)(2,1)} %get-tuple-element.287.v_ref, ...), custom_call_target="tpu_custom_call" | custom-call | flops 1024 | bytes 1024 | tf_op jit(solution)/shard_map/cross_attend_back/pallas_call | solution.py:850
  382.7 6.8 product.11.refs_0_
  389.5 6.9 norm_back.4
  399.8 9.6 %product.12 = bf16[512,1536]{1,0:T(8,128)(2,1)} custom-call(bf16[1024,3072]{1,0:T(8,128)(2,1)} %get-tuple-element.163.left_ref, bf16[1536,6144]{1,0:T(8,128)(2,1)} %all-gather.5.cloned.1.call-done.wi_ref.wo_ref.right_ref), custom_call_target="tpu_custom_call" | custom-call | flops 1024 | bytes 1024 | tf_op jit(solution)/shard_map/product/pallas_call | solution.py:564
  429.1 8.5 %collective-permute-done.9 = bf16[64,1536]{1,0:T(8,128)(2,1)S(1)} collective-permute-done((bf16[64,1536]{1,0:T(8,128)(2,1)S(1)}, bf16[64,1536]{1,0:T(8,128)(2,1)S(1)}, u32[]{:S(2)}, u32[]{:S(2)}) %collective-permute-start.9) | collective-permute-done | bytes 196640 | tf_op jit(solution)/shard_map/ppermute | solution.py:964
  475.5 20.1 %self_attend_back.2.right_ref.refs_0_ = bf16[1024,1152]{1,0:T(8,128)(2,1)} custom-call(s32[1]{0:T(128)} %bitcast.4.t_ref, bf16[1024,2304]{1,0:T(8,128)(2,1)} %fusion.8.q_ref.k_ref.v_ref, bf16[1024,2304]{1,0:T(8,128)(2,1)} %fusion.8.q_ref.k_ref.v_ref, bf16[1024,2304]{1,0:T(8,128)(2,1)} %fusion.8.q_ref.k_ref.v_ref, ...), custom_call_target="tpu_custom_call" | custom-call | flops 20000000000 | bytes 1024 | tf_op jit(solution)/shard_map/self_attend_back/pallas_call | solution.py:740
  495.5 9.2 %weight_halves.17 = (bf16[8,96,1152]{2,1,0:T(8,128)(2,1)}, bf16[8,96,1152]{2,1,0:T(8,128)(2,1)}) custom-call(s32[1]{0:T(128)} %bitcast.side_ref, bf16[1024,1536]{1,0:T(8,128)(2,1)} %fusion.7.left_ref, bf16[1024,1152]{1,0:T(8,128)(2,1)} %self_attend_back.2.right_ref.refs_0_), custom_call_target="tpu_custom_call" | custom-call | flops 1024 | bytes 1024 | tf_op jit(solution)/shard_map/weight_halves/pallas_call | solution.py:343
  504.8 6.7 weight_halves.18
  516.1 6.7 collective-permute-done.17.refs_2_
  547.8 20.0 %self_attend_back.3.right_ref.refs_1_ = bf16[1024,1152]{1,0:T(8,128)(2,1)} custom-call(s32[1]{0:T(128)} %bitcast.4.t_ref, bf16[1024,2304]{1,0:T(8,128)(2,1)} %fusion.8.q_ref.k_ref.v_ref, bf16[1024,2304]{1,0:T(8,128)(2,1)} %fusion.8.q_ref.k_ref.v_ref, bf16[1024,2304]{1,0:T(8,128)(2,1)} %fusion.8.q_ref.k_ref.v_ref, ...), custom_call_target="tpu_custom_call" | custom-call | flops 20000000000 | bytes 1024 | tf_op jit(solution)/shard_map/self_attend_back/pallas_call | solution.py:740
  567.8 9.3 %weight_halves.19 = (bf16[8,96,1152]{2,1,0:T(8,128)(2,1)}, bf16[8,96,1152]{2,1,0:T(8,128)(2,1)}) custom-call(s32[1]{0:T(128)} %bitcast.side_ref, bf16[1024,1536]{1,0:T(8,128)(2,1)} %fusion.7.left_ref, bf16[1024,1152]{1,0:T(8,128)(2,1)} %self_attend_back.3.right_ref.refs_1_), custom_call_target="tpu_custom_call" | custom-call | flops 1024 | bytes 1024 | tf_op jit(solution)/shard_map/weight_halves/pallas_call | solution.py:343
  581.2 17.8 %collective-permute-done.25.refs_1_ = bf16[4,96,1920]{2,1,0:T(8,128)(2,1)S(1)} collective-permute-done((bf16[4,96,1920]{2,1,0:T(8,128)(2,1)}, bf16[4,96,1920]{2,1,0:T(8,128)(2,1)S(1)}, u32[]{:S(2)}, u32[]{:S(2)}) %collective-permute-start.25) | collective-permute-done | bytes 1474592 | tf_op jit(solution)/shard_map/ppermute | solution.py:972
  603.4 8.2 %joint_product.2.refs_0_ = bf16[512,1536]{1,0:T(8,128)(2,1)} custom-call(bf16[1024,1152]{1,0:T(8,128)(2,1)} %self_attend_back.2.right_ref.refs_0_, bf16[1024,1152]{1,0:T(8,128)(2,1)} %self_attend_back.3.right_ref.refs_1_, bf16[1536,7680]{1,0:T(8,128)(2,1)} %all-gather.3.cloned.1.call-done.right_ref.refs_2_), custom_call_target="tpu_custom_call" | custom-call | flops 999999986991104 | bytes 1024 | tf_op jit(solution)/shard_map/joint_product/pallas_call | solution.py:537
  626.6 8.5 %joint_product.3.refs_0_ = f32[512,1536]{1,0:T(8,128)} custom-call(bf16[1024,1152]{1,0:T(8,128)(2,1)} %self_attend_back.2.right_ref.refs_0_, bf16[1024,1152]{1,0:T(8,128)(2,1)} %self_attend_back.3.right_ref.refs_1_, bf16[1536,7680]{1,0:T(8,128)(2,1)} %all-gather.3.cloned.1.call-done.right_ref.refs_2_), custom_call_target="tpu_custom_call" | custom-call | flops 1024 | bytes 1024 | tf_op jit(solution)/shard_map/joint_product/pallas_call | solution.py:537
  635.1 8.5 %collective-permute-done.28.refs_1_ = bf16[2,96,1920]{2,1,0:T(8,128)(2,1)} collective-permute-done((bf16[2,96,1920]{2,1,0:T(8,128)(2,1)}, bf16[2,96,1920]{2,1,0:T(8,128)(2,1)}, u32[]{:S(2)}, u32[]{:S(2)}) %collective-permute-start.28) | collective-permute-done | bytes 737312 | tf_op jit(solution)/shard_map/ppermute | solution.py:972
  684.4 6.8 norm_back.5
  (261 shorter events, 238.0 us)
Async XLA Ops:
  7.2 137.3 %all-gather.3.cloned.1.call-start = ((), (), s32[]{:S(2)}) async-start(), calls=%async_computation.2 | async-start | bytes 25067520 | tf_op jit(solution)/shard_map/all_gather | solution.py:967
  21.7 232.0 %all-gather.5.cloned.1.call-start = ((), (), s32[]{:S(2)}) async-start(), calls=%async_computation.3 | async-start | bytes 20054016 | tf_op jit(solution)/shard_map/all_gather | solution.py:967
  26.8 447.8 %reduce-scatter.3.cloned.1.call-start = ((), (), s32[]{:S(2)}) async-start(), calls=%async_computation.4 | async-start | bytes 10027008 | tf_op jit(solution)/shard_map/reduce_scatter | solution.py:1049
  26.9 35.6 %collective-permute-start.1 = (bf16[512,1536]{1,0:T(8,128)(2,1)S(1)}, bf16[512,1536]{1,0:T(8,128)(2,1)S(1)}, u32[]{:S(2)}, u32[]{:S(2)}) collective-permute-start(bf16[512,1536]{1,0:T(8,128)(2,1)S(1)} %copy-done), channel_id=1, source_target_pairs={{0,1},{1,0},{2,3},{3,2},{4,5},{5,4},{6,7},{7,6},{8,9},{9,8},{10,11... | collective-permute-start | bytes 4718600 | tf_op jit(solution)/shard_map/ppermute | solution.py:964
  62.5 34.8 %collective-permute-start.2 = (bf16[512,1536]{1,0:T(8,128)(2,1)S(1)}, bf16[512,1536]{1,0:T(8,128)(2,1)S(1)}, u32[]{:S(2)}, u32[]{:S(2)}) collective-permute-start(bf16[512,1536]{1,0:T(8,128)(2,1)S(1)} %copy-done.11), channel_id=1, source_target_pairs={{0,1},{1,0},{2,3},{3,2},{4,5},{5,4},{6,7},{7,6},{8,9},{9,8},{10,11... | collective-permute-start | bytes 4718600 | tf_op jit(solution)/shard_map/ppermute | solution.py:964
  184.6 41.5 %collective-permute-start.3 = (bf16[512,1536]{1,0:T(8,128)(2,1)S(1)}, bf16[512,1536]{1,0:T(8,128)(2,1)S(1)}, u32[]{:S(2)}, u32[]{:S(2)}) collective-permute-start(bf16[512,1536]{1,0:T(8,128)(2,1)S(1)} %convolution_convert_fusion.1), channel_id=1, source_target_pairs={{0,1},{1,0},{2,3},{3,2},{4,5},{5,4},{6,7},{7,6},{8,9},{9,8},{10,11... | collective-permute-start | bytes 4718600 | tf_op jit(solution)/shard_map/ppermute | solution.py:964
  186.2 39.2 %collective-permute-start.4 = (bf16[64,1536]{1,0:T(8,128)(2,1)S(1)}, bf16[64,1536]{1,0:T(8,128)(2,1)S(1)}, u32[]{:S(2)}, u32[]{:S(2)}) collective-permute-start(bf16[64,1536]{1,0:T(8,128)(2,1)S(1)} %fusion.32), channel_id=1, source_target_pairs={{0,1},{1,0},{2,3},{3,2},{4,5},{5,4},{6,7},{7,6},{8,9},{9,8},{10,11... | collective-permute-start | bytes 589832 | tf_op jit(solution)/shard_map/ppermute | solution.py:964
  252.3 38.1 %collective-permute-start.5 = (bf16[512,1536]{1,0:T(8,128)(2,1)S(1)}, bf16[512,1536]{1,0:T(8,128)(2,1)S(1)}, u32[]{:S(2)}, u32[]{:S(2)}) collective-permute-start(bf16[512,1536]{1,0:T(8,128)(2,1)S(1)} %add_convert_fusion.1.n_ref), channel_id=1, source_target_pairs={{0,1},{1,0},{2,3},{3,2},{4,5},{5,4},{6,7},{7,6},{8,9},{9,8},{10,11... | collective-permute-start | bytes 4718600 | tf_op jit(solution)/shard_map/ppermute | solution.py:964
  317.7 36.3 %collective-permute-start.6 = (bf16[512,1536]{1,0:T(8,128)(2,1)}, bf16[512,1536]{1,0:T(8,128)(2,1)}, u32[]{:S(2)}, u32[]{:S(2)}) collective-permute-start(bf16[512,1536]{1,0:T(8,128)(2,1)} %product.9), channel_id=1, source_target_pairs={{0,1},{1,0},{2,3},{3,2},{4,5},{5,4},{6,7},{7,6},{8,9},{9,8},{10,11... | collective-permute-start | bytes 4718600 | tf_op jit(solution)/shard_map/ppermute | solution.py:964
  334.2 320.7 %reduce-scatter.5.cloned.1.call-start = ((), (), s32[]{:S(2)}) async-start(), calls=%async_computation.5 | async-start | bytes 2949120 | tf_op jit(solution)/shard_map/reduce_scatter | solution.py:976
  396.4 49.2 %collective-permute-start.8 = (bf16[512,1536]{1,0:T(8,128)(2,1)}, bf16[512,1536]{1,0:T(8,128)(2,1)S(1)}, u32[]{:S(2)}, u32[]{:S(2)}) collective-permute-start(bf16[512,1536]{1,0:T(8,128)(2,1)} %get-tuple-element.162), channel_id=1, source_target_pairs={{0,1},{1,0},{2,3},{3,2},{4,5},{5,4},{6,7},{7,6},{8,9},{9,8},{10,11... | collective-permute-start | bytes 4718600 | tf_op jit(solution)/shard_map/ppermute | solution.py:964
  397.6 72.3 %collective-permute-start.12 = (bf16[4,96,3072]{2,1,0:T(8,128)(2,1)}, bf16[4,96,3072]{2,1,0:T(8,128)(2,1)}, u32[]{:S(2)}, u32[]{:S(2)}) collective-permute-start(bf16[4,96,3072]{2,1,0:T(8,128)(2,1)} %get-tuple-element.155), channel_id=1, source_target_pairs={{0,4},{2,6},{4,0},{6,2},{8,12},{10,14},{12,8},{14,10},{16,20},{18,... | collective-permute-start | bytes 7077896 | tf_op jit(solution)/shard_map/ppermute | solution.py:972
  398.8 38.8 %collective-permute-start.9 = (bf16[64,1536]{1,0:T(8,128)(2,1)S(1)}, bf16[64,1536]{1,0:T(8,128)(2,1)S(1)}, u32[]{:S(2)}, u32[]{:S(2)}) collective-permute-start(bf16[64,1536]{1,0:T(8,128)(2,1)S(1)} %pad_maximum_fusion.8), channel_id=1, source_target_pairs={{0,1},{1,0},{2,3},{3,2},{4,5},{5,4},{6,7},{7,6},{8,9},{9,8},{10,11... | collective-permute-start | bytes 589832 | tf_op jit(solution)/shard_map/ppermute | solution.py:964
  419.0 39.3 %collective-permute-start.10 = (bf16[8,96,768]{2,1,0:T(8,128)(2,1)}, bf16[8,96,768]{2,1,0:T(8,128)(2,1)}, u32[]{:S(2)}, u32[]{:S(2)}) collective-permute-start(bf16[8,96,768]{2,1,0:T(8,128)(2,1)} %get-tuple-element.167), channel_id=1, source_target_pairs={{0,2},{2,0},{4,6},{6,4},{8,10},{10,8},{12,14},{14,12},{16,18},{18,... | collective-permute-start | bytes 3538952 | tf_op jit(solution)/shard_map/ppermute | solution.py:972
  428.6 33.1 %collective-permute-start.11 = (bf16[8,96,768]{2,1,0:T(8,128)(2,1)}, bf16[8,96,768]{2,1,0:T(8,128)(2,1)}, u32[]{:S(2)}, u32[]{:S(2)}) collective-permute-start(bf16[8,96,768]{2,1,0:T(8,128)(2,1)} %get-tuple-element.171), channel_id=1, source_target_pairs={{0,2},{2,0},{4,6},{6,4},{8,10},{10,8},{12,14},{14,12},{16,18},{18,... | collective-permute-start | bytes 3538952 | tf_op jit(solution)/shard_map/ppermute | solution.py:972
  441.8 32.8 %collective-permute-start.14 = (bf16[8,96,768]{2,1,0:T(8,128)(2,1)}, bf16[8,96,768]{2,1,0:T(8,128)(2,1)}, u32[]{:S(2)}, u32[]{:S(2)}) collective-permute-start(bf16[8,96,768]{2,1,0:T(8,128)(2,1)} %get-tuple-element.174), channel_id=1, source_target_pairs={{0,2},{2,0},{4,6},{6,4},{8,10},{10,8},{12,14},{14,12},{16,18},{18,... | collective-permute-start | bytes 3538952 | tf_op jit(solution)/shard_map/ppermute | solution.py:972
  445.6 29.9 %collective-permute-start.15 = (bf16[8,96,768]{2,1,0:T(8,128)(2,1)}, bf16[8,96,768]{2,1,0:T(8,128)(2,1)}, u32[]{:S(2)}, u32[]{:S(2)}) collective-permute-start(bf16[8,96,768]{2,1,0:T(8,128)(2,1)} %get-tuple-element.176), channel_id=1, source_target_pairs={{0,2},{2,0},{4,6},{6,4},{8,10},{10,8},{12,14},{14,12},{16,18},{18,... | collective-permute-start | bytes 3538952 | tf_op jit(solution)/shard_map/ppermute | solution.py:972
  458.3 56.7 %collective-permute-start.16 = (bf16[8,96,768]{2,1,0:T(8,128)(2,1)}, bf16[8,96,768]{2,1,0:T(8,128)(2,1)S(1)}, u32[]{:S(2)}, u32[]{:S(2)}) collective-permute-start(bf16[8,96,768]{2,1,0:T(8,128)(2,1)} %get-tuple-element.165), channel_id=1, source_target_pairs={{0,2},{2,0},{4,6},{6,4},{8,10},{10,8},{12,14},{14,12},{16,18},{18,... | collective-permute-start | bytes 3538952 | tf_op jit(solution)/shard_map/ppermute | solution.py:972
  461.6 54.0 %collective-permute-start.18 = (bf16[8,96,768]{2,1,0:T(8,128)(2,1)}, bf16[8,96,768]{2,1,0:T(8,128)(2,1)S(1)}, u32[]{:S(2)}, u32[]{:S(2)}) collective-permute-start(bf16[8,96,768]{2,1,0:T(8,128)(2,1)} %get-tuple-element.169), channel_id=1, source_target_pairs={{0,2},{2,0},{4,6},{6,4},{8,10},{10,8},{12,14},{14,12},{16,18},{18,... | collective-permute-start | bytes 3538952 | tf_op jit(solution)/shard_map/ppermute | solution.py:972
  469.8 45.8 %collective-permute-start.19 = (bf16[8,96,768]{2,1,0:T(8,128)(2,1)}, bf16[8,96,768]{2,1,0:T(8,128)(2,1)}, u32[]{:S(2)}, u32[]{:S(2)}) collective-permute-start(bf16[8,96,768]{2,1,0:T(8,128)(2,1)} %totals.5), channel_id=1, source_target_pairs={{0,1},{1,0},{2,3},{3,2},{4,5},{5,4},{6,7},{7,6},{8,9},{9,8},{10,11... | collective-permute-start | bytes 3538952 | tf_op jit(solution)/shard_map/ppermute | solution.py:964
  474.6 48.3 %collective-permute-start.17 = (bf16[8,96,768]{2,1,0:T(8,128)(2,1)S(1)}, bf16[8,96,768]{2,1,0:T(8,128)(2,1)}, u32[]{:S(2)}, u32[]{:S(2)}) collective-permute-start(bf16[8,96,768]{2,1,0:T(8,128)(2,1)S(1)} %copy-done.22), channel_id=1, source_target_pairs={{0,1},{1,0},{2,3},{3,2},{4,5},{5,4},{6,7},{7,6},{8,9},{9,8},{10,11... | collective-permute-start | bytes 3538952 | tf_op jit(solution)/shard_map/ppermute | solution.py:964
  475.5 51.9 %collective-permute-start.20 = (bf16[2,96,3072]{2,1,0:T(8,128)(2,1)}, bf16[2,96,3072]{2,1,0:T(8,128)(2,1)}, u32[]{:S(2)}, u32[]{:S(2)}) collective-permute-start(bf16[2,96,3072]{2,1,0:T(8,128)(2,1)} %get-tuple-element.185), channel_id=1, source_target_pairs={{0,8},{2,10},{4,12},{6,14},{8,0},{10,2},{12,4},{14,6},{16,24},{18,... | collective-permute-start | bytes 3538952 | tf_op jit(solution)/shard_map/ppermute | solution.py:972
  515.0 29.2 %collective-permute-start.23 = (bf16[4,96,1536]{2,1,0:T(8,128)(2,1)}, bf16[4,96,1536]{2,1,0:T(8,128)(2,1)}, u32[]{:S(2)}, u32[]{:S(2)}) collective-permute-start(bf16[4,96,1536]{2,1,0:T(8,128)(2,1)} %get-tuple-element.202), channel_id=1, source_target_pairs={{0,4},{2,6},{4,0},{6,2},{8,12},{10,14},{12,8},{14,10},{16,20},{18,... | collective-permute-start | bytes 3538952 | tf_op jit(solution)/shard_map/ppermute | solution.py:972
  530.3 46.8 %collective-permute-start.24 = (bf16[4,96,1536]{2,1,0:T(8,128)(2,1)}, bf16[4,96,1536]{2,1,0:T(8,128)(2,1)S(1)}, u32[]{:S(2)}, u32[]{:S(2)}) collective-permute-start(bf16[4,96,1536]{2,1,0:T(8,128)(2,1)} %get-tuple-element.205), channel_id=1, source_target_pairs={{0,4},{2,6},{4,0},{6,2},{8,12},{10,14},{12,8},{14,10},{16,20},{18,... | collective-permute-start | bytes 3538952 | tf_op jit(solution)/shard_map/ppermute | solution.py:972
  530.9 130.7 %collective-permute-start.34 = (bf16[1,96,3072]{2,1,0:T(8,128)(2,1)}, bf16[1,96,3072]{2,1,0:T(8,128)(2,1)}, u32[]{:S(2)}, u32[]{:S(2)}) collective-permute-start(bf16[1,96,3072]{2,1,0:T(8,128)(2,1)} %get-tuple-element.207), channel_id=1, source_target_pairs={{0,16},{2,18},{4,20},{6,22},{8,24},{10,26},{12,28},{14,30},{16,0},... | collective-permute-start | bytes 1769480 | tf_op jit(solution)/shard_map/ppermute | solution.py:972
  537.0 78.1 %collective-permute-start.31 = (bf16[64,768]{1,0:T(8,128)(2,1)}, bf16[64,768]{1,0:T(8,128)(2,1)}, u32[]{:S(2)}, u32[]{:S(2)}) collective-permute-start(bf16[64,768]{1,0:T(8,128)(2,1)} %constant_dynamic-slice_fusion), channel_id=1, source_target_pairs={{0,1},{1,0},{2,3},{3,2},{4,5},{5,4},{6,7},{7,6},{8,9},{9,8},{10,11... | collective-permute-start | bytes 294920 | tf_op jit(solution)/shard_map/ppermute | solution.py:964
  538.7 76.5 %collective-permute-start.13 = (bf16[512,1536]{1,0:T(8,128)(2,1)}, bf16[512,1536]{1,0:T(8,128)(2,1)}, u32[]{:S(2)}, u32[]{:S(2)}) collective-permute-start(bf16[512,1536]{1,0:T(8,128)(2,1)} %product.12), channel_id=1, source_target_pairs={{0,1},{1,0},{2,3},{3,2},{4,5},{5,4},{6,7},{7,6},{8,9},{9,8},{10,11... | collective-permute-start | bytes 4718600 | tf_op jit(solution)/shard_map/ppermute | solution.py:964
  544.2 54.8 %collective-permute-start.25 = (bf16[4,96,1920]{2,1,0:T(8,128)(2,1)}, bf16[4,96,1920]{2,1,0:T(8,128)(2,1)S(1)}, u32[]{:S(2)}, u32[]{:S(2)}) collective-permute-start(bf16[4,96,1920]{2,1,0:T(8,128)(2,1)} %get-tuple-element.210), channel_id=1, source_target_pairs={{0,4},{2,6},{4,0},{6,2},{8,12},{10,14},{12,8},{14,10},{16,20},{18,... | collective-permute-start | bytes 4423688 | tf_op jit(solution)/shard_map/ppermute | solution.py:972
  577.1 39.7 %collective-permute-start.26 = (bf16[8,96,1152]{2,1,0:T(8,128)(2,1)}, bf16[8,96,1152]{2,1,0:T(8,128)(2,1)}, u32[]{:S(2)}, u32[]{:S(2)}) collective-permute-start(bf16[8,96,1152]{2,1,0:T(8,128)(2,1)} %get-tuple-element.214), channel_id=1, source_target_pairs={{0,2},{2,0},{4,6},{6,4},{8,10},{10,8},{12,14},{14,12},{16,18},{18,... | collective-permute-start | bytes 5308424 | tf_op jit(solution)/shard_map/ppermute | solution.py:972
  611.6 48.5 %collective-permute-start.27 = (bf16[512,1536]{1,0:T(8,128)(2,1)}, bf16[512,1536]{1,0:T(8,128)(2,1)}, u32[]{:S(2)}, u32[]{:S(2)}) collective-permute-start(bf16[512,1536]{1,0:T(8,128)(2,1)} %joint_product.2.refs_0_), channel_id=1, source_target_pairs={{0,1},{1,0},{2,3},{3,2},{4,5},{5,4},{6,7},{7,6},{8,9},{9,8},{10,11... | collective-permute-start | bytes 4718600 | tf_op jit(solution)/shard_map/ppermute | solution.py:964
  615.2 28.4 %collective-permute-start.28 = (bf16[2,96,1920]{2,1,0:T(8,128)(2,1)}, bf16[2,96,1920]{2,1,0:T(8,128)(2,1)}, u32[]{:S(2)}, u32[]{:S(2)}) collective-permute-start(bf16[2,96,1920]{2,1,0:T(8,128)(2,1)} %get-tuple-element.222), channel_id=1, source_target_pairs={{0,8},{2,10},{4,12},{6,14},{8,0},{10,2},{12,4},{14,6},{16,24},{18,... | collective-permute-start | bytes 2211848 | tf_op jit(solution)/shard_map/ppermute | solution.py:972
  619.8 32.5 %collective-permute-start.29 = (bf16[4,96,1152]{2,1,0:T(8,128)(2,1)}, bf16[4,96,1152]{2,1,0:T(8,128)(2,1)}, u32[]{:S(2)}, u32[]{:S(2)}) collective-permute-start(bf16[4,96,1152]{2,1,0:T(8,128)(2,1)} %get-tuple-element.225), channel_id=1, source_target_pairs={{0,4},{2,6},{4,0},{6,2},{8,12},{10,14},{12,8},{14,10},{16,20},{18,... | collective-permute-start | bytes 2654216 | tf_op jit(solution)/shard_map/ppermute | solution.py:972
  (56 other events, 552.0 us)
Sparse Core Ops, SparseCore 0:
  21.9 122.5 all-gather.2
  146.7 98.8 all-gather.4
  334.3 127.6 reduce-scatter.2
  581.4 57.3 reduce-scatter.4

commit v4 on v3

--- a/solution.py
+++ b/solution.py
@@ -370,7 +370,7 @@
     return count
 
 
-def fold_kernel(side_ref, *refs, counts):
+def fold_kernel(side_ref, *refs, counts, inner):
     send_ref, keep_ref = refs[-2:]
     side = side_ref[0]
     first, at = 0, 0
@@ -379,20 +379,21 @@
         size = terms[0].shape[2]
         for pair in range(keep_ref.shape[0]):
             for out_ref, bit in ((send_ref, 1 - side), (keep_ref, side)):
-                out_ref[pair, :, first : first + size] = added(terms, 2 * pair + bit)
+                row = (2 * (pair // inner) + bit) * inner + pair % inner
+                out_ref[pair, :, first : first + size] = added(terms, row)
         first, at = first + size, at + count
 
 
-def fold(side, *groups, cost=None):
+def fold(side, *groups, cost=None, inner=1):
     count, shard = groups[0][0].shape[0] // 2, groups[0][0].shape[1]
     sizes = [terms[0].shape[2] for terms in groups]
     row = sum(4 * shard * size * (len(terms) + 1) for size, terms in zip(sizes, groups))
-    per = pairs_per_step(count, row)
+    per = count if inner > 1 else pairs_per_step(count, row)
     shape = jax.ShapeDtypeStruct((count, shard, sum(sizes)), BF)
     spec = lambda size: pl.BlockSpec((2 * per, shard, size), lambda j, s: (j, 0, 0))
     part = pl.BlockSpec((per, shard, sum(sizes)), lambda j, s: (j, 0, 0))
     return pl.pallas_call(
-        partial(fold_kernel, counts=[len(terms) for terms in groups]),
+        partial(fold_kernel, counts=[len(terms) for terms in groups], inner=inner),
         out_shape=(shape, shape),
         grid_spec=pltpu.PrefetchScalarGridSpec(
             num_scalar_prefetch=1,
@@ -730,7 +731,7 @@
         out_ref[...] = dvb[...]
 
 
-def self_backward(t, qkv, mixed, d_mixed, lse, part):
+def self_backward(t, qkv, mixed, d_mixed, lse, part, cost):
     length, width = qkv.shape[0], qkv.shape[1] // CUTS
     pairs = width // (3 * PAIR)
     first = part * pairs
@@ -757,7 +758,7 @@
             + [pltpu.VMEM((length, PAIR), BF)] * 2,
         ),
         name="self_attend_back",
-        cost_estimate=MIDDLE,
+        cost_estimate=cost,
     )(t, qkv, qkv, qkv, mixed, d_mixed, lse)
 
 
@@ -1073,7 +1074,8 @@
     d_text_peer = peer(d_text_send)
     back2 = product(after(d_query2, d_text_send), first, NT, F32, first=6 * half)
     grad1, g1, sums2 = norm_back_rows(state1, norm_gains[1], grad2, [back2])
-    g1_peer = peer(g1)
+    d_text = (d_text_keep + after(d_text_peer, g1).astype(F32)).astype(BF)
+    g1_peer = peer(after(g1, d_text))
 
     out_part = product(after(active, g1), second, NT, BF, row=1, rows=rows, first=hidden)
     last = out_part
@@ -1084,16 +1086,14 @@
 
     co_own, co_away = two(g2, mixed2)
     cq_own, cq_away = two(normed2, d_query2)
-    d_text = (d_text_keep + after(d_text_peer, last).astype(F32)).astype(BF)
-    kv = two(text, d_text)
-    grads1 = jnp.concatenate([g1, after(g1_peer, last)], axis=0)
-    d_mixed1 = product(grads1, first, NN, BF, first=3 * half, size=half)
-    co_send = totals((after(co_away[0], d_mixed1), co_away[1]))
+    co_send = totals((after(co_away[0], last), co_away[1]))
     co_got = peer(co_send)
     cq_send = totals((after(cq_away[0], co_send), cq_away[1]))
     cq_got = peer(cq_send)
-    inner = fold(side_refs[2], (after(inner[1], cq_send), inner_got))
-    found0 = self_backward(t_ref, qkv, mixed1, after(d_mixed1, inner[0], outer_sum), lse1, 0)
+    last = cq_send
+    grads1 = jnp.concatenate([g1, after(g1_peer, last)], axis=0)
+    d_mixed1 = product(grads1, first, NN, BF, first=3 * half, size=half)
+    found0 = self_backward(t_ref, qkv, mixed1, d_mixed1, lse1, 0, LIGHT)
     text_terms = mm(after(d_text, found0), w_text, NT).astype(BF)
     text_keep, text_send = (
         lax.dynamic_slice(
@@ -1104,37 +1104,42 @@
 
     text_got = peer(text_send)
     out_away = peer(after(out_part, found0))
-    last = found0
+    inner = fold(side_refs[2], (after(inner[1], found0, outer_sum), inner_got))
+    last = inner[0]
     qkv0 = weight_core(normed1, found0)
     qkv0_got = swap(qkv0[0], 0)
     so = weight_core(grads1, mixed1)
     so_got = swap(so[0], 0)
-    kv = fold(side_refs[1], *[(after(keep, last), got) for keep, got in kv])
-    kv_got = swap(kv[0], 1)
+    kv = two(text, d_text)
     cross = fold(
         side_refs[1],
-        (after(co_own[0], kv[0]), co_own[1], co_got),
+        (after(co_own[0], last), co_own[1], co_got),
         (cq_own[0], cq_own[1], cq_got),
     )
     cross_got = swap(cross[0], 1)
     inner_first = after(inner[1], cross[0]), swap(inner[0], 2)
     inner = fold(side_refs[3], inner_first, cost=HEAVY)
-    most = fold(side_refs[1], (after(qkv0[1], inner[0]), qkv0_got), (so[1], so_got))
-    most_got = swap(most[0], 1)
-    kv = totals((after(kv[1], most[0]), kv_got))
-    found1 = self_backward(t_ref, qkv, mixed1, after(d_mixed1, kv), lse1, 1)
+    most = fold(
+        side_refs[2], (after(qkv0[1], inner[0]), qkv0_got), (so[1], so_got), inner=2
+    )
+    most_got = swap(most[0], 2)
+    kv = fold(side_refs[1], *[(after(keep, most[0]), got) for keep, got in kv])
+    kv_got = swap(kv[0], 1)
+    found1 = self_backward(t_ref, qkv, mixed1, after(d_mixed1, kv[0]), lse1, 1, MIDDLE)
     last = found1
     qkv1 = weight_core(normed1, found1)
     qkv1_got = swap(qkv1[0], 0)
-    cross = totals((after(cross[1], qkv1[0]), cross_got), (kv,))
+    cross = totals((after(cross[1], qkv1[0]), cross_got), (kv[1], kv_got))
     cross_sum = line_sum(cross)
-    most = fold(side_refs[2], (after(most[1], cross), most_got))
+    most = fold(side_refs[3], (after(most[1], cross), most_got), inner=2)
+    most_got = swap(most[0], 3)
     back1_part = joint_product([found0, after(found1, most[0])], first, BF, 1, rows, HEAVY)
     back1_away = peer(back1_part)
     qkv1 = fold(side_refs[1], (after(qkv1[1], back1_part), qkv1_got))
     qkv1_got = swap(qkv1[0], 1)
     back1_home = joint_product([found0, after(found1, qkv1[0])], first, F32, 0, rows, LIGHT)
-    most = line_step(*most, back1_home)
+    most = fold(side_refs[1], (after(most[1], back1_home), most_got))
+    most_got = swap(most[0], 1)
     sums0 = norm_sums(after(inputs_peer, most[0]), [back1_part])
     qkv1 = fold(side_refs[2], (after(qkv1[1], sums0), qkv1_got))
     sums1 = sums0 + norm_sums(after(inputs, qkv1[0], cross_sum), [back1_home])
@@ -1143,7 +1148,8 @@
         inputs, norm_gains[0], grad1, [back1_home, after(back1_away, qkv1[0])]
     )
     inner_sum = line_end(inner[0], after(inner[1], back1_home))
-    most_sum, qkv1_sum = line_end(*most), line_end(*qkv1)
+    most_sum = (most[1].astype(F32) + most_got.astype(F32)).reshape(shard, -1)
+    qkv1_sum = line_end(*qkv1)
     qkv0_sum, so_sum = most_sum[:, : 3 * part], most_sum[:, 3 * part :]
     output = (state2 + out_home + after(out_away, last).astype(F32)).astype(BF)
     text_grad = text_keep.astype(F32) + after(text_got, last).astype(F32)
@@ -1185,8 +1191,7 @@
     width = inputs.shape[1]
     return (
         sides == 2
-        and groups >= 16
-        and groups & (groups - 1) == 0
+        and groups == 16
         and text_states.shape[0] == groups
         and text_states.shape[1] == TEXT
         and inputs.shape[0] == groups * LEN

time: 716 us -> 747 us (1.043)
  waiting for transfers between devices: 208 us -> 241 us
    ppermute x21, waiting for transfers between devices: 38.6 us -> 84.5 us  [swap(): return lax.ppermute(send, 'dp', swaps[level])]
    ppermute x15, waiting for transfers between devices: 119 us -> 103 us  [peer(): return lax.ppermute(value, 'tensor', [(0, 1), (1, 0)])]
    unnamed x92 -> x84, local copies, waits for them, and re-layouts: 17.6 us -> 17.2 us
  transfers between devices with their start and end apart: 44 -> 44, of which waited for: 17 -> 12; matrix products, arithmetic and copies ran while one was open for 13% -> 13% of each run, Pallas kernels for 44% -> 41%
where the time goes in v4:
time: 747 us; the launch traced here: 735 us
  Pallas kernels  334 us (45%)
  waiting for transfers between devices  241 us (32%)
  matrix products  53.5 us (7%)
  starting transfers between devices  38 us (5%)
  local copies, waits for them, and re-layouts  27.8 us (4%)
  other arithmetic  26.7 us (4%)
  between operations  14.7 us (2%)
    ppermute x15, waiting for transfers between devices, peer(): return lax.ppermute(value, 'tensor', [(0, 1), (1, 0)])  103 us
    ppermute x21, waiting for transfers between devices, swap(): return lax.ppermute(send, 'dp', swaps[level])  84.5 us
    pallas_call x10, Pallas kernels, weight_halves(): pl.pallas_call(partial(weight_kernel, shard=shard), out_shape=(shape, sha...  67.3 us
    pallas_call x7, Pallas kernels, product(): pl.pallas_call(partial(product_kernel, dims=dims), grid=(size // tile,),...  57.8 us
    dot_general x8, matrix products, mm(): return lax.dot_general(left, right, dims, preferred_element_type=F32)  53.5 us
    all_gather x2, waiting for transfers between devices, gather(): return lax.all_gather(packed, 'dp', axis=0, tiled=True)  44.8 us
    pallas_call x2, Pallas kernels, self_backward(): pl.pallas_call(self_back_kernel, out_shape=jax.ShapeDtypeStruct((length,...  40.3 us
    pallas_call x11, Pallas kernels, fold(): pl.pallas_call(partial(fold_kernel, counts=[len(terms) for terms in group...  38.9 us
  transfers between devices with their start and end apart: 44, of which 12 were waited for; matrix products, arithmetic and copies ran while one was open for 13% of the time, Pallas kernels for 41%

profile of v4, /device:TPU:0, one launch (start us, length us, event | category | flops | bytes accessed | tf_op | source)
XLA Modules:
  0.0 735.4 jit_solution(7934518919521554249)
XLA Ops:
  30.6 31.9 %collective-permute-done.1.value_ref = bf16[512,1536]{1,0:T(8,128)(2,1)S(1)} collective-permute-done((bf16[512,1536]{1,0:T(8,128)(2,1)S(1)}, bf16[512,1536]{1,0:T(8,128)(2,1)S(1)}, u32[]{:S(2)}, u32[]{:S(2)}) %collective-permute-start.1) | collective-permute-done | bytes 1572896 | tf_op jit(solution)/shard_map/ppermute | solution.py:965
  70.3 27.0 %collective-permute-done.2.g_ref = bf16[512,1536]{1,0:T(8,128)(2,1)S(1)} collective-permute-done((bf16[512,1536]{1,0:T(8,128)(2,1)S(1)}, bf16[512,1536]{1,0:T(8,128)(2,1)S(1)}, u32[]{:S(2)}, u32[]{:S(2)}) %collective-permute-start.2) | collective-permute-done | bytes 1572896 | tf_op jit(solution)/shard_map/ppermute | solution.py:965
  99.7 44.8 %all-gather.3.cloned.1.call-done.right_ref.refs_2_ = bf16[1536,7680]{1,0:T(8,128)(2,1)} async-done(((bf16[96,7680]{1,0:T(8,128)(2,1)}), bf16[1536,7680]{1,0:T(8,128)(2,1)}) %all-gather.3.cloned.1.call-update) | async-done | bytes 23592976 | tf_op jit(solution)/shard_map/all_gather | solution.py:968
  147.9 12.1 %fusion.8.q_ref.k_ref.v_ref = bf16[1024,2304]{1,0:T(8,128)(2,1)} fusion(bf16[1024,1536]{1,0:T(8,128)(2,1)S(1)} %copy-done.3, bf16[1536,7680]{1,0:T(8,128)(2,1)} %all-gather.3.cloned.1.call-done.right_ref.refs_2_), kind=kOutput, calls=%fused_computation.11 | convolution fusion | flops 7250116608 | bytes 14942208 | tf_op jit(solution)/shard_map/dot_general | solution.py:315
  160.0 21.0 %self_attend.1 = (bf16[1024,768]{1,0:T(8,128)(2,1)}, f32[6,8,1024]{2,1,0:T(8,128)}) custom-call(s32[1]{0:T(128)} %bitcast.4.t_ref, bf16[1024,2304]{1,0:T(8,128)(2,1)} %fusion.8.q_ref.k_ref.v_ref, bf16[1024,2304]{1,0:T(8,128)(2,1)} %fusion.8.q_ref.k_ref.v_ref, bf16[1024,2304]{1,0:T(8,128)(2,1)} %fusion.8.q_ref.k_ref.v_ref), custom_call_target="tpu_custom_call" | custom-call | flops 1024 | bytes 1024 | tf_op jit(solution)/shard_map/self_attend/pallas_call | solution.py:650
  186.8 38.6 %collective-permute-done.4 = bf16[64,1536]{1,0:T(8,128)(2,1)S(1)} collective-permute-done((bf16[64,1536]{1,0:T(8,128)(2,1)S(1)}, bf16[64,1536]{1,0:T(8,128)(2,1)S(1)}, u32[]{:S(2)}, u32[]{:S(2)}) %collective-permute-start.4) | collective-permute-done | bytes 196640 | tf_op jit(solution)/shard_map/ppermute | solution.py:965
  231.9 6.7 fusion.23.q_ref
  238.6 6.8 cross_attend.1
  253.8 16.9 %ffn_middle.2 = (bf16[1024,3072]{1,0:T(8,128)(2,1)}, bf16[1024,3072]{1,0:T(8,128)(2,1)}) custom-call(bf16[512,1536]{1,0:T(8,128)(2,1)} %copy-done.8, bf16[512,1536]{1,0:T(8,128)(2,1)} %base_ref.1, bf16[1536,6144]{1,0:T(8,128)(2,1)} %all-gather.5.cloned.1.call-done.wi_ref.wo_ref.right_ref, bf16[1536,6144]{1,0:T(8,128)(2,1)} %all-gather.5.cloned.1.call-done.wi_ref.wo_ref.right_ref), custom_call_target="tpu_custom_call" | custom-call | flops 1024 | bytes 1024 | tf_op jit(solution)/shard_map/ffn_middle/pallas_call | solution.py:894
  270.7 9.8 %product.7 = f32[512,1536]{1,0:T(8,128)} custom-call(bf16[1024,3072]{1,0:T(8,128)(2,1)} %get-tuple-element.139.left_ref.refs_0_, bf16[1536,6144]{1,0:T(8,128)(2,1)} %all-gather.5.cloned.1.call-done.wi_ref.wo_ref.right_ref), custom_call_target="tpu_custom_call" | custom-call | flops 1024 | bytes 1024 | tf_op jit(solution)/shard_map/product/pallas_call | solution.py:565
  280.5 9.8 %product.8.refs_0_ = f32[512,1536]{1,0:T(8,128)} custom-call(bf16[1024,3072]{1,0:T(8,128)(2,1)} %get-tuple-element.140.left_ref.refs_1_, bf16[1536,6144]{1,0:T(8,128)(2,1)} %all-gather.5.cloned.1.call-done.wi_ref.wo_ref.right_ref), custom_call_target="tpu_custom_call" | custom-call | flops 1024 | bytes 1024 | tf_op jit(solution)/shard_map/product/pallas_call | solution.py:565
  291.5 16.9 %ffn_middle.3 = (bf16[1024,3072]{1,0:T(8,128)(2,1)}, bf16[1024,3072]{1,0:T(8,128)(2,1)}) custom-call(bf16[512,1536]{1,0:T(8,128)(2,1)} %copy-done.13, bf16[512,1536]{1,0:T(8,128)(2,1)} %copy-done.12, bf16[1536,6144]{1,0:T(8,128)(2,1)} %all-gather.5.cloned.1.call-done.wi_ref.wo_ref.right_ref, ...), custom_call_target="tpu_custom_call", output_to_operand_aliasing={{0}: (4, {}), {1}: (5, {})} | custom-call | flops 1024 | bytes 1024 | tf_op jit(solution)/shard_map/ffn_middle/pallas_call | solution.py:894
  308.4 9.4 %product.9 = bf16[512,1536]{1,0:T(8,128)(2,1)} custom-call(bf16[1024,3072]{1,0:T(8,128)(2,1)} %get-tuple-element.143.left_ref.right_ref, bf16[1536,6144]{1,0:T(8,128)(2,1)} %all-gather.5.cloned.1.call-done.wi_ref.wo_ref.right_ref), custom_call_target="tpu_custom_call" | custom-call | flops 1024 | bytes 1024 | tf_op jit(solution)/shard_map/product/pallas_call | solution.py:565
  318.9 15.2 %convolution_convert_fusion = bf16[1536,3072]{1,0:T(8,128)(2,1)} fusion(bf16[1024,1536]{1,0:T(8,128)(2,1)} %constant_dynamic-update-slice_fusion, bf16[1024,3072]{1,0:T(8,128)(2,1)} %get-tuple-element.162.left_ref), kind=kOutput, calls=%fused_computation | convolution fusion | flops 9668395008 | bytes 18874368 | tf_op jit(solution)/shard_map/dot_general | solution.py:315
  337.9 16.1 %weight_halves.10 = (bf16[8,96,3072]{2,1,0:T(8,128)(2,1)}, bf16[8,96,3072]{2,1,0:T(8,128)(2,1)}) custom-call(s32[1]{0:T(128)} %bitcast.side_ref, bf16[1024,1536]{1,0:T(8,128)(2,1)} %pad_maximum_fusion.1.left_ref, bf16[1024,3072]{1,0:T(8,128)(2,1)} %get-tuple-element.143.left_ref.right_ref), custom_call_target="tpu_custom_call" | custom-call | flops 1024 | bytes 1024 | tf_op jit(solution)/shard_map/weight_halves/pallas_call | solution.py:343
  354.0 7.3 norm_back.3
  367.1 6.3 fold.11
  373.5 7.3 cross_attend_back.1
  385.1 6.9 product.11.refs_0_
  392.0 6.9 norm_back.4
  400.0 9.6 %product.12 = bf16[512,1536]{1,0:T(8,128)(2,1)} custom-call(bf16[1024,3072]{1,0:T(8,128)(2,1)} %get-tuple-element.162.left_ref, bf16[1536,6144]{1,0:T(8,128)(2,1)} %all-gather.5.cloned.1.call-done.wi_ref.wo_ref.right_ref), custom_call_target="tpu_custom_call" | custom-call | flops 1024 | bytes 1024 | tf_op jit(solution)/shard_map/product/pallas_call | solution.py:565
  441.6 6.4 product.13.do_ref
  448.0 20.2 %self_attend_back.2.right_ref.refs_0_ = bf16[1024,1152]{1,0:T(8,128)(2,1)} custom-call(s32[1]{0:T(128)} %bitcast.4.t_ref, bf16[1024,2304]{1,0:T(8,128)(2,1)} %fusion.8.q_ref.k_ref.v_ref, bf16[1024,2304]{1,0:T(8,128)(2,1)} %fusion.8.q_ref.k_ref.v_ref, bf16[1024,2304]{1,0:T(8,128)(2,1)} %fusion.8.q_ref.k_ref.v_ref, ...), custom_call_target="tpu_custom_call" | custom-call | flops 1024 | bytes 1024 | tf_op jit(solution)/shard_map/self_attend_back/pallas_call | solution.py:741
  481.5 9.2 %weight_halves.15 = (bf16[8,96,1152]{2,1,0:T(8,128)(2,1)}, bf16[8,96,1152]{2,1,0:T(8,128)(2,1)}) custom-call(s32[1]{0:T(128)} %bitcast.side_ref, bf16[1024,1536]{1,0:T(8,128)(2,1)} %fusion.7.left_ref, bf16[1024,1152]{1,0:T(8,128)(2,1)} %self_attend_back.2.right_ref.refs_0_), custom_call_target="tpu_custom_call" | custom-call | flops 1024 | bytes 1024 | tf_op jit(solution)/shard_map/weight_halves/pallas_call | solution.py:343
  490.8 6.7 weight_halves.16
  526.4 20.0 %self_attend_back.3.right_ref.refs_1_ = bf16[1024,1152]{1,0:T(8,128)(2,1)} custom-call(s32[1]{0:T(128)} %bitcast.4.t_ref, bf16[1024,2304]{1,0:T(8,128)(2,1)} %fusion.8.q_ref.k_ref.v_ref, bf16[1024,2304]{1,0:T(8,128)(2,1)} %fusion.8.q_ref.k_ref.v_ref, bf16[1024,2304]{1,0:T(8,128)(2,1)} %fusion.8.q_ref.k_ref.v_ref, ...), custom_call_target="tpu_custom_call" | custom-call | flops 20000000000 | bytes 1024 | tf_op jit(solution)/shard_map/self_attend_back/pallas_call | solution.py:741
  546.4 9.3 %weight_halves.19 = (bf16[8,96,1152]{2,1,0:T(8,128)(2,1)}, bf16[8,96,1152]{2,1,0:T(8,128)(2,1)}) custom-call(s32[1]{0:T(128)} %bitcast.side_ref, bf16[1024,1536]{1,0:T(8,128)(2,1)} %fusion.7.left_ref, bf16[1024,1152]{1,0:T(8,128)(2,1)} %self_attend_back.3.right_ref.refs_1_), custom_call_target="tpu_custom_call" | custom-call | flops 1024 | bytes 1024 | tf_op jit(solution)/shard_map/weight_halves/pallas_call | solution.py:343
  555.7 13.1 %collective-permute-done.24.refs_3_ = bf16[4,96,1536]{2,1,0:T(8,128)(2,1)} collective-permute-done((bf16[4,96,1536]{2,1,0:T(8,128)(2,1)}, bf16[4,96,1536]{2,1,0:T(8,128)(2,1)}, u32[]{:S(2)}, u32[]{:S(2)}) %collective-permute-start.24) | collective-permute-done | bytes 1179680 | tf_op jit(solution)/shard_map/ppermute | solution.py:973
  576.8 8.6 %joint_product.2.refs_0_ = bf16[512,1536]{1,0:T(8,128)(2,1)} custom-call(bf16[1024,1152]{1,0:T(8,128)(2,1)} %self_attend_back.2.right_ref.refs_0_, bf16[1024,1152]{1,0:T(8,128)(2,1)} %self_attend_back.3.right_ref.refs_1_, bf16[1536,7680]{1,0:T(8,128)(2,1)} %all-gather.3.cloned.1.call-done.right_ref.refs_2_), custom_call_target="tpu_custom_call" | custom-call | flops 999999986991104 | bytes 1024 | tf_op jit(solution)/shard_map/joint_product/pallas_call | solution.py:538
  601.6 8.5 %joint_product.3.refs_0_ = f32[512,1536]{1,0:T(8,128)} custom-call(bf16[1024,1152]{1,0:T(8,128)(2,1)} %self_attend_back.2.right_ref.refs_0_, bf16[1024,1152]{1,0:T(8,128)(2,1)} %self_attend_back.3.right_ref.refs_1_, bf16[1536,7680]{1,0:T(8,128)(2,1)} %all-gather.3.cloned.1.call-done.right_ref.refs_2_), custom_call_target="tpu_custom_call" | custom-call | flops 1024 | bytes 1024 | tf_op jit(solution)/shard_map/joint_product/pallas_call | solution.py:538
  610.1 65.3 %collective-permute-done.28.refs_1_ = bf16[2,96,1920]{2,1,0:T(8,128)(2,1)} collective-permute-done((bf16[2,96,1920]{2,1,0:T(8,128)(2,1)}, bf16[2,96,1920]{2,1,0:T(8,128)(2,1)}, u32[]{:S(2)}, u32[]{:S(2)}) %collective-permute-start.28) | collective-permute-done | bytes 737312 | tf_op jit(solution)/shard_map/ppermute | solution.py:973
  715.1 6.8 norm_back.5
  (252 shorter events, 219.2 us)
Async XLA Ops:
  7.2 137.3 %all-gather.3.cloned.1.call-start = ((), (), s32[]{:S(2)}) async-start(), calls=%async_computation.2 | async-start | bytes 25067520 | tf_op jit(solution)/shard_map/all_gather | solution.py:968
  21.7 232.0 %all-gather.5.cloned.1.call-start = ((), (), s32[]{:S(2)}) async-start(), calls=%async_computation.3 | async-start | bytes 20054016 | tf_op jit(solution)/shard_map/all_gather | solution.py:968
  26.8 441.5 %reduce-scatter.3.cloned.1.call-start = ((), (), s32[]{:S(2)}) async-start(), calls=%async_computation.4 | async-start | bytes 10027008 | tf_op jit(solution)/shard_map/reduce_scatter | solution.py:1050
  26.9 35.6 %collective-permute-start.1 = (bf16[512,1536]{1,0:T(8,128)(2,1)S(1)}, bf16[512,1536]{1,0:T(8,128)(2,1)S(1)}, u32[]{:S(2)}, u32[]{:S(2)}) collective-permute-start(bf16[512,1536]{1,0:T(8,128)(2,1)S(1)} %copy-done), channel_id=1, source_target_pairs={{0,1},{1,0},{2,3},{3,2},{4,5},{5,4},{6,7},{7,6},{8,9},{9,8},{10,11... | collective-permute-start | bytes 4718600 | tf_op jit(solution)/shard_map/ppermute | solution.py:965
  62.5 34.8 %collective-permute-start.2 = (bf16[512,1536]{1,0:T(8,128)(2,1)S(1)}, bf16[512,1536]{1,0:T(8,128)(2,1)S(1)}, u32[]{:S(2)}, u32[]{:S(2)}) collective-permute-start(bf16[512,1536]{1,0:T(8,128)(2,1)S(1)} %copy-done.11), channel_id=1, source_target_pairs={{0,1},{1,0},{2,3},{3,2},{4,5},{5,4},{6,7},{7,6},{8,9},{9,8},{10,11... | collective-permute-start | bytes 4718600 | tf_op jit(solution)/shard_map/ppermute | solution.py:965
  184.6 41.5 %collective-permute-start.3 = (bf16[512,1536]{1,0:T(8,128)(2,1)S(1)}, bf16[512,1536]{1,0:T(8,128)(2,1)S(1)}, u32[]{:S(2)}, u32[]{:S(2)}) collective-permute-start(bf16[512,1536]{1,0:T(8,128)(2,1)S(1)} %convolution_convert_fusion.1), channel_id=1, source_target_pairs={{0,1},{1,0},{2,3},{3,2},{4,5},{5,4},{6,7},{7,6},{8,9},{9,8},{10,11... | collective-permute-start | bytes 4718600 | tf_op jit(solution)/shard_map/ppermute | solution.py:965
  186.2 39.2 %collective-permute-start.4 = (bf16[64,1536]{1,0:T(8,128)(2,1)S(1)}, bf16[64,1536]{1,0:T(8,128)(2,1)S(1)}, u32[]{:S(2)}, u32[]{:S(2)}) collective-permute-start(bf16[64,1536]{1,0:T(8,128)(2,1)S(1)} %fusion.32), channel_id=1, source_target_pairs={{0,1},{1,0},{2,3},{3,2},{4,5},{5,4},{6,7},{7,6},{8,9},{9,8},{10,11... | collective-permute-start | bytes 589832 | tf_op jit(solution)/shard_map/ppermute | solution.py:965
  252.3 38.0 %collective-permute-start.5 = (bf16[512,1536]{1,0:T(8,128)(2,1)S(1)}, bf16[512,1536]{1,0:T(8,128)(2,1)S(1)}, u32[]{:S(2)}, u32[]{:S(2)}) collective-permute-start(bf16[512,1536]{1,0:T(8,128)(2,1)S(1)} %add_convert_fusion.1.n_ref), channel_id=1, source_target_pairs={{0,1},{1,0},{2,3},{3,2},{4,5},{5,4},{6,7},{7,6},{8,9},{9,8},{10,11... | collective-permute-start | bytes 4718600 | tf_op jit(solution)/shard_map/ppermute | solution.py:965
  317.8 36.2 %collective-permute-start.6 = (bf16[512,1536]{1,0:T(8,128)(2,1)}, bf16[512,1536]{1,0:T(8,128)(2,1)}, u32[]{:S(2)}, u32[]{:S(2)}) collective-permute-start(bf16[512,1536]{1,0:T(8,128)(2,1)} %product.9), channel_id=1, source_target_pairs={{0,1},{1,0},{2,3},{3,2},{4,5},{5,4},{6,7},{7,6},{8,9},{9,8},{10,11... | collective-permute-start | bytes 4718600 | tf_op jit(solution)/shard_map/ppermute | solution.py:965
  334.2 351.5 %reduce-scatter.5.cloned.1.call-start = ((), (), s32[]{:S(2)}) async-start(), calls=%async_computation.5 | async-start | bytes 2949120 | tf_op jit(solution)/shard_map/reduce_scatter | solution.py:977
  382.7 16.3 %collective-permute-start.8 = (bf16[64,1536]{1,0:T(8,128)(2,1)S(1)}, bf16[64,1536]{1,0:T(8,128)(2,1)S(1)}, u32[]{:S(2)}, u32[]{:S(2)}) collective-permute-start(bf16[64,1536]{1,0:T(8,128)(2,1)S(1)} %pad_maximum_fusion.8), channel_id=1, source_target_pairs={{0,1},{1,0},{2,3},{3,2},{4,5},{5,4},{6,7},{7,6},{8,9},{9,8},{10,11... | collective-permute-start | bytes 589832 | tf_op jit(solution)/shard_map/ppermute | solution.py:965
  383.9 84.3 %collective-permute-start.13 = (bf16[4,96,3072]{2,1,0:T(8,128)(2,1)}, bf16[4,96,3072]{2,1,0:T(8,128)(2,1)}, u32[]{:S(2)}, u32[]{:S(2)}) collective-permute-start(bf16[4,96,3072]{2,1,0:T(8,128)(2,1)} %get-tuple-element.154), channel_id=1, source_target_pairs={{0,4},{2,6},{4,0},{6,2},{8,12},{10,14},{12,8},{14,10},{16,20},{18,... | collective-permute-start | bytes 7077896 | tf_op jit(solution)/shard_map/ppermute | solution.py:973
  399.1 39.4 %collective-permute-start.9 = (bf16[512,1536]{1,0:T(8,128)(2,1)}, bf16[512,1536]{1,0:T(8,128)(2,1)}, u32[]{:S(2)}, u32[]{:S(2)}) collective-permute-start(bf16[512,1536]{1,0:T(8,128)(2,1)} %get-tuple-element.164), channel_id=1, source_target_pairs={{0,1},{1,0},{2,3},{3,2},{4,5},{5,4},{6,7},{7,6},{8,9},{9,8},{10,11... | collective-permute-start | bytes 4718600 | tf_op jit(solution)/shard_map/ppermute | solution.py:965
  429.3 74.9 %collective-permute-start.14 = (bf16[8,96,768]{2,1,0:T(8,128)(2,1)}, bf16[8,96,768]{2,1,0:T(8,128)(2,1)}, u32[]{:S(2)}, u32[]{:S(2)}) collective-permute-start(bf16[8,96,768]{2,1,0:T(8,128)(2,1)} %get-tuple-element.166), channel_id=1, source_target_pairs={{0,2},{2,0},{4,6},{6,4},{8,10},{10,8},{12,14},{14,12},{16,18},{18,... | collective-permute-start | bytes 3538952 | tf_op jit(solution)/shard_map/ppermute | solution.py:973
  430.9 74.6 %collective-permute-start.16 = (bf16[8,96,768]{2,1,0:T(8,128)(2,1)}, bf16[8,96,768]{2,1,0:T(8,128)(2,1)}, u32[]{:S(2)}, u32[]{:S(2)}) collective-permute-start(bf16[8,96,768]{2,1,0:T(8,128)(2,1)} %get-tuple-element.170), channel_id=1, source_target_pairs={{0,2},{2,0},{4,6},{6,4},{8,10},{10,8},{12,14},{14,12},{16,18},{18,... | collective-permute-start | bytes 3538952 | tf_op jit(solution)/shard_map/ppermute | solution.py:973
  434.3 71.1 %collective-permute-start.15 = (bf16[8,96,768]{2,1,0:T(8,128)(2,1)}, bf16[8,96,768]{2,1,0:T(8,128)(2,1)}, u32[]{:S(2)}, u32[]{:S(2)}) collective-permute-start(bf16[8,96,768]{2,1,0:T(8,128)(2,1)} %totals.3), channel_id=1, source_target_pairs={{0,1},{1,0},{2,3},{3,2},{4,5},{5,4},{6,7},{7,6},{8,9},{9,8},{10,11... | collective-permute-start | bytes 3538952 | tf_op jit(solution)/shard_map/ppermute | solution.py:965
  440.0 66.0 %collective-permute-start.17 = (bf16[8,96,768]{2,1,0:T(8,128)(2,1)}, bf16[8,96,768]{2,1,0:T(8,128)(2,1)}, u32[]{:S(2)}, u32[]{:S(2)}) collective-permute-start(bf16[8,96,768]{2,1,0:T(8,128)(2,1)} %totals.4), channel_id=1, source_target_pairs={{0,1},{1,0},{2,3},{3,2},{4,5},{5,4},{6,7},{7,6},{8,9},{9,8},{10,11... | collective-permute-start | bytes 3538952 | tf_op jit(solution)/shard_map/ppermute | solution.py:965
  471.8 38.7 %collective-permute-start.18 = (bf16[2,96,3072]{2,1,0:T(8,128)(2,1)}, bf16[2,96,3072]{2,1,0:T(8,128)(2,1)S(1)}, u32[]{:S(2)}, u32[]{:S(2)}) collective-permute-start(bf16[2,96,3072]{2,1,0:T(8,128)(2,1)} %get-tuple-element.183), channel_id=1, source_target_pairs={{0,8},{2,10},{4,12},{6,14},{8,0},{10,2},{12,4},{14,6},{16,24},{18,... | collective-permute-start | bytes 3538952 | tf_op jit(solution)/shard_map/ppermute | solution.py:973
  504.2 86.0 %collective-permute-start.31 = (bf16[64,768]{1,0:T(8,128)(2,1)}, bf16[64,768]{1,0:T(8,128)(2,1)}, u32[]{:S(2)}, u32[]{:S(2)}) collective-permute-start(bf16[64,768]{1,0:T(8,128)(2,1)} %constant_dynamic-slice_fusion), channel_id=1, source_target_pairs={{0,1},{1,0},{2,3},{3,2},{4,5},{5,4},{6,7},{7,6},{8,9},{9,8},{10,11... | collective-permute-start | bytes 294920 | tf_op jit(solution)/shard_map/ppermute | solution.py:965
  506.0 15.3 %collective-permute-start.21 = (bf16[8,96,768]{2,1,0:T(8,128)(2,1)}, bf16[8,96,768]{2,1,0:T(8,128)(2,1)}, u32[]{:S(2)}, u32[]{:S(2)}) collective-permute-start(bf16[8,96,768]{2,1,0:T(8,128)(2,1)} %get-tuple-element.194), channel_id=1, source_target_pairs={{0,2},{2,0},{4,6},{6,4},{8,10},{10,8},{12,14},{14,12},{16,18},{18,... | collective-permute-start | bytes 3538952 | tf_op jit(solution)/shard_map/ppermute | solution.py:973
  514.4 75.8 %collective-permute-start.12 = (bf16[512,1536]{1,0:T(8,128)(2,1)}, bf16[512,1536]{1,0:T(8,128)(2,1)}, u32[]{:S(2)}, u32[]{:S(2)}) collective-permute-start(bf16[512,1536]{1,0:T(8,128)(2,1)} %product.12), channel_id=1, source_target_pairs={{0,1},{1,0},{2,3},{3,2},{4,5},{5,4},{6,7},{7,6},{8,9},{9,8},{10,11... | collective-permute-start | bytes 4718600 | tf_op jit(solution)/shard_map/ppermute | solution.py:965
  515.2 40.5 %collective-permute-start.23 = (bf16[4,96,1536]{2,1,0:T(8,128)(2,1)}, bf16[4,96,1536]{2,1,0:T(8,128)(2,1)S(1)}, u32[]{:S(2)}, u32[]{:S(2)}) collective-permute-start(bf16[4,96,1536]{2,1,0:T(8,128)(2,1)} %get-tuple-element.199), channel_id=1, source_target_pairs={{0,4},{2,6},{4,0},{6,2},{8,12},{10,14},{12,8},{14,10},{16,20},{18,... | collective-permute-start | bytes 3538952 | tf_op jit(solution)/shard_map/ppermute | solution.py:973
  524.9 43.9 %collective-permute-start.24 = (bf16[4,96,1536]{2,1,0:T(8,128)(2,1)}, bf16[4,96,1536]{2,1,0:T(8,128)(2,1)}, u32[]{:S(2)}, u32[]{:S(2)}) collective-permute-start(bf16[4,96,1536]{2,1,0:T(8,128)(2,1)} %get-tuple-element.208), channel_id=1, source_target_pairs={{0,4},{2,6},{4,0},{6,2},{8,12},{10,14},{12,8},{14,10},{16,20},{18,... | collective-permute-start | bytes 3538952 | tf_op jit(solution)/shard_map/ppermute | solution.py:973
  525.8 46.6 %collective-permute-start.25 = (bf16[4,96,1920]{2,1,0:T(8,128)(2,1)}, bf16[4,96,1920]{2,1,0:T(8,128)(2,1)S(1)}, u32[]{:S(2)}, u32[]{:S(2)}) collective-permute-start(bf16[4,96,1920]{2,1,0:T(8,128)(2,1)} %get-tuple-element.204), channel_id=1, source_target_pairs={{0,8},{2,10},{4,12},{6,14},{8,0},{10,2},{12,4},{14,6},{16,24},{18,... | collective-permute-start | bytes 4423688 | tf_op jit(solution)/shard_map/ppermute | solution.py:973
  555.7 36.1 %collective-permute-start.26 = (bf16[8,96,1152]{2,1,0:T(8,128)(2,1)}, bf16[8,96,1152]{2,1,0:T(8,128)(2,1)}, u32[]{:S(2)}, u32[]{:S(2)}) collective-permute-start(bf16[8,96,1152]{2,1,0:T(8,128)(2,1)} %get-tuple-element.211), channel_id=1, source_target_pairs={{0,2},{2,0},{4,6},{6,4},{8,10},{10,8},{12,14},{14,12},{16,18},{18,... | collective-permute-start | bytes 5308424 | tf_op jit(solution)/shard_map/ppermute | solution.py:973
  585.4 105.5 %collective-permute-start.27 = (bf16[512,1536]{1,0:T(8,128)(2,1)}, bf16[512,1536]{1,0:T(8,128)(2,1)}, u32[]{:S(2)}, u32[]{:S(2)}) collective-permute-start(bf16[512,1536]{1,0:T(8,128)(2,1)} %joint_product.2.refs_0_), channel_id=1, source_target_pairs={{0,1},{1,0},{2,3},{3,2},{4,5},{5,4},{6,7},{7,6},{8,9},{9,8},{10,11... | collective-permute-start | bytes 4718600 | tf_op jit(solution)/shard_map/ppermute | solution.py:965
  588.8 103.6 %collective-permute-start.34 = (bf16[1,96,3072]{2,1,0:T(8,128)(2,1)}, bf16[1,96,3072]{2,1,0:T(8,128)(2,1)}, u32[]{:S(2)}, u32[]{:S(2)}) collective-permute-start(bf16[1,96,3072]{2,1,0:T(8,128)(2,1)} %get-tuple-element.201), channel_id=1, source_target_pairs={{0,16},{2,18},{4,20},{6,22},{8,24},{10,26},{12,28},{14,30},{16,0},... | collective-permute-start | bytes 1769480 | tf_op jit(solution)/shard_map/ppermute | solution.py:973
  590.2 85.2 %collective-permute-start.28 = (bf16[2,96,1920]{2,1,0:T(8,128)(2,1)}, bf16[2,96,1920]{2,1,0:T(8,128)(2,1)}, u32[]{:S(2)}, u32[]{:S(2)}) collective-permute-start(bf16[2,96,1920]{2,1,0:T(8,128)(2,1)} %get-tuple-element.220), channel_id=1, source_target_pairs={{0,16},{2,18},{4,20},{6,22},{8,24},{10,26},{12,28},{14,30},{16,0},... | collective-permute-start | bytes 2211848 | tf_op jit(solution)/shard_map/ppermute | solution.py:973
  594.8 88.3 %collective-permute-start.29 = (bf16[4,96,1152]{2,1,0:T(8,128)(2,1)}, bf16[4,96,1152]{2,1,0:T(8,128)(2,1)}, u32[]{:S(2)}, u32[]{:S(2)}) collective-permute-start(bf16[4,96,1152]{2,1,0:T(8,128)(2,1)} %get-tuple-element.223), channel_id=1, source_target_pairs={{0,4},{2,6},{4,0},{6,2},{8,12},{10,14},{12,8},{14,10},{16,20},{18,... | collective-permute-start | bytes 2654216 | tf_op jit(solution)/shard_map/ppermute | solution.py:973
  677.8 17.4 %collective-permute-start.32 = (bf16[1,96,1920]{2,1,0:T(8,128)(2,1)}, bf16[1,96,1920]{2,1,0:T(8,128)(2,1)S(1)}, u32[]{:S(2)}, u32[]{:S(2)}) collective-permute-start(bf16[1,96,1920]{2,1,0:T(8,128)(2,1)} %get-tuple-element.228), channel_id=1, source_target_pairs={{0,4},{2,6},{4,0},{6,2},{8,12},{10,14},{12,8},{14,10},{16,20},{18,... | collective-permute-start | bytes 1105928 | tf_op jit(solution)/shard_map/ppermute | solution.py:973
  711.1 15.1 %collective-permute-start.33 = (bf16[1,96,1152]{2,1,0:T(8,128)(2,1)}, bf16[1,96,1152]{2,1,0:T(8,128)(2,1)S(1)}, u32[]{:S(2)}, u32[]{:S(2)}) collective-permute-start(bf16[1,96,1152]{2,1,0:T(8,128)(2,1)} %get-tuple-element.235), channel_id=1, source_target_pairs={{0,16},{2,18},{4,20},{6,22},{8,24},{10,26},{12,28},{14,30},{16,0},... | collective-permute-start | bytes 663560 | tf_op jit(solution)/shard_map/ppermute | solution.py:973
  711.1 14.4 %collective-permute-start.39 = (f32[6,1536]{1,0:T(8,128)S(1)}, f32[6,1536]{1,0:T(8,128)S(1)}, u32[]{:S(2)}, u32[]{:S(2)}) collective-permute-start(f32[6,1536]{1,0:T(8,128)S(1)} %add.136), channel_id=1, source_target_pairs={{0,16},{2,18},{4,20},{6,22},{8,24},{10,26},{12,28},{14,30},{16,0},... | collective-permute-start | bytes 110600 | tf_op jit(solution)/shard_map/ppermute | solution.py:1164
  (52 other events, 553.4 us)
Sparse Core Ops, SparseCore 0:
  21.9 122.5 all-gather.2
  146.7 98.8 all-gather.4
  334.3 128.0 reduce-scatter.2
  572.6 80.4 reduce-scatter.4

commit v5 on v4

--- a/solution.py
+++ b/solution.py
@@ -1131,23 +1131,23 @@
     qkv1_got = swap(qkv1[0], 0)
     cross = totals((after(cross[1], qkv1[0]), cross_got), (kv[1], kv_got))
     cross_sum = line_sum(cross)
-    most = fold(side_refs[3], (after(most[1], cross), most_got), inner=2)
+    inner_sum = line_end(inner[0], after(inner[1], cross))
+    most = fold(side_refs[3], (after(most[1], inner_sum), most_got), inner=2)
     most_got = swap(most[0], 3)
     back1_part = joint_product([found0, after(found1, most[0])], first, BF, 1, rows, HEAVY)
     back1_away = peer(back1_part)
     qkv1 = fold(side_refs[1], (after(qkv1[1], back1_part), qkv1_got))
     qkv1_got = swap(qkv1[0], 1)
     back1_home = joint_product([found0, after(found1, qkv1[0])], first, F32, 0, rows, LIGHT)
-    most = fold(side_refs[1], (after(most[1], back1_home), most_got))
+    qkv1 = fold(side_refs[2], (after(qkv1[1], back1_home), qkv1_got))
+    sums0 = norm_sums(after(inputs_peer, qkv1[0]), [back1_part])
+    sums1 = sums0 + norm_sums(after(inputs, sums0), [back1_home])
+    most = fold(side_refs[1], (after(most[1], sums1), most_got))
     most_got = swap(most[0], 1)
-    sums0 = norm_sums(after(inputs_peer, most[0]), [back1_part])
-    qkv1 = fold(side_refs[2], (after(qkv1[1], sums0), qkv1_got))
-    sums1 = sums0 + norm_sums(after(inputs, qkv1[0], cross_sum), [back1_home])
-    qkv1 = line_step(*qkv1, sums1)
+    qkv1 = line_step(*qkv1, most[0])
     input_grad, _, _ = norm_back_rows(
-        inputs, norm_gains[0], grad1, [back1_home, after(back1_away, qkv1[0])]
-    )
-    inner_sum = line_end(inner[0], after(inner[1], back1_home))
+        inputs, norm_gains[0], grad1, [back1_home, after(back1_away, qkv1[0], cross_sum)]
+    )
     most_sum = (most[1].astype(F32) + most_got.astype(F32)).reshape(shard, -1)
     qkv1_sum = line_end(*qkv1)
     qkv0_sum, so_sum = most_sum[:, : 3 * part], most_sum[:, 3 * part :]

time: 747 us -> 735 us (0.984)
  waiting for transfers between devices: 241 us -> 220 us
    ppermute x21, waiting for transfers between devices: 84.5 us -> 63.4 us  [swap(): return lax.ppermute(send, 'dp', swaps[level])]
    unnamed x84 -> x88, local copies, waits for them, and re-layouts: 17.2 us -> 17.4 us
  transfers between devices with their start and end apart: 44 -> 44, of which waited for: 12 -> 11; matrix products, arithmetic and copies ran while one was open for 13% -> 14% of each run, Pallas kernels for 41% -> 41%
where the time goes in v5:
time: 735 us; the launch traced here: 723 us
  Pallas kernels  334 us (45%)
  waiting for transfers between devices  220 us (30%)
  matrix products  53.8 us (7%)
  starting transfers between devices  40.6 us (6%)
  local copies, waits for them, and re-layouts  30.8 us (4%)
  other arithmetic  28.8 us (4%)
  between operations  14.7 us (2%)
    ppermute x15, waiting for transfers between devices, peer(): return lax.ppermute(value, 'tensor', [(0, 1), (1, 0)])  103 us
    pallas_call x10, Pallas kernels, weight_halves(): pl.pallas_call(partial(weight_kernel, shard=shard), out_shape=(shape, sha...  67.6 us
    ppermute x21, waiting for transfers between devices, swap(): return lax.ppermute(send, 'dp', swaps[level])  63.4 us
    pallas_call x7, Pallas kernels, product(): pl.pallas_call(partial(product_kernel, dims=dims), grid=(size // tile,),...  57.8 us
    dot_general x8, matrix products, mm(): return lax.dot_general(left, right, dims, preferred_element_type=F32)  53.8 us
    all_gather x2, waiting for transfers between devices, gather(): return lax.all_gather(packed, 'dp', axis=0, tiled=True)  44.8 us
    pallas_call x2, Pallas kernels, self_backward(): pl.pallas_call(self_back_kernel, out_shape=jax.ShapeDtypeStruct((length,...  40.3 us
    pallas_call x11, Pallas kernels, fold(): pl.pallas_call(partial(fold_kernel, counts=[len(terms) for terms in group...  38.9 us
  transfers between devices with their start and end apart: 44, of which 11 were waited for; matrix products, arithmetic and copies ran while one was open for 14% of the time, Pallas kernels for 41%

profile of v5, /device:TPU:0, one launch (start us, length us, event | category | flops | bytes accessed | tf_op | source)
XLA Modules:
  0.0 723.0 jit_solution(7886560004176189338)
XLA Ops:
  30.6 31.9 %collective-permute-done.1.value_ref = bf16[512,1536]{1,0:T(8,128)(2,1)S(1)} collective-permute-done((bf16[512,1536]{1,0:T(8,128)(2,1)S(1)}, bf16[512,1536]{1,0:T(8,128)(2,1)S(1)}, u32[]{:S(2)}, u32[]{:S(2)}) %collective-permute-start.1) | collective-permute-done | bytes 1572896 | tf_op jit(solution)/shard_map/ppermute | solution.py:965
  70.3 27.0 %collective-permute-done.2.g_ref = bf16[512,1536]{1,0:T(8,128)(2,1)S(1)} collective-permute-done((bf16[512,1536]{1,0:T(8,128)(2,1)S(1)}, bf16[512,1536]{1,0:T(8,128)(2,1)S(1)}, u32[]{:S(2)}, u32[]{:S(2)}) %collective-permute-start.2) | collective-permute-done | bytes 1572896 | tf_op jit(solution)/shard_map/ppermute | solution.py:965
  99.7 44.8 %all-gather.3.cloned.1.call-done.right_ref.refs_2_ = bf16[1536,7680]{1,0:T(8,128)(2,1)} async-done(((bf16[96,7680]{1,0:T(8,128)(2,1)}), bf16[1536,7680]{1,0:T(8,128)(2,1)}) %all-gather.3.cloned.1.call-update) | async-done | bytes 23592976 | tf_op jit(solution)/shard_map/all_gather | solution.py:968
  147.9 12.1 %fusion.8.q_ref.k_ref.v_ref = bf16[1024,2304]{1,0:T(8,128)(2,1)} fusion(bf16[1024,1536]{1,0:T(8,128)(2,1)S(1)} %copy-done.3, bf16[1536,7680]{1,0:T(8,128)(2,1)} %all-gather.3.cloned.1.call-done.right_ref.refs_2_), kind=kOutput, calls=%fused_computation.11 | convolution fusion | flops 7250116608 | bytes 14942208 | tf_op jit(solution)/shard_map/dot_general | solution.py:315
  160.0 21.0 %self_attend.1 = (bf16[1024,768]{1,0:T(8,128)(2,1)}, f32[6,8,1024]{2,1,0:T(8,128)}) custom-call(s32[1]{0:T(128)} %bitcast.4.t_ref, bf16[1024,2304]{1,0:T(8,128)(2,1)} %fusion.8.q_ref.k_ref.v_ref, bf16[1024,2304]{1,0:T(8,128)(2,1)} %fusion.8.q_ref.k_ref.v_ref, bf16[1024,2304]{1,0:T(8,128)(2,1)} %fusion.8.q_ref.k_ref.v_ref), custom_call_target="tpu_custom_call" | custom-call | flops 1024 | bytes 1024 | tf_op jit(solution)/shard_map/self_attend/pallas_call | solution.py:650
  186.7 38.6 %collective-permute-done.4 = bf16[64,1536]{1,0:T(8,128)(2,1)S(1)} collective-permute-done((bf16[64,1536]{1,0:T(8,128)(2,1)S(1)}, bf16[64,1536]{1,0:T(8,128)(2,1)S(1)}, u32[]{:S(2)}, u32[]{:S(2)}) %collective-permute-start.4) | collective-permute-done | bytes 196640 | tf_op jit(solution)/shard_map/ppermute | solution.py:965
  231.9 6.7 fusion.23.q_ref
  238.6 6.8 cross_attend.1
  253.7 16.9 %ffn_middle.2 = (bf16[1024,3072]{1,0:T(8,128)(2,1)}, bf16[1024,3072]{1,0:T(8,128)(2,1)}) custom-call(bf16[512,1536]{1,0:T(8,128)(2,1)} %copy-done.8, bf16[512,1536]{1,0:T(8,128)(2,1)} %base_ref.1, bf16[1536,6144]{1,0:T(8,128)(2,1)} %all-gather.5.cloned.1.call-done.wi_ref.wo_ref.right_ref, bf16[1536,6144]{1,0:T(8,128)(2,1)} %all-gather.5.cloned.1.call-done.wi_ref.wo_ref.right_ref), custom_call_target="tpu_custom_call" | custom-call | flops 1024 | bytes 1024 | tf_op jit(solution)/shard_map/ffn_middle/pallas_call | solution.py:894
  270.6 9.8 %product.7 = f32[512,1536]{1,0:T(8,128)} custom-call(bf16[1024,3072]{1,0:T(8,128)(2,1)} %get-tuple-element.139.left_ref.refs_0_, bf16[1536,6144]{1,0:T(8,128)(2,1)} %all-gather.5.cloned.1.call-done.wi_ref.wo_ref.right_ref), custom_call_target="tpu_custom_call" | custom-call | flops 1024 | bytes 1024 | tf_op jit(solution)/shard_map/product/pallas_call | solution.py:565
  280.4 9.8 %product.8.refs_0_ = f32[512,1536]{1,0:T(8,128)} custom-call(bf16[1024,3072]{1,0:T(8,128)(2,1)} %get-tuple-element.140.left_ref.refs_1_, bf16[1536,6144]{1,0:T(8,128)(2,1)} %all-gather.5.cloned.1.call-done.wi_ref.wo_ref.right_ref), custom_call_target="tpu_custom_call" | custom-call | flops 1024 | bytes 1024 | tf_op jit(solution)/shard_map/product/pallas_call | solution.py:565
  291.4 16.9 %ffn_middle.3 = (bf16[1024,3072]{1,0:T(8,128)(2,1)}, bf16[1024,3072]{1,0:T(8,128)(2,1)}) custom-call(bf16[512,1536]{1,0:T(8,128)(2,1)} %copy-done.13, bf16[512,1536]{1,0:T(8,128)(2,1)} %copy-done.12, bf16[1536,6144]{1,0:T(8,128)(2,1)} %all-gather.5.cloned.1.call-done.wi_ref.wo_ref.right_ref, ...), custom_call_target="tpu_custom_call", output_to_operand_aliasing={{0}: (4, {}), {1}: (5, {})} | custom-call | flops 1024 | bytes 1024 | tf_op jit(solution)/shard_map/ffn_middle/pallas_call | solution.py:894
  308.3 9.5 %product.9 = bf16[512,1536]{1,0:T(8,128)(2,1)} custom-call(bf16[1024,3072]{1,0:T(8,128)(2,1)} %get-tuple-element.143.left_ref.right_ref, bf16[1536,6144]{1,0:T(8,128)(2,1)} %all-gather.5.cloned.1.call-done.wi_ref.wo_ref.right_ref), custom_call_target="tpu_custom_call" | custom-call | flops 1024 | bytes 1024 | tf_op jit(solution)/shard_map/product/pallas_call | solution.py:565
  318.9 15.5 %convolution_convert_fusion = bf16[1536,3072]{1,0:T(8,128)(2,1)} fusion(bf16[1024,1536]{1,0:T(8,128)(2,1)} %constant_dynamic-update-slice_fusion, bf16[1024,3072]{1,0:T(8,128)(2,1)} %get-tuple-element.162.left_ref), kind=kOutput, calls=%fused_computation | convolution fusion | flops 9668395008 | bytes 18874368 | tf_op jit(solution)/shard_map/dot_general | solution.py:315
  338.2 16.3 %weight_halves.10 = (bf16[8,96,3072]{2,1,0:T(8,128)(2,1)}, bf16[8,96,3072]{2,1,0:T(8,128)(2,1)}) custom-call(s32[1]{0:T(128)} %bitcast.side_ref, bf16[1024,1536]{1,0:T(8,128)(2,1)} %pad_maximum_fusion.1.left_ref, bf16[1024,3072]{1,0:T(8,128)(2,1)} %get-tuple-element.143.left_ref.right_ref), custom_call_target="tpu_custom_call" | custom-call | flops 1024 | bytes 1024 | tf_op jit(solution)/shard_map/weight_halves/pallas_call | solution.py:343
  354.4 7.3 %norm_back.3 = (f32[512,1536]{1,0:T(8,128)}, bf16[512,1536]{1,0:T(8,128)(2,1)}, f32[8,1536]{1,0:T(8,128)}) custom-call(f32[512,1536]{1,0:T(8,128)} %copy-done.1, f32[1,1536]{1,0:T(1,128)} %get-tuple-element.278.gain_ref, bf16[512,1536]{1,0:T(8,128)(2,1)} %base_ref.1, f32[512,1536]{1,0:T(8,128)} %product.8.refs_0_, ...), custom_call_target="tpu_custom_call" | custom-call | flops 999999986991104 | bytes 1024 | tf_op jit(solution)/shard_map/norm_back/pallas_call | solution.py:511
  373.9 7.4 %cross_attend_back.1 = (bf16[512,1536]{1,0:T(8,128)(2,1)}, f32[64,1536]{1,0:T(8,128)}, f32[64,1536]{1,0:T(8,128)}) custom-call(bf16[512,1536]{1,0:T(8,128)(2,1)} %fusion.23.q_ref, bf16[64,1536]{1,0:T(8,128)(2,1)} %get-tuple-element.284.k_ref, bf16[64,1536]{1,0:T(8,128)(2,1)} %get-tuple-element.285.v_ref, ...), custom_call_target="tpu_custom_call" | custom-call | flops 1024 | bytes 1024 | tf_op jit(solution)/shard_map/cross_attend_back/pallas_call | solution.py:851
  385.3 6.8 product.11.refs_0_
  392.1 6.9 norm_back.4
  401.0 9.6 %product.12 = bf16[512,1536]{1,0:T(8,128)(2,1)} custom-call(bf16[1024,3072]{1,0:T(8,128)(2,1)} %get-tuple-element.162.left_ref, bf16[1536,6144]{1,0:T(8,128)(2,1)} %all-gather.5.cloned.1.call-done.wi_ref.wo_ref.right_ref), custom_call_target="tpu_custom_call" | custom-call | flops 1024 | bytes 1024 | tf_op jit(solution)/shard_map/product/pallas_call | solution.py:565
  448.8 20.2 %self_attend_back.2.right_ref.refs_0_ = bf16[1024,1152]{1,0:T(8,128)(2,1)} custom-call(s32[1]{0:T(128)} %bitcast.4.t_ref, bf16[1024,2304]{1,0:T(8,128)(2,1)} %fusion.8.q_ref.k_ref.v_ref, bf16[1024,2304]{1,0:T(8,128)(2,1)} %fusion.8.q_ref.k_ref.v_ref, bf16[1024,2304]{1,0:T(8,128)(2,1)} %fusion.8.q_ref.k_ref.v_ref, ...), custom_call_target="tpu_custom_call" | custom-call | flops 1024 | bytes 1024 | tf_op jit(solution)/shard_map/self_attend_back/pallas_call | solution.py:741
  477.0 9.2 %weight_halves.15 = (bf16[8,96,1152]{2,1,0:T(8,128)(2,1)}, bf16[8,96,1152]{2,1,0:T(8,128)(2,1)}) custom-call(s32[1]{0:T(128)} %bitcast.side_ref, bf16[1024,1536]{1,0:T(8,128)(2,1)} %fusion.7.left_ref, bf16[1024,1152]{1,0:T(8,128)(2,1)} %self_attend_back.2.right_ref.refs_0_), custom_call_target="tpu_custom_call" | custom-call | flops 1024 | bytes 1024 | tf_op jit(solution)/shard_map/weight_halves/pallas_call | solution.py:343
  486.2 6.7 weight_halves.16
  523.5 20.1 %self_attend_back.3.right_ref.refs_1_ = bf16[1024,1152]{1,0:T(8,128)(2,1)} custom-call(s32[1]{0:T(128)} %bitcast.4.t_ref, bf16[1024,2304]{1,0:T(8,128)(2,1)} %fusion.8.q_ref.k_ref.v_ref, bf16[1024,2304]{1,0:T(8,128)(2,1)} %fusion.8.q_ref.k_ref.v_ref, bf16[1024,2304]{1,0:T(8,128)(2,1)} %fusion.8.q_ref.k_ref.v_ref, ...), custom_call_target="tpu_custom_call" | custom-call | flops 20000000000 | bytes 1024 | tf_op jit(solution)/shard_map/self_attend_back/pallas_call | solution.py:741
  543.6 9.2 %weight_halves.19 = (bf16[8,96,1152]{2,1,0:T(8,128)(2,1)}, bf16[8,96,1152]{2,1,0:T(8,128)(2,1)}) custom-call(s32[1]{0:T(128)} %bitcast.side_ref, bf16[1024,1536]{1,0:T(8,128)(2,1)} %fusion.7.left_ref, bf16[1024,1152]{1,0:T(8,128)(2,1)} %self_attend_back.3.right_ref.refs_1_), custom_call_target="tpu_custom_call" | custom-call | flops 1024 | bytes 1024 | tf_op jit(solution)/shard_map/weight_halves/pallas_call | solution.py:343
  553.0 10.8 %collective-permute-done.24.refs_3_ = bf16[4,96,1536]{2,1,0:T(8,128)(2,1)} collective-permute-done((bf16[4,96,1536]{2,1,0:T(8,128)(2,1)}, bf16[4,96,1536]{2,1,0:T(8,128)(2,1)}, u32[]{:S(2)}, u32[]{:S(2)}) %collective-permute-start.24) | collective-permute-done | bytes 1179680 | tf_op jit(solution)/shard_map/ppermute | solution.py:973
  574.0 8.1 %joint_product.2.refs_0_ = bf16[512,1536]{1,0:T(8,128)(2,1)} custom-call(bf16[1024,1152]{1,0:T(8,128)(2,1)} %self_attend_back.2.right_ref.refs_0_, bf16[1024,1152]{1,0:T(8,128)(2,1)} %self_attend_back.3.right_ref.refs_1_, bf16[1536,7680]{1,0:T(8,128)(2,1)} %all-gather.3.cloned.1.call-done.right_ref.refs_2_), custom_call_target="tpu_custom_call" | custom-call | flops 999999986991104 | bytes 1024 | tf_op jit(solution)/shard_map/joint_product/pallas_call | solution.py:538
  596.5 8.5 %joint_product.3.refs_0_ = f32[512,1536]{1,0:T(8,128)} custom-call(bf16[1024,1152]{1,0:T(8,128)(2,1)} %self_attend_back.2.right_ref.refs_0_, bf16[1024,1152]{1,0:T(8,128)(2,1)} %self_attend_back.3.right_ref.refs_1_, bf16[1536,7680]{1,0:T(8,128)(2,1)} %all-gather.3.cloned.1.call-done.right_ref.refs_2_), custom_call_target="tpu_custom_call" | custom-call | flops 1024 | bytes 1024 | tf_op jit(solution)/shard_map/joint_product/pallas_call | solution.py:538
  620.1 40.0 %collective-permute-done.30.refs_1_ = bf16[2,96,1920]{2,1,0:T(8,128)(2,1)} collective-permute-done((bf16[2,96,1920]{2,1,0:T(8,128)(2,1)}, bf16[2,96,1920]{2,1,0:T(8,128)(2,1)}, u32[]{:S(2)}, u32[]{:S(2)}) %collective-permute-start.30) | collective-permute-done | bytes 737312 | tf_op jit(solution)/shard_map/ppermute | solution.py:973
  680.0 7.3 %collective-permute-done.38 = f32[6,1536]{1,0:T(8,128)S(1)} collective-permute-done((f32[6,1536]{1,0:T(8,128)S(1)}, f32[6,1536]{1,0:T(8,128)S(1)}, u32[]{:S(2)}, u32[]{:S(2)}) %collective-permute-start.38) | collective-permute-done | bytes 36896 | tf_op jit(solution)/shard_map/ppermute | solution.py:1164
  694.4 10.5 %collective-permute-done.34 = bf16[1,96,1152]{2,1,0:T(8,128)(2,1)S(1)} collective-permute-done((bf16[1,96,1152]{2,1,0:T(8,128)(2,1)}, bf16[1,96,1152]{2,1,0:T(8,128)(2,1)S(1)}, u32[]{:S(2)}, u32[]{:S(2)}) %collective-permute-start.34) | collective-permute-done | bytes 221216 | tf_op jit(solution)/shard_map/ppermute | solution.py:973
  708.2 6.8 norm_back.5
  (256 shorter events, 229.3 us)
Async XLA Ops:
  7.2 137.3 %all-gather.3.cloned.1.call-start = ((), (), s32[]{:S(2)}) async-start(), calls=%async_computation.2 | async-start | bytes 25067520 | tf_op jit(solution)/shard_map/all_gather | solution.py:968
  21.7 232.0 %all-gather.5.cloned.1.call-start = ((), (), s32[]{:S(2)}) async-start(), calls=%async_computation.3 | async-start | bytes 20054016 | tf_op jit(solution)/shard_map/all_gather | solution.py:968
  26.8 442.2 %reduce-scatter.3.cloned.1.call-start = ((), (), s32[]{:S(2)}) async-start(), calls=%async_computation.4 | async-start | bytes 10027008 | tf_op jit(solution)/shard_map/reduce_scatter | solution.py:1050
  26.9 35.6 %collective-permute-start.1 = (bf16[512,1536]{1,0:T(8,128)(2,1)S(1)}, bf16[512,1536]{1,0:T(8,128)(2,1)S(1)}, u32[]{:S(2)}, u32[]{:S(2)}) collective-permute-start(bf16[512,1536]{1,0:T(8,128)(2,1)S(1)} %copy-done), channel_id=1, source_target_pairs={{0,1},{1,0},{2,3},{3,2},{4,5},{5,4},{6,7},{7,6},{8,9},{9,8},{10,11... | collective-permute-start | bytes 4718600 | tf_op jit(solution)/shard_map/ppermute | solution.py:965
  62.5 34.8 %collective-permute-start.2 = (bf16[512,1536]{1,0:T(8,128)(2,1)S(1)}, bf16[512,1536]{1,0:T(8,128)(2,1)S(1)}, u32[]{:S(2)}, u32[]{:S(2)}) collective-permute-start(bf16[512,1536]{1,0:T(8,128)(2,1)S(1)} %copy-done.11), channel_id=1, source_target_pairs={{0,1},{1,0},{2,3},{3,2},{4,5},{5,4},{6,7},{7,6},{8,9},{9,8},{10,11... | collective-permute-start | bytes 4718600 | tf_op jit(solution)/shard_map/ppermute | solution.py:965
  184.6 41.5 %collective-permute-start.3 = (bf16[512,1536]{1,0:T(8,128)(2,1)S(1)}, bf16[512,1536]{1,0:T(8,128)(2,1)S(1)}, u32[]{:S(2)}, u32[]{:S(2)}) collective-permute-start(bf16[512,1536]{1,0:T(8,128)(2,1)S(1)} %convolution_convert_fusion.1), channel_id=1, source_target_pairs={{0,1},{1,0},{2,3},{3,2},{4,5},{5,4},{6,7},{7,6},{8,9},{9,8},{10,11... | collective-permute-start | bytes 4718600 | tf_op jit(solution)/shard_map/ppermute | solution.py:965
  186.2 39.2 %collective-permute-start.4 = (bf16[64,1536]{1,0:T(8,128)(2,1)S(1)}, bf16[64,1536]{1,0:T(8,128)(2,1)S(1)}, u32[]{:S(2)}, u32[]{:S(2)}) collective-permute-start(bf16[64,1536]{1,0:T(8,128)(2,1)S(1)} %fusion.32), channel_id=1, source_target_pairs={{0,1},{1,0},{2,3},{3,2},{4,5},{5,4},{6,7},{7,6},{8,9},{9,8},{10,11... | collective-permute-start | bytes 589832 | tf_op jit(solution)/shard_map/ppermute | solution.py:965
  252.3 38.0 %collective-permute-start.5 = (bf16[512,1536]{1,0:T(8,128)(2,1)S(1)}, bf16[512,1536]{1,0:T(8,128)(2,1)S(1)}, u32[]{:S(2)}, u32[]{:S(2)}) collective-permute-start(bf16[512,1536]{1,0:T(8,128)(2,1)S(1)} %add_convert_fusion.1.n_ref), channel_id=1, source_target_pairs={{0,1},{1,0},{2,3},{3,2},{4,5},{5,4},{6,7},{7,6},{8,9},{9,8},{10,11... | collective-permute-start | bytes 4718600 | tf_op jit(solution)/shard_map/ppermute | solution.py:965
  317.7 36.7 %collective-permute-start.6 = (bf16[512,1536]{1,0:T(8,128)(2,1)}, bf16[512,1536]{1,0:T(8,128)(2,1)}, u32[]{:S(2)}, u32[]{:S(2)}) collective-permute-start(bf16[512,1536]{1,0:T(8,128)(2,1)} %product.9), channel_id=1, source_target_pairs={{0,1},{1,0},{2,3},{3,2},{4,5},{5,4},{6,7},{7,6},{8,9},{9,8},{10,11... | collective-permute-start | bytes 4718600 | tf_op jit(solution)/shard_map/ppermute | solution.py:965
  334.5 373.8 %reduce-scatter.5.cloned.1.call-start = ((), (), s32[]{:S(2)}) async-start(), calls=%async_computation.5 | async-start | bytes 2949120 | tf_op jit(solution)/shard_map/reduce_scatter | solution.py:977
  354.4 13.2 %collective-permute-start.7 = (bf16[8,96,3072]{2,1,0:T(8,128)(2,1)}, bf16[8,96,3072]{2,1,0:T(8,128)(2,1)}, u32[]{:S(2)}, u32[]{:S(2)}) collective-permute-start(bf16[8,96,3072]{2,1,0:T(8,128)(2,1)} %get-tuple-element.147), channel_id=1, source_target_pairs={{0,2},{2,0},{4,6},{6,4},{8,10},{10,8},{12,14},{14,12},{16,18},{18,... | collective-permute-start | bytes 14155784 | tf_op jit(solution)/shard_map/ppermute | solution.py:973
  383.2 15.9 %collective-permute-start.8 = (bf16[64,1536]{1,0:T(8,128)(2,1)S(1)}, bf16[64,1536]{1,0:T(8,128)(2,1)S(1)}, u32[]{:S(2)}, u32[]{:S(2)}) collective-permute-start(bf16[64,1536]{1,0:T(8,128)(2,1)S(1)} %pad_maximum_fusion.8), channel_id=1, source_target_pairs={{0,1},{1,0},{2,3},{3,2},{4,5},{5,4},{6,7},{7,6},{8,9},{9,8},{10,11... | collective-permute-start | bytes 589832 | tf_op jit(solution)/shard_map/ppermute | solution.py:965
  384.3 84.7 %collective-permute-start.13 = (bf16[4,96,3072]{2,1,0:T(8,128)(2,1)}, bf16[4,96,3072]{2,1,0:T(8,128)(2,1)}, u32[]{:S(2)}, u32[]{:S(2)}) collective-permute-start(bf16[4,96,3072]{2,1,0:T(8,128)(2,1)} %get-tuple-element.154), channel_id=1, source_target_pairs={{0,4},{2,6},{4,0},{6,2},{8,12},{10,14},{12,8},{14,10},{16,20},{18,... | collective-permute-start | bytes 7077896 | tf_op jit(solution)/shard_map/ppermute | solution.py:973
  399.9 39.4 %collective-permute-start.9 = (bf16[512,1536]{1,0:T(8,128)(2,1)}, bf16[512,1536]{1,0:T(8,128)(2,1)}, u32[]{:S(2)}, u32[]{:S(2)}) collective-permute-start(bf16[512,1536]{1,0:T(8,128)(2,1)} %get-tuple-element.164), channel_id=1, source_target_pairs={{0,1},{1,0},{2,3},{3,2},{4,5},{5,4},{6,7},{7,6},{8,9},{9,8},{10,11... | collective-permute-start | bytes 4718600 | tf_op jit(solution)/shard_map/ppermute | solution.py:965
  430.4 69.4 %collective-permute-start.14 = (bf16[8,96,768]{2,1,0:T(8,128)(2,1)}, bf16[8,96,768]{2,1,0:T(8,128)(2,1)}, u32[]{:S(2)}, u32[]{:S(2)}) collective-permute-start(bf16[8,96,768]{2,1,0:T(8,128)(2,1)} %get-tuple-element.166), channel_id=1, source_target_pairs={{0,2},{2,0},{4,6},{6,4},{8,10},{10,8},{12,14},{14,12},{16,18},{18,... | collective-permute-start | bytes 3538952 | tf_op jit(solution)/shard_map/ppermute | solution.py:973
  431.9 69.1 %collective-permute-start.16 = (bf16[8,96,768]{2,1,0:T(8,128)(2,1)}, bf16[8,96,768]{2,1,0:T(8,128)(2,1)}, u32[]{:S(2)}, u32[]{:S(2)}) collective-permute-start(bf16[8,96,768]{2,1,0:T(8,128)(2,1)} %get-tuple-element.170), channel_id=1, source_target_pairs={{0,2},{2,0},{4,6},{6,4},{8,10},{10,8},{12,14},{14,12},{16,18},{18,... | collective-permute-start | bytes 3538952 | tf_op jit(solution)/shard_map/ppermute | solution.py:973
  435.4 65.6 %collective-permute-start.15 = (bf16[8,96,768]{2,1,0:T(8,128)(2,1)}, bf16[8,96,768]{2,1,0:T(8,128)(2,1)}, u32[]{:S(2)}, u32[]{:S(2)}) collective-permute-start(bf16[8,96,768]{2,1,0:T(8,128)(2,1)} %totals.3), channel_id=1, source_target_pairs={{0,1},{1,0},{2,3},{3,2},{4,5},{5,4},{6,7},{7,6},{8,9},{9,8},{10,11... | collective-permute-start | bytes 3538952 | tf_op jit(solution)/shard_map/ppermute | solution.py:965
  440.8 60.8 %collective-permute-start.17 = (bf16[8,96,768]{2,1,0:T(8,128)(2,1)}, bf16[8,96,768]{2,1,0:T(8,128)(2,1)}, u32[]{:S(2)}, u32[]{:S(2)}) collective-permute-start(bf16[8,96,768]{2,1,0:T(8,128)(2,1)} %totals.4), channel_id=1, source_target_pairs={{0,1},{1,0},{2,3},{3,2},{4,5},{5,4},{6,7},{7,6},{8,9},{9,8},{10,11... | collective-permute-start | bytes 3538952 | tf_op jit(solution)/shard_map/ppermute | solution.py:965
  472.6 33.4 %collective-permute-start.18 = (bf16[2,96,3072]{2,1,0:T(8,128)(2,1)}, bf16[2,96,3072]{2,1,0:T(8,128)(2,1)S(1)}, u32[]{:S(2)}, u32[]{:S(2)}) collective-permute-start(bf16[2,96,3072]{2,1,0:T(8,128)(2,1)} %get-tuple-element.183), channel_id=1, source_target_pairs={{0,8},{2,10},{4,12},{6,14},{8,0},{10,2},{12,4},{14,6},{16,24},{18,... | collective-permute-start | bytes 3538952 | tf_op jit(solution)/shard_map/ppermute | solution.py:973
  499.8 96.7 %collective-permute-start.12 = (bf16[512,1536]{1,0:T(8,128)(2,1)}, bf16[512,1536]{1,0:T(8,128)(2,1)}, u32[]{:S(2)}, u32[]{:S(2)}) collective-permute-start(bf16[512,1536]{1,0:T(8,128)(2,1)} %product.12), channel_id=1, source_target_pairs={{0,1},{1,0},{2,3},{3,2},{4,5},{5,4},{6,7},{7,6},{8,9},{9,8},{10,11... | collective-permute-start | bytes 4718600 | tf_op jit(solution)/shard_map/ppermute | solution.py:965
  501.5 16.8 %collective-permute-start.21 = (bf16[8,96,768]{2,1,0:T(8,128)(2,1)}, bf16[8,96,768]{2,1,0:T(8,128)(2,1)}, u32[]{:S(2)}, u32[]{:S(2)}) collective-permute-start(bf16[8,96,768]{2,1,0:T(8,128)(2,1)} %get-tuple-element.194), channel_id=1, source_target_pairs={{0,2},{2,0},{4,6},{6,4},{8,10},{10,8},{12,14},{14,12},{16,18},{18,... | collective-permute-start | bytes 3538952 | tf_op jit(solution)/shard_map/ppermute | solution.py:973
  509.9 43.0 %collective-permute-start.23 = (bf16[4,96,1536]{2,1,0:T(8,128)(2,1)}, bf16[4,96,1536]{2,1,0:T(8,128)(2,1)S(1)}, u32[]{:S(2)}, u32[]{:S(2)}) collective-permute-start(bf16[4,96,1536]{2,1,0:T(8,128)(2,1)} %get-tuple-element.199), channel_id=1, source_target_pairs={{0,4},{2,6},{4,0},{6,2},{8,12},{10,14},{12,8},{14,10},{16,20},{18,... | collective-permute-start | bytes 3538952 | tf_op jit(solution)/shard_map/ppermute | solution.py:973
  511.0 56.5 %collective-permute-start.25 = (bf16[1,96,3072]{2,1,0:T(8,128)(2,1)}, bf16[1,96,3072]{2,1,0:T(8,128)(2,1)}, u32[]{:S(2)}, u32[]{:S(2)}) collective-permute-start(bf16[1,96,3072]{2,1,0:T(8,128)(2,1)} %get-tuple-element.201), channel_id=1, source_target_pairs={{0,16},{2,18},{4,20},{6,22},{8,24},{10,26},{12,28},{14,30},{16,0},... | collective-permute-start | bytes 1769480 | tf_op jit(solution)/shard_map/ppermute | solution.py:973
  521.9 41.9 %collective-permute-start.24 = (bf16[4,96,1536]{2,1,0:T(8,128)(2,1)}, bf16[4,96,1536]{2,1,0:T(8,128)(2,1)}, u32[]{:S(2)}, u32[]{:S(2)}) collective-permute-start(bf16[4,96,1536]{2,1,0:T(8,128)(2,1)} %get-tuple-element.208), channel_id=1, source_target_pairs={{0,4},{2,6},{4,0},{6,2},{8,12},{10,14},{12,8},{14,10},{16,20},{18,... | collective-permute-start | bytes 3538952 | tf_op jit(solution)/shard_map/ppermute | solution.py:973
  522.5 47.2 %collective-permute-start.26 = (bf16[4,96,1920]{2,1,0:T(8,128)(2,1)}, bf16[4,96,1920]{2,1,0:T(8,128)(2,1)S(1)}, u32[]{:S(2)}, u32[]{:S(2)}) collective-permute-start(bf16[4,96,1920]{2,1,0:T(8,128)(2,1)} %get-tuple-element.204), channel_id=1, source_target_pairs={{0,8},{2,10},{4,12},{6,14},{8,0},{10,2},{12,4},{14,6},{16,24},{18,... | collective-permute-start | bytes 4423688 | tf_op jit(solution)/shard_map/ppermute | solution.py:973
  552.9 30.0 %collective-permute-start.27 = (bf16[8,96,1152]{2,1,0:T(8,128)(2,1)}, bf16[8,96,1152]{2,1,0:T(8,128)(2,1)}, u32[]{:S(2)}, u32[]{:S(2)}) collective-permute-start(bf16[8,96,1152]{2,1,0:T(8,128)(2,1)} %get-tuple-element.211), channel_id=1, source_target_pairs={{0,2},{2,0},{4,6},{6,4},{8,10},{10,8},{12,14},{14,12},{16,18},{18,... | collective-permute-start | bytes 5308424 | tf_op jit(solution)/shard_map/ppermute | solution.py:973
  582.1 84.3 %collective-permute-start.28 = (bf16[512,1536]{1,0:T(8,128)(2,1)}, bf16[512,1536]{1,0:T(8,128)(2,1)}, u32[]{:S(2)}, u32[]{:S(2)}) collective-permute-start(bf16[512,1536]{1,0:T(8,128)(2,1)} %joint_product.2.refs_0_), channel_id=1, source_target_pairs={{0,1},{1,0},{2,3},{3,2},{4,5},{5,4},{6,7},{7,6},{8,9},{9,8},{10,11... | collective-permute-start | bytes 4718600 | tf_op jit(solution)/shard_map/ppermute | solution.py:965
  586.0 21.1 %collective-permute-start.29 = (bf16[4,96,1152]{2,1,0:T(8,128)(2,1)}, bf16[4,96,1152]{2,1,0:T(8,128)(2,1)S(1)}, u32[]{:S(2)}, u32[]{:S(2)}) collective-permute-start(bf16[4,96,1152]{2,1,0:T(8,128)(2,1)} %get-tuple-element.225), channel_id=1, source_target_pairs={{0,4},{2,6},{4,0},{6,2},{8,12},{10,14},{12,8},{14,10},{16,20},{18,... | collective-permute-start | bytes 2654216 | tf_op jit(solution)/shard_map/ppermute | solution.py:973
  591.0 69.1 %collective-permute-start.30 = (bf16[2,96,1920]{2,1,0:T(8,128)(2,1)}, bf16[2,96,1920]{2,1,0:T(8,128)(2,1)}, u32[]{:S(2)}, u32[]{:S(2)}) collective-permute-start(bf16[2,96,1920]{2,1,0:T(8,128)(2,1)} %get-tuple-element.222), channel_id=1, source_target_pairs={{0,16},{2,18},{4,20},{6,22},{8,24},{10,26},{12,28},{14,30},{16,0},... | collective-permute-start | bytes 2211848 | tf_op jit(solution)/shard_map/ppermute | solution.py:973
  594.1 77.8 %collective-permute-start.32 = (bf16[64,768]{1,0:T(8,128)(2,1)}, bf16[64,768]{1,0:T(8,128)(2,1)}, u32[]{:S(2)}, u32[]{:S(2)}) collective-permute-start(bf16[64,768]{1,0:T(8,128)(2,1)} %constant_dynamic-slice_fusion), channel_id=1, source_target_pairs={{0,1},{1,0},{2,3},{3,2},{4,5},{5,4},{6,7},{7,6},{8,9},{9,8},{10,11... | collective-permute-start | bytes 294920 | tf_op jit(solution)/shard_map/ppermute | solution.py:965
  673.7 15.7 %collective-permute-start.31 = (bf16[2,96,1152]{2,1,0:T(8,128)(2,1)S(1)}, bf16[2,96,1152]{2,1,0:T(8,128)(2,1)S(1)}, u32[]{:S(2)}, u32[]{:S(2)}) collective-permute-start(bf16[2,96,1152]{2,1,0:T(8,128)(2,1)S(1)} %copy-done.41), channel_id=1, source_target_pairs={{0,8},{2,10},{4,12},{6,14},{8,0},{10,2},{12,4},{14,6},{16,24},{18,... | collective-permute-start | bytes 1327112 | tf_op jit(solution)/shard_map/ppermute | solution.py:973
  692.2 12.8 %collective-permute-start.34 = (bf16[1,96,1152]{2,1,0:T(8,128)(2,1)}, bf16[1,96,1152]{2,1,0:T(8,128)(2,1)S(1)}, u32[]{:S(2)}, u32[]{:S(2)}) collective-permute-start(bf16[1,96,1152]{2,1,0:T(8,128)(2,1)} %get-tuple-element.237), channel_id=1, source_target_pairs={{0,16},{2,18},{4,20},{6,22},{8,24},{10,26},{12,28},{14,30},{16,0},... | collective-permute-start | bytes 663560 | tf_op jit(solution)/shard_map/ppermute | solution.py:973
  (54 other events, 697.5 us)
Sparse Core Ops, SparseCore 0:
  21.9 122.5 all-gather.2
  146.7 98.8 all-gather.4
  334.6 128.0 reduce-scatter.2
  591.1 68.8 reduce-scatter.4

commit v6 on v5

--- a/solution.py
+++ b/solution.py
@@ -1119,10 +1119,8 @@
     cross_got = swap(cross[0], 1)
     inner_first = after(inner[1], cross[0]), swap(inner[0], 2)
     inner = fold(side_refs[3], inner_first, cost=HEAVY)
-    most = fold(
-        side_refs[2], (after(qkv0[1], inner[0]), qkv0_got), (so[1], so_got), inner=2
-    )
-    most_got = swap(most[0], 2)
+    most = fold(side_refs[1], (after(qkv0[1], inner[0]), qkv0_got), (so[1], so_got))
+    most_got = swap(most[0], 1)
     kv = fold(side_refs[1], *[(after(keep, most[0]), got) for keep, got in kv])
     kv_got = swap(kv[0], 1)
     found1 = self_backward(t_ref, qkv, mixed1, after(d_mixed1, kv[0]), lse1, 1, MIDDLE)
@@ -1132,8 +1130,7 @@
     cross = totals((after(cross[1], qkv1[0]), cross_got), (kv[1], kv_got))
     cross_sum = line_sum(cross)
     inner_sum = line_end(inner[0], after(inner[1], cross))
-    most = fold(side_refs[3], (after(most[1], inner_sum), most_got), inner=2)
-    most_got = swap(most[0], 3)
+    most = fold(side_refs[2], (after(most[1], inner_sum), most_got))
     back1_part = joint_product([found0, after(found1, most[0])], first, BF, 1, rows, HEAVY)
     back1_away = peer(back1_part)
     qkv1 = fold(side_refs[1], (after(qkv1[1], back1_part), qkv1_got))
@@ -1142,14 +1139,12 @@
     qkv1 = fold(side_refs[2], (after(qkv1[1], back1_home), qkv1_got))
     sums0 = norm_sums(after(inputs_peer, qkv1[0]), [back1_part])
     sums1 = sums0 + norm_sums(after(inputs, sums0), [back1_home])
-    most = fold(side_refs[1], (after(most[1], sums1), most_got))
-    most_got = swap(most[0], 1)
+    most = line_step(*most, sums1)
     qkv1 = line_step(*qkv1, most[0])
     input_grad, _, _ = norm_back_rows(
         inputs, norm_gains[0], grad1, [back1_home, after(back1_away, qkv1[0], cross_sum)]
     )
-    most_sum = (most[1].astype(F32) + most_got.astype(F32)).reshape(shard, -1)
-    qkv1_sum = line_end(*qkv1)
+    most_sum, qkv1_sum = line_end(*most), line_end(*qkv1)
     qkv0_sum, so_sum = most_sum[:, : 3 * part], most_sum[:, 3 * part :]
     output = (state2 + out_home + after(out_away, last).astype(F32)).astype(BF)
     text_grad = text_keep.astype(F32) + after(text_got, last).astype(F32)

time: 735 us -> 739 us (level)
  waiting for transfers between devices: 220 us -> 228 us
    ppermute x21, waiting for transfers between devices: 63.4 us -> 74.6 us  [swap(): return lax.ppermute(send, 'dp', swaps[level])]
  transfers between devices with their start and end apart: 44 -> 44, of which waited for: 11 -> 12; matrix products, arithmetic and copies ran while one was open for 14% -> 14% of each run, Pallas kernels for 41% -> 41%
where the time goes in v6:
time: 739 us; the launch traced here: 727 us
  Pallas kernels  334 us (45%)
  waiting for transfers between devices  228 us (31%)
  matrix products  53.8 us (7%)
  starting transfers between devices  37.4 us (5%)
  local copies, waits for them, and re-layouts  30.8 us (4%)
  other arithmetic  28.9 us (4%)
  between operations  14.7 us (2%)
    ppermute x15, waiting for transfers between devices, peer(): return lax.ppermute(value, 'tensor', [(0, 1), (1, 0)])  103 us
    ppermute x21, waiting for transfers between devices, swap(): return lax.ppermute(send, 'dp', swaps[level])  74.6 us
    pallas_call x10, Pallas kernels, weight_halves(): pl.pallas_call(partial(weight_kernel, shard=shard), out_shape=(shape, sha...  67.6 us
    pallas_call x7, Pallas kernels, product(): pl.pallas_call(partial(product_kernel, dims=dims), grid=(size // tile,),...  57.8 us
    dot_general x8, matrix products, mm(): return lax.dot_general(left, right, dims, preferred_element_type=F32)  53.8 us
    all_gather x2, waiting for transfers between devices, gather(): return lax.all_gather(packed, 'dp', axis=0, tiled=True)  44.8 us
    pallas_call x2, Pallas kernels, self_backward(): pl.pallas_call(self_back_kernel, out_shape=jax.ShapeDtypeStruct((length,...  40.3 us
    pallas_call x11, Pallas kernels, fold(): pl.pallas_call(partial(fold_kernel, counts=[len(terms) for terms in group...  38 us
  transfers between devices with their start and end apart: 44, of which 12 were waited for; matrix products, arithmetic and copies ran while one was open for 14% of the time, Pallas kernels for 41%

profile of v6, /device:TPU:0, one launch (start us, length us, event | category | flops | bytes accessed | tf_op | source)
XLA Modules:
  0.0 727.3 jit_solution(2523144072170357007)
XLA Ops:
  30.6 31.9 %collective-permute-done.1.value_ref = bf16[512,1536]{1,0:T(8,128)(2,1)S(1)} collective-permute-done((bf16[512,1536]{1,0:T(8,128)(2,1)S(1)}, bf16[512,1536]{1,0:T(8,128)(2,1)S(1)}, u32[]{:S(2)}, u32[]{:S(2)}) %collective-permute-start.1) | collective-permute-done | bytes 1572896 | tf_op jit(solution)/shard_map/ppermute | solution.py:965
  70.3 27.0 %collective-permute-done.2.g_ref = bf16[512,1536]{1,0:T(8,128)(2,1)S(1)} collective-permute-done((bf16[512,1536]{1,0:T(8,128)(2,1)S(1)}, bf16[512,1536]{1,0:T(8,128)(2,1)S(1)}, u32[]{:S(2)}, u32[]{:S(2)}) %collective-permute-start.2) | collective-permute-done | bytes 1572896 | tf_op jit(solution)/shard_map/ppermute | solution.py:965
  99.7 44.8 %all-gather.3.cloned.1.call-done.right_ref.refs_2_ = bf16[1536,7680]{1,0:T(8,128)(2,1)} async-done(((bf16[96,7680]{1,0:T(8,128)(2,1)}), bf16[1536,7680]{1,0:T(8,128)(2,1)}) %all-gather.3.cloned.1.call-update) | async-done | bytes 23592976 | tf_op jit(solution)/shard_map/all_gather | solution.py:968
  147.9 12.1 %fusion.8.q_ref.k_ref.v_ref = bf16[1024,2304]{1,0:T(8,128)(2,1)} fusion(bf16[1024,1536]{1,0:T(8,128)(2,1)S(1)} %copy-done.3, bf16[1536,7680]{1,0:T(8,128)(2,1)} %all-gather.3.cloned.1.call-done.right_ref.refs_2_), kind=kOutput, calls=%fused_computation.11 | convolution fusion | flops 7250116608 | bytes 14942208 | tf_op jit(solution)/shard_map/dot_general | solution.py:315
  160.0 21.0 %self_attend.1 = (bf16[1024,768]{1,0:T(8,128)(2,1)}, f32[6,8,1024]{2,1,0:T(8,128)}) custom-call(s32[1]{0:T(128)} %bitcast.4.t_ref, bf16[1024,2304]{1,0:T(8,128)(2,1)} %fusion.8.q_ref.k_ref.v_ref, bf16[1024,2304]{1,0:T(8,128)(2,1)} %fusion.8.q_ref.k_ref.v_ref, bf16[1024,2304]{1,0:T(8,128)(2,1)} %fusion.8.q_ref.k_ref.v_ref), custom_call_target="tpu_custom_call" | custom-call | flops 1024 | bytes 1024 | tf_op jit(solution)/shard_map/self_attend/pallas_call | solution.py:650
  186.7 38.6 %collective-permute-done.4 = bf16[64,1536]{1,0:T(8,128)(2,1)S(1)} collective-permute-done((bf16[64,1536]{1,0:T(8,128)(2,1)S(1)}, bf16[64,1536]{1,0:T(8,128)(2,1)S(1)}, u32[]{:S(2)}, u32[]{:S(2)}) %collective-permute-start.4) | collective-permute-done | bytes 196640 | tf_op jit(solution)/shard_map/ppermute | solution.py:965
  231.9 6.7 fusion.23.q_ref
  238.6 6.8 cross_attend.1
  253.7 16.9 %ffn_middle.2 = (bf16[1024,3072]{1,0:T(8,128)(2,1)}, bf16[1024,3072]{1,0:T(8,128)(2,1)}) custom-call(bf16[512,1536]{1,0:T(8,128)(2,1)} %copy-done.8, bf16[512,1536]{1,0:T(8,128)(2,1)} %base_ref.1, bf16[1536,6144]{1,0:T(8,128)(2,1)} %all-gather.5.cloned.1.call-done.wi_ref.wo_ref.right_ref, bf16[1536,6144]{1,0:T(8,128)(2,1)} %all-gather.5.cloned.1.call-done.wi_ref.wo_ref.right_ref), custom_call_target="tpu_custom_call" | custom-call | flops 1024 | bytes 1024 | tf_op jit(solution)/shard_map/ffn_middle/pallas_call | solution.py:894
  270.6 9.8 %product.7 = f32[512,1536]{1,0:T(8,128)} custom-call(bf16[1024,3072]{1,0:T(8,128)(2,1)} %get-tuple-element.139.left_ref.refs_0_, bf16[1536,6144]{1,0:T(8,128)(2,1)} %all-gather.5.cloned.1.call-done.wi_ref.wo_ref.right_ref), custom_call_target="tpu_custom_call" | custom-call | flops 1024 | bytes 1024 | tf_op jit(solution)/shard_map/product/pallas_call | solution.py:565
  280.4 9.8 %product.8.refs_0_ = f32[512,1536]{1,0:T(8,128)} custom-call(bf16[1024,3072]{1,0:T(8,128)(2,1)} %get-tuple-element.140.left_ref.refs_1_, bf16[1536,6144]{1,0:T(8,128)(2,1)} %all-gather.5.cloned.1.call-done.wi_ref.wo_ref.right_ref), custom_call_target="tpu_custom_call" | custom-call | flops 1024 | bytes 1024 | tf_op jit(solution)/shard_map/product/pallas_call | solution.py:565
  291.4 16.9 %ffn_middle.3 = (bf16[1024,3072]{1,0:T(8,128)(2,1)}, bf16[1024,3072]{1,0:T(8,128)(2,1)}) custom-call(bf16[512,1536]{1,0:T(8,128)(2,1)} %copy-done.13, bf16[512,1536]{1,0:T(8,128)(2,1)} %copy-done.12, bf16[1536,6144]{1,0:T(8,128)(2,1)} %all-gather.5.cloned.1.call-done.wi_ref.wo_ref.right_ref, ...), custom_call_target="tpu_custom_call", output_to_operand_aliasing={{0}: (4, {}), {1}: (5, {})} | custom-call | flops 1024 | bytes 1024 | tf_op jit(solution)/shard_map/ffn_middle/pallas_call | solution.py:894
  308.3 9.5 %product.9 = bf16[512,1536]{1,0:T(8,128)(2,1)} custom-call(bf16[1024,3072]{1,0:T(8,128)(2,1)} %get-tuple-element.143.left_ref.right_ref, bf16[1536,6144]{1,0:T(8,128)(2,1)} %all-gather.5.cloned.1.call-done.wi_ref.wo_ref.right_ref), custom_call_target="tpu_custom_call" | custom-call | flops 1024 | bytes 1024 | tf_op jit(solution)/shard_map/product/pallas_call | solution.py:565
  318.9 15.5 %convolution_convert_fusion = bf16[1536,3072]{1,0:T(8,128)(2,1)} fusion(bf16[1024,1536]{1,0:T(8,128)(2,1)} %constant_dynamic-update-slice_fusion, bf16[1024,3072]{1,0:T(8,128)(2,1)} %get-tuple-element.162.left_ref), kind=kOutput, calls=%fused_computation | convolution fusion | flops 9668395008 | bytes 18874368 | tf_op jit(solution)/shard_map/dot_general | solution.py:315
  338.2 16.3 %weight_halves.10 = (bf16[8,96,3072]{2,1,0:T(8,128)(2,1)}, bf16[8,96,3072]{2,1,0:T(8,128)(2,1)}) custom-call(s32[1]{0:T(128)} %bitcast.side_ref, bf16[1024,1536]{1,0:T(8,128)(2,1)} %pad_maximum_fusion.1.left_ref, bf16[1024,3072]{1,0:T(8,128)(2,1)} %get-tuple-element.143.left_ref.right_ref), custom_call_target="tpu_custom_call" | custom-call | flops 1024 | bytes 1024 | tf_op jit(solution)/shard_map/weight_halves/pallas_call | solution.py:343
  354.4 7.3 norm_back.3
  373.9 7.4 %cross_attend_back.1 = (bf16[512,1536]{1,0:T(8,128)(2,1)}, f32[64,1536]{1,0:T(8,128)}, f32[64,1536]{1,0:T(8,128)}) custom-call(bf16[512,1536]{1,0:T(8,128)(2,1)} %fusion.23.q_ref, bf16[64,1536]{1,0:T(8,128)(2,1)} %get-tuple-element.284.k_ref, bf16[64,1536]{1,0:T(8,128)(2,1)} %get-tuple-element.285.v_ref, ...), custom_call_target="tpu_custom_call" | custom-call | flops 1024 | bytes 1024 | tf_op jit(solution)/shard_map/cross_attend_back/pallas_call | solution.py:851
  385.3 6.8 product.11.refs_0_
  392.1 6.9 norm_back.4
  401.0 9.6 %product.12 = bf16[512,1536]{1,0:T(8,128)(2,1)} custom-call(bf16[1024,3072]{1,0:T(8,128)(2,1)} %get-tuple-element.162.left_ref, bf16[1536,6144]{1,0:T(8,128)(2,1)} %all-gather.5.cloned.1.call-done.wi_ref.wo_ref.right_ref), custom_call_target="tpu_custom_call" | custom-call | flops 1024 | bytes 1024 | tf_op jit(solution)/shard_map/product/pallas_call | solution.py:565
  448.8 20.2 %self_attend_back.2.right_ref.refs_0_ = bf16[1024,1152]{1,0:T(8,128)(2,1)} custom-call(s32[1]{0:T(128)} %bitcast.4.t_ref, bf16[1024,2304]{1,0:T(8,128)(2,1)} %fusion.8.q_ref.k_ref.v_ref, bf16[1024,2304]{1,0:T(8,128)(2,1)} %fusion.8.q_ref.k_ref.v_ref, bf16[1024,2304]{1,0:T(8,128)(2,1)} %fusion.8.q_ref.k_ref.v_ref, ...), custom_call_target="tpu_custom_call" | custom-call | flops 1024 | bytes 1024 | tf_op jit(solution)/shard_map/self_attend_back/pallas_call | solution.py:741
  477.0 9.2 %weight_halves.15 = (bf16[8,96,1152]{2,1,0:T(8,128)(2,1)}, bf16[8,96,1152]{2,1,0:T(8,128)(2,1)}) custom-call(s32[1]{0:T(128)} %bitcast.side_ref, bf16[1024,1536]{1,0:T(8,128)(2,1)} %fusion.7.left_ref, bf16[1024,1152]{1,0:T(8,128)(2,1)} %self_attend_back.2.right_ref.refs_0_), custom_call_target="tpu_custom_call" | custom-call | flops 1024 | bytes 1024 | tf_op jit(solution)/shard_map/weight_halves/pallas_call | solution.py:343
  523.1 20.1 %self_attend_back.3.right_ref.refs_1_ = bf16[1024,1152]{1,0:T(8,128)(2,1)} custom-call(s32[1]{0:T(128)} %bitcast.4.t_ref, bf16[1024,2304]{1,0:T(8,128)(2,1)} %fusion.8.q_ref.k_ref.v_ref, bf16[1024,2304]{1,0:T(8,128)(2,1)} %fusion.8.q_ref.k_ref.v_ref, bf16[1024,2304]{1,0:T(8,128)(2,1)} %fusion.8.q_ref.k_ref.v_ref, ...), custom_call_target="tpu_custom_call" | custom-call | flops 20000000000 | bytes 1024 | tf_op jit(solution)/shard_map/self_attend_back/pallas_call | solution.py:741
  543.2 9.3 %weight_halves.19 = (bf16[8,96,1152]{2,1,0:T(8,128)(2,1)}, bf16[8,96,1152]{2,1,0:T(8,128)(2,1)}) custom-call(s32[1]{0:T(128)} %bitcast.side_ref, bf16[1024,1536]{1,0:T(8,128)(2,1)} %fusion.7.left_ref, bf16[1024,1152]{1,0:T(8,128)(2,1)} %self_attend_back.3.right_ref.refs_1_), custom_call_target="tpu_custom_call" | custom-call | flops 1024 | bytes 1024 | tf_op jit(solution)/shard_map/weight_halves/pallas_call | solution.py:343
  552.6 11.8 %collective-permute-done.24.refs_3_ = bf16[4,96,1536]{2,1,0:T(8,128)(2,1)} collective-permute-done((bf16[4,96,1536]{2,1,0:T(8,128)(2,1)}, bf16[4,96,1536]{2,1,0:T(8,128)(2,1)}, u32[]{:S(2)}, u32[]{:S(2)}) %collective-permute-start.24) | collective-permute-done | bytes 1179680 | tf_op jit(solution)/shard_map/ppermute | solution.py:973
  570.2 25.1 %collective-permute-done.26.refs_1_ = bf16[4,96,1920]{2,1,0:T(8,128)(2,1)S(1)} collective-permute-done((bf16[4,96,1920]{2,1,0:T(8,128)(2,1)}, bf16[4,96,1920]{2,1,0:T(8,128)(2,1)S(1)}, u32[]{:S(2)}, u32[]{:S(2)}) %collective-permute-start.26) | collective-permute-done | bytes 1474592 | tf_op jit(solution)/shard_map/ppermute | solution.py:973
  599.7 8.1 %joint_product.2.refs_0_ = bf16[512,1536]{1,0:T(8,128)(2,1)} custom-call(bf16[1024,1152]{1,0:T(8,128)(2,1)} %self_attend_back.2.right_ref.refs_0_, bf16[1024,1152]{1,0:T(8,128)(2,1)} %self_attend_back.3.right_ref.refs_1_, bf16[1536,7680]{1,0:T(8,128)(2,1)} %all-gather.3.cloned.1.call-done.right_ref.refs_2_), custom_call_target="tpu_custom_call" | custom-call | flops 999999986991104 | bytes 1024 | tf_op jit(solution)/shard_map/joint_product/pallas_call | solution.py:538
  620.3 8.9 %joint_product.3.refs_0_ = f32[512,1536]{1,0:T(8,128)} custom-call(bf16[1024,1152]{1,0:T(8,128)(2,1)} %self_attend_back.2.right_ref.refs_0_, bf16[1024,1152]{1,0:T(8,128)(2,1)} %self_attend_back.3.right_ref.refs_1_, bf16[1536,7680]{1,0:T(8,128)(2,1)} %all-gather.3.cloned.1.call-done.right_ref.refs_2_), custom_call_target="tpu_custom_call" | custom-call | flops 1024 | bytes 1024 | tf_op jit(solution)/shard_map/joint_product/pallas_call | solution.py:538
  645.8 11.9 %collective-permute-done.30.refs_1_ = bf16[2,96,1920]{2,1,0:T(8,128)(2,1)} collective-permute-done((bf16[2,96,1920]{2,1,0:T(8,128)(2,1)}, bf16[2,96,1920]{2,1,0:T(8,128)(2,1)}, u32[]{:S(2)}, u32[]{:S(2)}) %collective-permute-start.30) | collective-permute-done | bytes 737312 | tf_op jit(solution)/shard_map/ppermute | solution.py:973
  672.9 12.6 %collective-permute-done.33 = bf16[1,96,1920]{2,1,0:T(8,128)(2,1)} collective-permute-done((bf16[1,96,1920]{2,1,0:T(8,128)(2,1)}, bf16[1,96,1920]{2,1,0:T(8,128)(2,1)}, u32[]{:S(2)}, u32[]{:S(2)}) %collective-permute-start.33) | collective-permute-done | bytes 368672 | tf_op jit(solution)/shard_map/ppermute | solution.py:973
  699.7 9.6 %collective-permute-done.34 = bf16[1,96,1152]{2,1,0:T(8,128)(2,1)S(1)} collective-permute-done((bf16[1,96,1152]{2,1,0:T(8,128)(2,1)}, bf16[1,96,1152]{2,1,0:T(8,128)(2,1)S(1)}, u32[]{:S(2)}, u32[]{:S(2)}) %collective-permute-start.34) | collective-permute-done | bytes 221216 | tf_op jit(solution)/shard_map/ppermute | solution.py:973
  712.5 6.8 norm_back.5
  (256 shorter events, 237.5 us)
Async XLA Ops:
  7.2 137.3 %all-gather.3.cloned.1.call-start = ((), (), s32[]{:S(2)}) async-start(), calls=%async_computation.2 | async-start | bytes 25067520 | tf_op jit(solution)/shard_map/all_gather | solution.py:968
  21.7 232.0 %all-gather.5.cloned.1.call-start = ((), (), s32[]{:S(2)}) async-start(), calls=%async_computation.3 | async-start | bytes 20054016 | tf_op jit(solution)/shard_map/all_gather | solution.py:968
  26.8 442.2 %reduce-scatter.3.cloned.1.call-start = ((), (), s32[]{:S(2)}) async-start(), calls=%async_computation.4 | async-start | bytes 10027008 | tf_op jit(solution)/shard_map/reduce_scatter | solution.py:1050
  26.9 35.6 %collective-permute-start.1 = (bf16[512,1536]{1,0:T(8,128)(2,1)S(1)}, bf16[512,1536]{1,0:T(8,128)(2,1)S(1)}, u32[]{:S(2)}, u32[]{:S(2)}) collective-permute-start(bf16[512,1536]{1,0:T(8,128)(2,1)S(1)} %copy-done), channel_id=1, source_target_pairs={{0,1},{1,0},{2,3},{3,2},{4,5},{5,4},{6,7},{7,6},{8,9},{9,8},{10,11... | collective-permute-start | bytes 4718600 | tf_op jit(solution)/shard_map/ppermute | solution.py:965
  62.5 34.8 %collective-permute-start.2 = (bf16[512,1536]{1,0:T(8,128)(2,1)S(1)}, bf16[512,1536]{1,0:T(8,128)(2,1)S(1)}, u32[]{:S(2)}, u32[]{:S(2)}) collective-permute-start(bf16[512,1536]{1,0:T(8,128)(2,1)S(1)} %copy-done.11), channel_id=1, source_target_pairs={{0,1},{1,0},{2,3},{3,2},{4,5},{5,4},{6,7},{7,6},{8,9},{9,8},{10,11... | collective-permute-start | bytes 4718600 | tf_op jit(solution)/shard_map/ppermute | solution.py:965
  184.6 41.5 %collective-permute-start.3 = (bf16[512,1536]{1,0:T(8,128)(2,1)S(1)}, bf16[512,1536]{1,0:T(8,128)(2,1)S(1)}, u32[]{:S(2)}, u32[]{:S(2)}) collective-permute-start(bf16[512,1536]{1,0:T(8,128)(2,1)S(1)} %convolution_convert_fusion.1), channel_id=1, source_target_pairs={{0,1},{1,0},{2,3},{3,2},{4,5},{5,4},{6,7},{7,6},{8,9},{9,8},{10,11... | collective-permute-start | bytes 4718600 | tf_op jit(solution)/shard_map/ppermute | solution.py:965
  186.2 39.2 %collective-permute-start.4 = (bf16[64,1536]{1,0:T(8,128)(2,1)S(1)}, bf16[64,1536]{1,0:T(8,128)(2,1)S(1)}, u32[]{:S(2)}, u32[]{:S(2)}) collective-permute-start(bf16[64,1536]{1,0:T(8,128)(2,1)S(1)} %fusion.32), channel_id=1, source_target_pairs={{0,1},{1,0},{2,3},{3,2},{4,5},{5,4},{6,7},{7,6},{8,9},{9,8},{10,11... | collective-permute-start | bytes 589832 | tf_op jit(solution)/shard_map/ppermute | solution.py:965
  252.3 38.0 %collective-permute-start.5 = (bf16[512,1536]{1,0:T(8,128)(2,1)S(1)}, bf16[512,1536]{1,0:T(8,128)(2,1)S(1)}, u32[]{:S(2)}, u32[]{:S(2)}) collective-permute-start(bf16[512,1536]{1,0:T(8,128)(2,1)S(1)} %add_convert_fusion.1.n_ref), channel_id=1, source_target_pairs={{0,1},{1,0},{2,3},{3,2},{4,5},{5,4},{6,7},{7,6},{8,9},{9,8},{10,11... | collective-permute-start | bytes 4718600 | tf_op jit(solution)/shard_map/ppermute | solution.py:965
  317.7 36.7 %collective-permute-start.6 = (bf16[512,1536]{1,0:T(8,128)(2,1)}, bf16[512,1536]{1,0:T(8,128)(2,1)}, u32[]{:S(2)}, u32[]{:S(2)}) collective-permute-start(bf16[512,1536]{1,0:T(8,128)(2,1)} %product.9), channel_id=1, source_target_pairs={{0,1},{1,0},{2,3},{3,2},{4,5},{5,4},{6,7},{7,6},{8,9},{9,8},{10,11... | collective-permute-start | bytes 4718600 | tf_op jit(solution)/shard_map/ppermute | solution.py:965
  334.5 378.1 %reduce-scatter.5.cloned.1.call-start = ((), (), s32[]{:S(2)}) async-start(), calls=%async_computation.5 | async-start | bytes 2949120 | tf_op jit(solution)/shard_map/reduce_scatter | solution.py:977
  383.2 15.9 %collective-permute-start.8 = (bf16[64,1536]{1,0:T(8,128)(2,1)S(1)}, bf16[64,1536]{1,0:T(8,128)(2,1)S(1)}, u32[]{:S(2)}, u32[]{:S(2)}) collective-permute-start(bf16[64,1536]{1,0:T(8,128)(2,1)S(1)} %pad_maximum_fusion.8), channel_id=1, source_target_pairs={{0,1},{1,0},{2,3},{3,2},{4,5},{5,4},{6,7},{7,6},{8,9},{9,8},{10,11... | collective-permute-start | bytes 589832 | tf_op jit(solution)/shard_map/ppermute | solution.py:965
  384.3 84.7 %collective-permute-start.13 = (bf16[4,96,3072]{2,1,0:T(8,128)(2,1)}, bf16[4,96,3072]{2,1,0:T(8,128)(2,1)}, u32[]{:S(2)}, u32[]{:S(2)}) collective-permute-start(bf16[4,96,3072]{2,1,0:T(8,128)(2,1)} %get-tuple-element.154), channel_id=1, source_target_pairs={{0,4},{2,6},{4,0},{6,2},{8,12},{10,14},{12,8},{14,10},{16,20},{18,... | collective-permute-start | bytes 7077896 | tf_op jit(solution)/shard_map/ppermute | solution.py:973
  399.9 39.4 %collective-permute-start.9 = (bf16[512,1536]{1,0:T(8,128)(2,1)}, bf16[512,1536]{1,0:T(8,128)(2,1)}, u32[]{:S(2)}, u32[]{:S(2)}) collective-permute-start(bf16[512,1536]{1,0:T(8,128)(2,1)} %get-tuple-element.164), channel_id=1, source_target_pairs={{0,1},{1,0},{2,3},{3,2},{4,5},{5,4},{6,7},{7,6},{8,9},{9,8},{10,11... | collective-permute-start | bytes 4718600 | tf_op jit(solution)/shard_map/ppermute | solution.py:965
  430.4 69.4 %collective-permute-start.14 = (bf16[8,96,768]{2,1,0:T(8,128)(2,1)}, bf16[8,96,768]{2,1,0:T(8,128)(2,1)}, u32[]{:S(2)}, u32[]{:S(2)}) collective-permute-start(bf16[8,96,768]{2,1,0:T(8,128)(2,1)} %get-tuple-element.166), channel_id=1, source_target_pairs={{0,2},{2,0},{4,6},{6,4},{8,10},{10,8},{12,14},{14,12},{16,18},{18,... | collective-permute-start | bytes 3538952 | tf_op jit(solution)/shard_map/ppermute | solution.py:973
  431.9 69.1 %collective-permute-start.16 = (bf16[8,96,768]{2,1,0:T(8,128)(2,1)}, bf16[8,96,768]{2,1,0:T(8,128)(2,1)}, u32[]{:S(2)}, u32[]{:S(2)}) collective-permute-start(bf16[8,96,768]{2,1,0:T(8,128)(2,1)} %get-tuple-element.170), channel_id=1, source_target_pairs={{0,2},{2,0},{4,6},{6,4},{8,10},{10,8},{12,14},{14,12},{16,18},{18,... | collective-permute-start | bytes 3538952 | tf_op jit(solution)/shard_map/ppermute | solution.py:973
  435.4 65.6 %collective-permute-start.15 = (bf16[8,96,768]{2,1,0:T(8,128)(2,1)}, bf16[8,96,768]{2,1,0:T(8,128)(2,1)}, u32[]{:S(2)}, u32[]{:S(2)}) collective-permute-start(bf16[8,96,768]{2,1,0:T(8,128)(2,1)} %totals.3), channel_id=1, source_target_pairs={{0,1},{1,0},{2,3},{3,2},{4,5},{5,4},{6,7},{7,6},{8,9},{9,8},{10,11... | collective-permute-start | bytes 3538952 | tf_op jit(solution)/shard_map/ppermute | solution.py:965
  440.8 60.8 %collective-permute-start.17 = (bf16[8,96,768]{2,1,0:T(8,128)(2,1)}, bf16[8,96,768]{2,1,0:T(8,128)(2,1)}, u32[]{:S(2)}, u32[]{:S(2)}) collective-permute-start(bf16[8,96,768]{2,1,0:T(8,128)(2,1)} %totals.4), channel_id=1, source_target_pairs={{0,1},{1,0},{2,3},{3,2},{4,5},{5,4},{6,7},{7,6},{8,9},{9,8},{10,11... | collective-permute-start | bytes 3538952 | tf_op jit(solution)/shard_map/ppermute | solution.py:965
  472.6 33.5 %collective-permute-start.18 = (bf16[2,96,3072]{2,1,0:T(8,128)(2,1)}, bf16[2,96,3072]{2,1,0:T(8,128)(2,1)S(1)}, u32[]{:S(2)}, u32[]{:S(2)}) collective-permute-start(bf16[2,96,3072]{2,1,0:T(8,128)(2,1)} %get-tuple-element.183), channel_id=1, source_target_pairs={{0,8},{2,10},{4,12},{6,14},{8,0},{10,2},{12,4},{14,6},{16,24},{18,... | collective-permute-start | bytes 3538952 | tf_op jit(solution)/shard_map/ppermute | solution.py:973
  499.8 120.5 %collective-permute-start.12 = (bf16[512,1536]{1,0:T(8,128)(2,1)}, bf16[512,1536]{1,0:T(8,128)(2,1)}, u32[]{:S(2)}, u32[]{:S(2)}) collective-permute-start(bf16[512,1536]{1,0:T(8,128)(2,1)} %product.12), channel_id=1, source_target_pairs={{0,1},{1,0},{2,3},{3,2},{4,5},{5,4},{6,7},{7,6},{8,9},{9,8},{10,11... | collective-permute-start | bytes 4718600 | tf_op jit(solution)/shard_map/ppermute | solution.py:965
  501.5 16.0 %collective-permute-start.21 = (bf16[8,96,768]{2,1,0:T(8,128)(2,1)}, bf16[8,96,768]{2,1,0:T(8,128)(2,1)}, u32[]{:S(2)}, u32[]{:S(2)}) collective-permute-start(bf16[8,96,768]{2,1,0:T(8,128)(2,1)} %get-tuple-element.194), channel_id=1, source_target_pairs={{0,2},{2,0},{4,6},{6,4},{8,10},{10,8},{12,14},{14,12},{16,18},{18,... | collective-permute-start | bytes 3538952 | tf_op jit(solution)/shard_map/ppermute | solution.py:973
  509.9 42.6 %collective-permute-start.23 = (bf16[4,96,1536]{2,1,0:T(8,128)(2,1)}, bf16[4,96,1536]{2,1,0:T(8,128)(2,1)S(1)}, u32[]{:S(2)}, u32[]{:S(2)}) collective-permute-start(bf16[4,96,1536]{2,1,0:T(8,128)(2,1)} %get-tuple-element.199), channel_id=1, source_target_pairs={{0,4},{2,6},{4,0},{6,2},{8,12},{10,14},{12,8},{14,10},{16,20},{18,... | collective-permute-start | bytes 3538952 | tf_op jit(solution)/shard_map/ppermute | solution.py:973
  511.0 57.0 %collective-permute-start.25 = (bf16[1,96,3072]{2,1,0:T(8,128)(2,1)}, bf16[1,96,3072]{2,1,0:T(8,128)(2,1)}, u32[]{:S(2)}, u32[]{:S(2)}) collective-permute-start(bf16[1,96,3072]{2,1,0:T(8,128)(2,1)} %get-tuple-element.201), channel_id=1, source_target_pairs={{0,16},{2,18},{4,20},{6,22},{8,24},{10,26},{12,28},{14,30},{16,0},... | collective-permute-start | bytes 1769480 | tf_op jit(solution)/shard_map/ppermute | solution.py:973
  521.1 43.3 %collective-permute-start.24 = (bf16[4,96,1536]{2,1,0:T(8,128)(2,1)}, bf16[4,96,1536]{2,1,0:T(8,128)(2,1)}, u32[]{:S(2)}, u32[]{:S(2)}) collective-permute-start(bf16[4,96,1536]{2,1,0:T(8,128)(2,1)} %get-tuple-element.208), channel_id=1, source_target_pairs={{0,4},{2,6},{4,0},{6,2},{8,12},{10,14},{12,8},{14,10},{16,20},{18,... | collective-permute-start | bytes 3538952 | tf_op jit(solution)/shard_map/ppermute | solution.py:973
  521.6 73.7 %collective-permute-start.26 = (bf16[4,96,1920]{2,1,0:T(8,128)(2,1)}, bf16[4,96,1920]{2,1,0:T(8,128)(2,1)S(1)}, u32[]{:S(2)}, u32[]{:S(2)}) collective-permute-start(bf16[4,96,1920]{2,1,0:T(8,128)(2,1)} %get-tuple-element.204), channel_id=1, source_target_pairs={{0,4},{2,6},{4,0},{6,2},{8,12},{10,14},{12,8},{14,10},{16,20},{18,... | collective-permute-start | bytes 4423688 | tf_op jit(solution)/shard_map/ppermute | solution.py:973
  552.5 56.1 %collective-permute-start.27 = (bf16[8,96,1152]{2,1,0:T(8,128)(2,1)}, bf16[8,96,1152]{2,1,0:T(8,128)(2,1)}, u32[]{:S(2)}, u32[]{:S(2)}) collective-permute-start(bf16[8,96,1152]{2,1,0:T(8,128)(2,1)} %get-tuple-element.211), channel_id=1, source_target_pairs={{0,2},{2,0},{4,6},{6,4},{8,10},{10,8},{12,14},{14,12},{16,18},{18,... | collective-permute-start | bytes 5308424 | tf_op jit(solution)/shard_map/ppermute | solution.py:973
  607.8 55.2 %collective-permute-start.28 = (bf16[512,1536]{1,0:T(8,128)(2,1)}, bf16[512,1536]{1,0:T(8,128)(2,1)}, u32[]{:S(2)}, u32[]{:S(2)}) collective-permute-start(bf16[512,1536]{1,0:T(8,128)(2,1)} %joint_product.2.refs_0_), channel_id=1, source_target_pairs={{0,1},{1,0},{2,3},{3,2},{4,5},{5,4},{6,7},{7,6},{8,9},{9,8},{10,11... | collective-permute-start | bytes 4718600 | tf_op jit(solution)/shard_map/ppermute | solution.py:965
  611.7 21.1 %collective-permute-start.29 = (bf16[4,96,1152]{2,1,0:T(8,128)(2,1)}, bf16[4,96,1152]{2,1,0:T(8,128)(2,1)S(1)}, u32[]{:S(2)}, u32[]{:S(2)}) collective-permute-start(bf16[4,96,1152]{2,1,0:T(8,128)(2,1)} %get-tuple-element.225), channel_id=1, source_target_pairs={{0,4},{2,6},{4,0},{6,2},{8,12},{10,14},{12,8},{14,10},{16,20},{18,... | collective-permute-start | bytes 2654216 | tf_op jit(solution)/shard_map/ppermute | solution.py:973
  616.7 41.1 %collective-permute-start.30 = (bf16[2,96,1920]{2,1,0:T(8,128)(2,1)}, bf16[2,96,1920]{2,1,0:T(8,128)(2,1)}, u32[]{:S(2)}, u32[]{:S(2)}) collective-permute-start(bf16[2,96,1920]{2,1,0:T(8,128)(2,1)} %get-tuple-element.222), channel_id=1, source_target_pairs={{0,8},{2,10},{4,12},{6,14},{8,0},{10,2},{12,4},{14,6},{16,24},{18,... | collective-permute-start | bytes 2211848 | tf_op jit(solution)/shard_map/ppermute | solution.py:973
  617.9 49.6 %collective-permute-start.32 = (bf16[64,768]{1,0:T(8,128)(2,1)}, bf16[64,768]{1,0:T(8,128)(2,1)}, u32[]{:S(2)}, u32[]{:S(2)}) collective-permute-start(bf16[64,768]{1,0:T(8,128)(2,1)} %constant_dynamic-slice_fusion), channel_id=1, source_target_pairs={{0,1},{1,0},{2,3},{3,2},{4,5},{5,4},{6,7},{7,6},{8,9},{9,8},{10,11... | collective-permute-start | bytes 294920 | tf_op jit(solution)/shard_map/ppermute | solution.py:965
  660.1 25.4 %collective-permute-start.33 = (bf16[1,96,1920]{2,1,0:T(8,128)(2,1)}, bf16[1,96,1920]{2,1,0:T(8,128)(2,1)}, u32[]{:S(2)}, u32[]{:S(2)}) collective-permute-start(bf16[1,96,1920]{2,1,0:T(8,128)(2,1)} %get-tuple-element.235), channel_id=1, source_target_pairs={{0,16},{2,18},{4,20},{6,22},{8,24},{10,26},{12,28},{14,30},{16,0},... | collective-permute-start | bytes 1105928 | tf_op jit(solution)/shard_map/ppermute | solution.py:973
  669.3 24.6 %collective-permute-start.31 = (bf16[2,96,1152]{2,1,0:T(8,128)(2,1)S(1)}, bf16[2,96,1152]{2,1,0:T(8,128)(2,1)S(1)}, u32[]{:S(2)}, u32[]{:S(2)}) collective-permute-start(bf16[2,96,1152]{2,1,0:T(8,128)(2,1)S(1)} %copy-done.41), channel_id=1, source_target_pairs={{0,8},{2,10},{4,12},{6,14},{8,0},{10,2},{12,4},{14,6},{16,24},{18,... | collective-permute-start | bytes 1327112 | tf_op jit(solution)/shard_map/ppermute | solution.py:973
  672.4 14.1 %collective-permute-start.37 = (f32[6,1536]{1,0:T(8,128)S(1)}, f32[6,1536]{1,0:T(8,128)S(1)}, u32[]{:S(2)}, u32[]{:S(2)}) collective-permute-start(f32[6,1536]{1,0:T(8,128)S(1)} %add.134), channel_id=1, source_target_pairs={{0,4},{2,6},{4,0},{6,2},{8,12},{10,14},{12,8},{14,10},{16,20},{18,... | collective-permute-start | bytes 110600 | tf_op jit(solution)/shard_map/ppermute | solution.py:1159
  (54 other events, 566.2 us)
Sparse Core Ops, SparseCore 0:
  21.9 122.5 all-gather.2
  146.7 98.8 all-gather.4
  334.6 128.0 reduce-scatter.2
  616.8 69.4 reduce-scatter.4
